TPU v7x, 32 devices: a whole 2x2x4 slice. The times are simulated.
32 devices in a mesh: lat: 8 (over y, x, core), lon: 4 (over z).
Axes of the slice: x: 2, y: 2, z: 4, core: 2. Of those that a mesh axis runs over, the one named last changes fastest.
Arguments:
- queries: bfloat16 [8, 8, 64, 1024], P('lat', 'lon'), may hold values from -36 to 36
- keys_values: bfloat16 [2, 8, 8, 64, 1024], P(None, 'lat', 'lon'), may hold values from -4 to 4
- cotangent: bfloat16 [8, 8, 64, 1024], P('lat', 'lon'), may hold values from -6 to 6
- blocks: int32 [8, 8, 6], P('lat', 'lon'), may hold values from 0 to 63, as said below
Outputs:
- attended: bfloat16 [8, 8, 64, 1024], P('lat', 'lon')
- grad_queries: bfloat16 [8, 8, 64, 1024], P('lat', 'lon')
- grad_keys_values: bfloat16 [2, 8, 8, 64, 1024], P(None, 'lat', 'lon')
Inputs may be any that keep to these rules, and one draw needn't show every extreme that they name: Entry 0 of each query block's list is the block itself. The other 5 entries are distinct blocks other than itself, whose band differs by at most one from the query block's band and whose sector differs by at most one, counted cyclically over 8 sectors.
All inputs are finite; a program needn't handle non-finite values.
Results may differ from a plain program's by a relative error of at most 0.0085.
Values may be sent and summed in bfloat16 or wider, within the bound.
No kernel may reach another device: no remote copies, remote signals or barrier semaphores. Data moves between devices by JAX's collectives and lax.ppermute only.
A program may use at most 128 MiB of HBM per device.

v0:
```python
import jax
import jax.numpy as jnp
from jax import lax
from jax.sharding import PartitionSpec as P

HEADS = 16
HEAD_DIM = 64
D = 1024
CELLS = 64


def shifted(value, axis, steps):
    count = lax.axis_size(axis)
    pairs = [(source, (source + steps) % count) for source in range(count)]
    return lax.ppermute(value, axis, pairs)


def passed_along(value, axis, steps):
    count = lax.axis_size(axis)
    first, last = (max(0, -steps), min(count, count - steps))
    return lax.ppermute(value, axis, [(source, source + steps) for source in range(first, last)])


def extended_2(cells, sides, width):
    for axis, dim in sides:
        count = lax.axis_size(axis)
        head = lax.slice_in_dim(cells, 0, width, axis=dim)
        tail = lax.slice_in_dim(cells, cells.shape[dim] - width, cells.shape[dim], axis=dim)
        cells = jnp.concatenate(
            [
                lax.ppermute(tail, axis, [(i, (i + 1) % count) for i in range(count)]),
                cells,
                lax.ppermute(head, axis, [((i + 1) % count, i) for i in range(count)]),
            ],
            axis=dim,
        )
    return cells


def band_attend(query_row, upstream_row, key_row, value_row, listed_row):
    scale = HEAD_DIM ** (-0.5)
    sector_cols = query_row.shape[0]
    query_heads = query_row.reshape(sector_cols, CELLS, HEADS, HEAD_DIM)
    upstream_heads = upstream_row.reshape(sector_cols, CELLS, HEADS, HEAD_DIM)
    key_heads = key_row.reshape(sector_cols, 9 * CELLS, HEADS, HEAD_DIM)
    value_heads = value_row.reshape(sector_cols, 9 * CELLS, HEADS, HEAD_DIM)
    keep = jnp.repeat(listed_row, CELLS, axis=1)[:, None, None, :]
    scores = (
        jnp.einsum("bihe,bjhe->bhij", query_heads, key_heads, preferred_element_type=jnp.float32)
        * scale
    )
    highest = jnp.max(jnp.where(keep, scores, -jnp.inf), axis=3, keepdims=True)
    raised = jnp.where(keep, jnp.exp(jnp.minimum(scores - highest, 0.0)), 0.0)
    total = jnp.sum(raised, axis=3, keepdims=True)
    weights = raised / total
    weights_low = weights.astype(jnp.bfloat16)
    attended = jnp.einsum(
        "bhij,bjhe->bihe", weights_low, value_heads, preferred_element_type=jnp.float32
    )
    attended = attended.reshape(sector_cols, CELLS, D).astype(jnp.bfloat16)
    pressure = jnp.einsum(
        "bihe,bjhe->bhij", upstream_heads, value_heads, preferred_element_type=jnp.float32
    )
    inner = jnp.sum(weights * pressure, axis=3, keepdims=True)
    score_grad = (weights * (pressure - inner) * scale).astype(jnp.bfloat16)
    grad_query = jnp.einsum(
        "bhij,bjhe->bihe", score_grad, key_heads, preferred_element_type=jnp.float32
    )
    grad_query = grad_query.reshape(sector_cols, CELLS, D).astype(jnp.bfloat16)
    grad_key = jnp.einsum(
        "bhij,bihe->bjhe", score_grad, query_heads, preferred_element_type=jnp.float32
    )
    grad_value = jnp.einsum(
        "bhij,bihe->bjhe", weights_low, upstream_heads, preferred_element_type=jnp.float32
    )
    stats = jnp.stack([highest[..., 0], total[..., 0], inner[..., 0]], axis=1)
    return (
        attended,
        grad_query,
        grad_key.reshape(sector_cols, 9, CELLS, D),
        grad_value.reshape(sector_cols, 9, CELLS, D),
        stats,
    )


def sector_section(grads, sector_cols):
    from_next = shifted(grads[:, :, 0].astype(jnp.bfloat16), "lon", -1).astype(jnp.float32)
    from_prior = shifted(grads[:, :, sector_cols + 1].astype(jnp.bfloat16), "lon", 1).astype(
        jnp.float32
    )
    grads = grads.at[:, :, sector_cols].add(from_next)
    grads = grads.at[:, :, 1].add(from_prior)
    return grads[:, :, 1 : sector_cols + 1]


def band_section(grads, band_rows):
    from_next = passed_along(grads[:, 0], "lat", -1)
    from_prior = passed_along(grads[:, band_rows + 1], "lat", 1)
    grads = grads.at[:, band_rows].add(from_next)
    grads = grads.at[:, 1].add(from_prior)
    return grads[:, 1 : band_rows + 1]


def body(queries, keys_values, cotangent, blocks):
    band_rows = queries.shape[0]
    sector_cols = queries.shape[1]
    sector_total = sector_cols * lax.axis_size("lon")
    extended = extended_2(keys_values, (("lat", 1), ("lon", 2)), 1)
    ext_rows = band_rows + 2
    ext_cols = sector_cols + 2
    lat_index = lax.axis_index("lat")
    lon_index = lax.axis_index("lon")
    band_index = blocks // sector_total
    sector_index = blocks % sector_total
    local_row = band_index - lat_index * band_rows + 1
    local_col = (sector_index - lon_index * sector_cols + 1) % sector_total
    relative = (local_row - jnp.arange(band_rows, dtype=jnp.int32)[:, None, None]) * 3 + (
        local_col - jnp.arange(sector_cols, dtype=jnp.int32)[None, :, None]
    )
    listed = jnp.any(relative[..., None] == jnp.arange(9, dtype=jnp.int32), axis=2)
    grads = jnp.zeros((2, ext_rows, ext_cols, CELLS, D), jnp.float32)
    stat_rows = []
    key_row = jnp.concatenate(
        [extended[0, dr, dc : dc + sector_cols] for dr in range(3) for dc in range(3)], axis=1
    )
    value_row = jnp.concatenate(
        [extended[1, dr, dc : dc + sector_cols] for dr in range(3) for dc in range(3)], axis=1
    )
    attended_row, grad_row, grad_key, grad_value, stats = band_attend(
        queries[0], cotangent[0], key_row, value_row, listed[0]
    )
    for offset in range(9):
        dr = offset // 3
        dc = offset % 3
        grads = grads.at[0, dr, dc : dc + sector_cols].add(grad_key[:, offset])
        grads = grads.at[1, dr, dc : dc + sector_cols].add(grad_value[:, offset])
    attended_rows = [attended_row]
    grad_rows = [grad_row]
    stat_rows.append(stats)
    grads = band_section(sector_section(grads, sector_cols), band_rows)
    attended = jnp.stack(attended_rows)
    grad_queries = jnp.stack(grad_rows)
    return (attended, grad_queries, grads.astype(jnp.bfloat16))


def solution(mesh):
    placed = (
        P("lat", "lon", None, None),
        P(None, "lat", "lon", None, None),
        P("lat", "lon", None, None),
        P("lat", "lon", None),
    )
    return jax.shard_map(
        body,
        mesh=mesh,
        in_specs=placed,
        out_specs=(
            P("lat", "lon", None, None),
            P("lat", "lon", None, None),
            P(None, "lat", "lon", None, None),
        ),
        check_vma=False,
    )
```

profile of v0, /device:TPU:3, one launch (start us, length us, event | category | flops | bytes accessed | tf_op | source)
XLA Modules:
  0.0 229.3 jit_solution(16342516020014247490)
XLA Ops:
  4.3 9.4 %collective-permute-done = bf16[2,1,2,64,1024]{4,3,2,1,0:T(8,128)(2,1)S(1)} collective-permute-done((bf16[2,1,2,64,1024]{4,3,2,1,0:T(8,128)(2,1)}, bf16[2,1,2,64,1024]{4,3,2,1,0:T(8,128)(2,1)S(1)}, u32[]{:S(2)}, u32[]{:S(2)}) %collective-permute-start) | collective-permute-done | bytes 524320 | tf_op jit(solution)/shard_map/ppermute | solution.py:31
  17.5 3.3 %collective-permute-start.3 = (bf16[2,3,1,64,1024]{4,3,2,1,0:T(8,128)(2,1)}, bf16[2,3,1,64,1024]{4,3,2,1,0:T(8,128)(2,1)}, u32[]{:S(2)}, u32[]{:S(2)}) collective-permute-start(bf16[2,3,1,64,1024]{4,3,2,1,0:T(8,128)(2,1)} %get-tuple-element.292), channel_id=1, source_target_pairs={{1,0},{2,1},{3,2},{0,3},{5,4},{6,5},{7,6},{4,7},{9,8},{10,9},{11,1... | collective-permute-start | bytes 2359304 | tf_op jit(solution)/shard_map/ppermute | solution.py:33
  31.9 6.6 %collective-permute-done.3 = bf16[2,3,1,64,1024]{4,3,2,1,0:T(8,128)(2,1)} collective-permute-done((bf16[2,3,1,64,1024]{4,3,2,1,0:T(8,128)(2,1)}, bf16[2,3,1,64,1024]{4,3,2,1,0:T(8,128)(2,1)}, u32[]{:S(2)}, u32[]{:S(2)}) %collective-permute-start.3) | collective-permute-done | bytes 786464 | tf_op jit(solution)/shard_map/ppermute | solution.py:33
  38.5 2.0 pad_maximum_fusion
  47.6 7.9 %collective-permute-done.2 = bf16[2,3,1,64,1024]{4,3,2,1,0:T(8,128)(2,1)} collective-permute-done((bf16[2,3,1,64,1024]{4,3,2,1,0:T(8,128)(2,1)}, bf16[2,3,1,64,1024]{4,3,2,1,0:T(8,128)(2,1)}, u32[]{:S(2)}, u32[]{:S(2)}) %collective-permute-start.2) | collective-permute-done | bytes 786464 | tf_op jit(solution)/shard_map/ppermute | solution.py:31
  55.5 2.0 pad_maximum_fusion.1
  64.7 5.3 %concatenate.151 = bf16[2,576,16,64]{1,3,2,0:T(8,128)(2,1)S(1)} concatenate(bf16[2,64,16,64]{1,3,2,0:T(8,128)(2,1)} %bitcast.291, bf16[2,64,16,64]{1,3,2,0:T(8,128)(2,1)} %bitcast.279, bf16[2,64,16,64]{1,3,2,0:T(8,128)(2,1)} %bitcast.285, bf16[2,64,16,64]{1,3,2,0:T(8,128)(2,1)} %bitcast.290, bf16[2,64,16,64]{1,3,2,0:T(8,128)(2,1)} %bitcast.275, ...), dimensions={1} | concatenate | bytes 4718592 | tf_op jit(solution)/shard_map/concatenate | solution.py:126
  70.0 4.3 %fusion.80 = f32[2,16,576,64]{2,3,1,0:T(8,128)} fusion(bf16[2,64,16,64]{1,3,2,0:T(8,128)(2,1)} %bitcast.292, bf16[2,576,16,64]{1,3,2,0:T(8,128)(2,1)S(1)} %concatenate.151), kind=kOutput, calls=%fused_computation.133 | convolution fusion | flops 150994944 | bytes 7340032 | tf_op jit(solution)/shard_map/bihe,bjhe->bhij/dot_general | solution.py:61
  74.3 6.7 %concatenate.161 = bf16[2,576,16,64]{1,3,2,0:T(8,128)(2,1)} concatenate(bf16[2,64,16,64]{1,3,2,0:T(8,128)(2,1)} %bitcast.288, bf16[2,64,16,64]{1,3,2,0:T(8,128)(2,1)} %bitcast.277, bf16[2,64,16,64]{1,3,2,0:T(8,128)(2,1)} %bitcast.282, bf16[2,64,16,64]{1,3,2,0:T(8,128)(2,1)} %bitcast.287, bf16[2,64,16,64]{1,3,2,0:T(8,128)(2,1)S(1)} %bitcast.274, ...), dimensions={1} | concatenate | bytes 4718592 | tf_op jit(solution)/shard_map/concatenate | solution.py:123
  81.0 7.6 %bitcast_reduce_fusion = (f32[2,16,64]{2,1,0:T(8,128)S(1)}, f32[2,16,576,64]{2,3,1,0:T(8,128)}) fusion(pred[2,576]{1,0:T(4,128)(4,1)S(1)} %broadcast_in_dim.31, bf16[2,64,16,64]{1,3,2,0:T(8,128)(2,1)} %bitcast.294, bf16[2,576,16,64]{1,3,2,0:T(8,128)(2,1)} %concatenate.161), kind=kOutput, calls=%fused_computation.8 | convolution fusion | flops 310248000 | bytes 7349376 | tf_op jit(solution)/shard_map/sub | solution.py:53
  88.6 5.8 %convolution_bitcast_fusion = f32[2,576,16,64]{1,3,2,0:T(8,128)} fusion(bf16[2,64,16,64]{1,3,2,0:T(8,128)(2,1)S(1)} %bitcast.293, f32[2,16,576,64]{2,3,1,0:T(8,128)} %get-tuple-element.304, f32[2,16,64]{2,1,0:T(8,128)S(1)} %get-tuple-element.303), kind=kOutput, calls=%fused_computation.16 | convolution fusion | flops 153354240 | bytes 9707520 | tf_op jit(solution)/shard_map/bhij,bihe->bjhe/dot_general | solution.py:73
  94.4 21.4 %convolution_bitcast_fusion.1 = f32[2,576,16,64]{1,3,2,0:T(8,128)} fusion(bf16[2,64,16,64]{1,3,2,0:T(8,128)(2,1)} %bitcast.295, f32[2,16,576,64]{2,3,1,0:T(8,128)} %fusion.80, f32[2,16,576,64]{2,3,1,0:T(8,128)} %get-tuple-element.304, f32[2,16,64]{2,1,0:T(8,128)S(1)} %get-tuple-element.303), kind=kOutput, calls=%fused_computation.17 | convolution fusion | flops 159255104 | bytes 14426112 | tf_op jit(solution)/shard_map/bhij,bihe->bjhe/dot_general | solution.py:70
  115.8 8.5 %copy.125 = f32[2,576,16,64]{3,2,1,0:T(8,128)} copy(f32[2,576,16,64]{1,3,2,0:T(8,128)} %convolution_bitcast_fusion) | data formatting | bytes 9437184 | tf_op jit(solution)/shard_map/bhij,bihe->bjhe/transpose | solution.py:73
  124.3 8.9 %reshape.1034 = f32[2,9,64,1024]{3,2,1,0:T(8,128)} reshape(f32[2,576,16,64]{3,2,1,0:T(8,128)} %copy.125) | data formatting | bytes 9437184 | tf_op jit(solution)/shard_map/reshape | solution.py:81
  133.2 8.5 %copy.122 = f32[2,576,16,64]{3,2,1,0:T(8,128)} copy(f32[2,576,16,64]{1,3,2,0:T(8,128)} %convolution_bitcast_fusion.1) | data formatting | bytes 9437184 | tf_op jit(solution)/shard_map/bhij,bihe->bjhe/transpose | solution.py:70
  141.7 8.9 %reshape.1033 = f32[2,9,64,1024]{3,2,1,0:T(8,128)} reshape(f32[2,576,16,64]{3,2,1,0:T(8,128)} %copy.122) | data formatting | bytes 9437184 | tf_op jit(solution)/shard_map/reshape | solution.py:80
  155.8 2.0 fusion.43
  159.1 2.0 collective-permute-start.4
  162.3 15.7 %collective-permute-done.4 = bf16[2,3,64,1024]{3,2,1,0:T(8,128)(2,1)S(1)} collective-permute-done((bf16[2,3,64,1024]{3,2,1,0:T(8,128)(2,1)S(1)}, bf16[2,3,64,1024]{3,2,1,0:T(8,128)(2,1)S(1)}, u32[]{:S(2)}, u32[]{:S(2)}) %collective-permute-start.4) | collective-permute-done | bytes 786464 | tf_op jit(solution)/shard_map/ppermute | solution.py:15
  178.3 17.1 %collective-permute-done.5 = bf16[2,3,64,1024]{3,2,1,0:T(8,128)(2,1)S(1)} collective-permute-done((bf16[2,3,64,1024]{3,2,1,0:T(8,128)(2,1)S(1)}, bf16[2,3,64,1024]{3,2,1,0:T(8,128)(2,1)S(1)}, u32[]{:S(2)}, u32[]{:S(2)}) %collective-permute-start.5) | collective-permute-done | bytes 786464 | tf_op jit(solution)/shard_map/ppermute | solution.py:15
  197.6 3.2 %collective-permute-start.6 = (f32[2,2,64,1024]{3,2,1,0:T(8,128)}, f32[2,2,64,1024]{3,2,1,0:T(8,128)}, u32[]{:S(2)}, u32[]{:S(2)}) collective-permute-start(f32[2,2,64,1024]{3,2,1,0:T(8,128)} %get-tuple-element.276), channel_id=1, source_target_pairs={{4,0},{8,4},{12,8},{16,12},{20,16},{24,20},{28,24},{5,1},{9,5},{13... | collective-permute-start | bytes 3145736 | tf_op jit(solution)/shard_map/ppermute | solution.py:21
  200.8 3.2 %collective-permute-start.7 = (f32[2,2,64,1024]{3,2,1,0:T(8,128)}, f32[2,2,64,1024]{3,2,1,0:T(8,128)}, u32[]{:S(2)}, u32[]{:S(2)}) collective-permute-start(f32[2,2,64,1024]{3,2,1,0:T(8,128)} %get-tuple-element.277), channel_id=1, source_target_pairs={{0,4},{4,8},{8,12},{12,16},{16,20},{20,24},{24,28},{1,5},{5,9},{9,... | collective-permute-start | bytes 3145736 | tf_op jit(solution)/shard_map/ppermute | solution.py:21
  206.1 19.5 %fusion.20 = bf16[2,16,64,64]{3,2,1,0:T(8,128)(2,1)S(1)} fusion(bf16[2,576,16,64]{1,3,2,0:T(8,128)(2,1)} %concatenate.161, f32[2,16,576,64]{2,3,1,0:T(8,128)} %fusion.80, f32[2,16,576,64]{2,3,1,0:T(8,128)} %get-tuple-element.304, f32[2,16,64]{2,1,0:T(8,128)S(1)} %get-tuple-element.303), kind=kOutput, calls=%fused_computation.28 | convolution fusion | flops 159386176 | bytes 12066816 | tf_op jit(solution)/shard_map/bhij,bjhe->bihe/dot_general | solution.py:66
  226.5 2.9 %fusion.27 = bf16[2,1,2,64,1024]{4,3,2,1,0:T(8,128)(2,1)} fusion(f32[2,2,64,1024]{3,2,1,0:T(8,128)} %collective-permute-done.7, f32[2,2,64,1024]{3,2,1,0:T(8,128)} %collective-permute-done.6, f32[2,3,4,64,1024]{4,3,2,1,0:T(8,128)} %copy-done), kind=kLoop, calls=%fused_computation.38 | loop fusion | flops 786432 | bytes 3670016
  (85 shorter events, 45.4 us)
Async XLA Ops:
  0.6 20.2 %copy-start.6 = (s32[1,2,6]{2,1,0:T(2,128)S(1)}, s32[1,2,6]{2,1,0:T(2,128)}, u32[]{:S(2)}) copy-start(s32[1,2,6]{2,1,0:T(2,128)} %param.51) | copy-start | bytes 148
  0.6 20.5 %copy-start.4 = (bf16[1,2,64,1024]{3,2,1,0:T(8,128)(2,1)S(1)}, bf16[1,2,64,1024]{3,2,1,0:T(8,128)(2,1)}, u32[]{:S(2)}) copy-start(bf16[1,2,64,1024]{3,2,1,0:T(8,128)(2,1)} %param.48) | copy-start | bytes 786436
  0.7 21.5 %copy-start.5 = (bf16[1,2,64,1024]{3,2,1,0:T(8,128)(2,1)S(1)}, bf16[1,2,64,1024]{3,2,1,0:T(8,128)(2,1)}, u32[]{:S(2)}) copy-start(bf16[1,2,64,1024]{3,2,1,0:T(8,128)(2,1)} %param.50) | copy-start | bytes 786436
  0.7 13.0 %collective-permute-start = (bf16[2,1,2,64,1024]{4,3,2,1,0:T(8,128)(2,1)}, bf16[2,1,2,64,1024]{4,3,2,1,0:T(8,128)(2,1)S(1)}, u32[]{:S(2)}, u32[]{:S(2)}) collective-permute-start(bf16[2,1,2,64,1024]{4,3,2,1,0:T(8,128)(2,1)} %param.49), channel_id=1, source_target_pairs={{0,4},{4,8},{8,12},{12,16},{16,20},{20,24},{24,28},{28,0},{1,5},{5... | collective-permute-start | bytes 1572872 | tf_op jit(solution)/shard_map/ppermute | solution.py:31
  2.5 13.6 %collective-permute-start.1 = (bf16[2,1,2,64,1024]{4,3,2,1,0:T(8,128)(2,1)}, bf16[2,1,2,64,1024]{4,3,2,1,0:T(8,128)(2,1)S(1)}, u32[]{:S(2)}, u32[]{:S(2)}) collective-permute-start(bf16[2,1,2,64,1024]{4,3,2,1,0:T(8,128)(2,1)} %param.49), channel_id=1, source_target_pairs={{4,0},{8,4},{12,8},{16,12},{20,16},{24,20},{28,24},{0,28},{5,1},{9... | collective-permute-start | bytes 1572872 | tf_op jit(solution)/shard_map/ppermute | solution.py:33
  17.5 21.0 %collective-permute-start.3 = (bf16[2,3,1,64,1024]{4,3,2,1,0:T(8,128)(2,1)}, bf16[2,3,1,64,1024]{4,3,2,1,0:T(8,128)(2,1)}, u32[]{:S(2)}, u32[]{:S(2)}) collective-permute-start(bf16[2,3,1,64,1024]{4,3,2,1,0:T(8,128)(2,1)} %get-tuple-element.292), channel_id=1, source_target_pairs={{1,0},{2,1},{3,2},{0,3},{5,4},{6,5},{7,6},{4,7},{9,8},{10,9},{11,1... | collective-permute-start | bytes 2359304 | tf_op jit(solution)/shard_map/ppermute | solution.py:33
  20.8 34.7 %collective-permute-start.2 = (bf16[2,3,1,64,1024]{4,3,2,1,0:T(8,128)(2,1)}, bf16[2,3,1,64,1024]{4,3,2,1,0:T(8,128)(2,1)}, u32[]{:S(2)}, u32[]{:S(2)}) collective-permute-start(bf16[2,3,1,64,1024]{4,3,2,1,0:T(8,128)(2,1)} %get-tuple-element.293), channel_id=1, source_target_pairs={{0,1},{1,2},{2,3},{3,0},{4,5},{5,6},{6,7},{7,4},{8,9},{9,10},{10,1... | collective-permute-start | bytes 2359304 | tf_op jit(solution)/shard_map/ppermute | solution.py:31
  81.0 7.6 %copy-start.3 = (bf16[1,2,64,1024]{2,3,1,0:T(8,128)(2,1)S(1)}, bf16[1,2,64,1024]{2,3,1,0:T(8,128)(2,1)}, u32[]{:S(2)}) copy-start(bf16[1,2,64,1024]{2,3,1,0:T(8,128)(2,1)} %copy.170) | copy-start | bytes 786436
  150.6 2.5 %copy-start.1 = (f32[2,9,64,1024]{3,2,1,0:T(8,128)S(1)}, f32[2,9,64,1024]{3,2,1,0:T(8,128)}, u32[]{:S(2)}) copy-start(f32[2,9,64,1024]{3,2,1,0:T(8,128)} %reshape.1034) | copy-start | bytes 14155780
  151.8 3.0 %copy-start.2 = (f32[2,9,64,1024]{3,2,1,0:T(8,128)S(1)}, f32[2,9,64,1024]{3,2,1,0:T(8,128)}, u32[]{:S(2)}) copy-start(f32[2,9,64,1024]{3,2,1,0:T(8,128)} %reshape.1033) | copy-start | bytes 14155780
  159.1 18.9 %collective-permute-start.4 = (bf16[2,3,64,1024]{3,2,1,0:T(8,128)(2,1)S(1)}, bf16[2,3,64,1024]{3,2,1,0:T(8,128)(2,1)S(1)}, u32[]{:S(2)}, u32[]{:S(2)}) collective-permute-start(bf16[2,3,64,1024]{3,2,1,0:T(8,128)(2,1)S(1)} %get-tuple-element.279), channel_id=1, source_target_pairs={{0,3},{1,0},{2,1},{3,2},{4,7},{5,4},{6,5},{7,6},{8,11},{9,8},{10,9... | collective-permute-start | bytes 2359304 | tf_op jit(solution)/shard_map/ppermute | solution.py:15
  161.1 34.3 %collective-permute-start.5 = (bf16[2,3,64,1024]{3,2,1,0:T(8,128)(2,1)S(1)}, bf16[2,3,64,1024]{3,2,1,0:T(8,128)(2,1)S(1)}, u32[]{:S(2)}, u32[]{:S(2)}) collective-permute-start(bf16[2,3,64,1024]{3,2,1,0:T(8,128)(2,1)S(1)} %get-tuple-element.278), channel_id=1, source_target_pairs={{0,1},{1,2},{2,3},{3,0},{4,5},{5,6},{6,7},{7,4},{8,9},{9,10},{10,1... | collective-permute-start | bytes 2359304 | tf_op jit(solution)/shard_map/ppermute | solution.py:15
  162.3 41.8 %slice-start = ((s8[5242880]{0:T(1024)(128)(4,1)}), s8[1048576]{0:T(1024)(128)(4,1)S(1)}, s32[]{:S(2)}) async-start(s8[5242880]{0:T(1024)(128)(4,1)} %bitcast.298), calls=%async_computation | async-start | bytes 2097152
  178.3 25.8 %slice-start.1 = ((s8[5242880]{0:T(1024)(128)(4,1)}), s8[4194304]{0:T(1024)(128)(4,1)S(1)}, s32[]{:S(2)}) async-start(s8[5242880]{0:T(1024)(128)(4,1)} %bitcast.298), calls=%async_computation.1 | async-start | bytes 8388608
  195.9 9.3 %copy-start = (f32[2,3,4,64,1024]{4,3,2,1,0:T(8,128)}, f32[2,3,4,64,1024]{4,3,2,1,0:T(8,128)S(1)}, u32[]{:S(2)}) copy-start(f32[2,3,4,64,1024]{4,3,2,1,0:T(8,128)S(1)} %fusion.14) | copy-start | bytes 18874372
  197.6 28.9 %collective-permute-start.6 = (f32[2,2,64,1024]{3,2,1,0:T(8,128)}, f32[2,2,64,1024]{3,2,1,0:T(8,128)}, u32[]{:S(2)}, u32[]{:S(2)}) collective-permute-start(f32[2,2,64,1024]{3,2,1,0:T(8,128)} %get-tuple-element.276), channel_id=1, source_target_pairs={{4,0},{8,4},{12,8},{16,12},{20,16},{24,20},{28,24},{5,1},{9,5},{13... | collective-permute-start | bytes 3145736 | tf_op jit(solution)/shard_map/ppermute | solution.py:21
  200.8 25.7 %collective-permute-start.7 = (f32[2,2,64,1024]{3,2,1,0:T(8,128)}, f32[2,2,64,1024]{3,2,1,0:T(8,128)}, u32[]{:S(2)}, u32[]{:S(2)}) collective-permute-start(f32[2,2,64,1024]{3,2,1,0:T(8,128)} %get-tuple-element.277), channel_id=1, source_target_pairs={{0,4},{4,8},{8,12},{12,16},{16,20},{20,24},{24,28},{1,5},{5,9},{9,... | collective-permute-start | bytes 3145736 | tf_op jit(solution)/shard_map/ppermute | solution.py:21
where the time goes:
time: 232 us; the launch traced here: 229 us
  local copies, waits for them, and re-layouts  83.5 us (36%)
  matrix products  59.7 us (26%)
  waiting for transfers between devices  58.1 us (25%)
  starting transfers between devices  13.7 us (6%)
  other arithmetic  13.4 us (6%)
    ppermute x2, waiting for transfers between devices, shifted(): return lax.ppermute(value, axis, pairs)  32.8 us
    dot_general x1, matrix products, band_attend(): jnp.einsum('bhij,bihe->bjhe', score_grad, query_heads, preferred_element_...  21.4 us
    dot_general x1, matrix products, band_attend(): jnp.einsum('bhij,bjhe->bihe', score_grad, key_heads, preferred_element_ty...  19.5 us
    ppermute x2, waiting for transfers between devices, extended_2(): lax.ppermute(tail, axis, [(i, (i + 1) % count) for i in range(count)])  17.4 us
    slice x12, local copies, waits for them, and re-layouts, body(): extended[0, dr, dc:dc + sector_cols]  14.7 us
    slice x9, local copies, waits for them, and re-layouts, body(): extended[1, dr, dc:dc + sector_cols]  9.2 us
    reshape x1, local copies, waits for them, and re-layouts, band_attend(): grad_value.reshape(sector_cols, 9, CELLS, D)  8.88 us
    reshape x1, local copies, waits for them, and re-layouts, band_attend(): grad_key.reshape(sector_cols, 9, CELLS, D)  8.86 us
  transfers between devices with their start and end apart: 8, of which 6 were waited for; matrix products, arithmetic and copies ran while one was open for 20% of the time, Pallas kernels for 0%

commit v1 on v0

v1 whole, which is shorter than its diff:
```python
import jax
import jax.numpy as jnp
from jax import lax
from jax.experimental import pallas as pl
from jax.experimental.pallas import tpu as pltpu
from jax.sharding import PartitionSpec as P

HEAD_DIM = 64
GROUP = 4
LANES = GROUP * HEAD_DIM
LOG2E = 1.4426950408889634


def lon_shift(value, steps):
    count = lax.axis_size("lon")
    return lax.ppermute(value, "lon", [(i, (i + steps) % count) for i in range(count)])


def intra_swap(value):
    count = lax.axis_size("lat")
    return lax.ppermute(value, "lat", [(i, i ^ 1) for i in range(count) if i ^ 1 < count])


def inter_swap(value):
    count = lax.axis_size("lat")
    pairs = [(i, i + 1 if i % 2 else i - 1) for i in range(count)]
    return lax.ppermute(value, "lat", [(i, j) for i, j in pairs if 0 <= j < count])


def dot(a, b, dims):
    return lax.dot_general(a, b, (dims, ((), ())), preferred_element_type=jnp.float32)


def attention_kernel(
    slots,
    q_ref,
    c_ref,
    own_ref,
    intra_ref,
    inter_ref,
    west_ref,
    east_ref,
    side_ref,
    xk_ref,
    xwv_ref,
    xev_ref,
    att_ref,
    gq_ref,
    gown_ref,
    gside_ref,
    gintra_ref,
    ginter_ref,
    gxk_ref,
    gxwv_ref,
    gxev_ref,
    kv,
    grad,
):
    cols = q_ref.shape[1]
    cells = q_ref.shape[2]
    wide = cols + 2
    samples = slots.shape[1]
    scale = HEAD_DIM**-0.5
    for part in range(2):
        for c in range(cols):
            kv[part, c] = own_ref[part, 0, c]
            kv[part, wide + c] = intra_ref[part, 0, c]
            kv[part, 2 * wide + c] = inter_ref[part, 0, c]
        kv[part, cols] = west_ref[part, 0, 0]
        kv[part, cols + 1] = east_ref[part, 0, 0]
        kv[part, wide + cols] = side_ref[part, 0, 0]
        kv[part, wide + cols + 1] = side_ref[part, 0, 1]
    kv[0, 2 * wide + cols] = xk_ref[0, 0, 0]
    kv[0, 2 * wide + cols + 1] = xk_ref[0, 0, 1]
    kv[1, 2 * wide + cols] = xwv_ref[0, 0, 0]
    kv[1, 2 * wide + cols + 1] = xev_ref[0, 0, 0]
    grad[...] = jnp.zeros_like(grad)

    head = lax.broadcasted_iota(jnp.int32, (cells, LANES), 1) // HEAD_DIM
    masks = [head == h for h in range(GROUP)]

    def spread(rows):
        zero = jnp.zeros_like(rows)
        return jnp.concatenate([jnp.where(m, rows, zero) for m in masks], axis=0)

    def gathered(rows):
        out = rows[:cells]
        for h in range(1, GROUP):
            out = jnp.where(masks[h], rows[h * cells : (h + 1) * cells], out)
        return out

    for b in range(cols):
        listed = [slots[b, s] for s in range(samples)]
        query = spread(q_ref[0, b])
        upstream = spread(c_ref[0, b])
        keys = jnp.concatenate([kv[0, s] for s in listed], axis=0)
        values = jnp.concatenate([kv[1, s] for s in listed], axis=0)
        scores = dot(keys, query, ((1,), (1,)))
        highest = jnp.max(scores, axis=0, keepdims=True)
        raised = jnp.exp2((scores - highest) * (scale * LOG2E))
        weights = raised * (1.0 / jnp.sum(raised, axis=0, keepdims=True))
        low = weights.astype(jnp.bfloat16)
        pressure = dot(values, upstream, ((1,), (1,)))
        inner = jnp.sum(weights * pressure, axis=0, keepdims=True)
        score_grad = (weights * (pressure - inner) * scale).astype(jnp.bfloat16)
        att_ref[0, b] = gathered(dot(low, values, ((0,), (0,)))).astype(att_ref.dtype)
        gq_ref[0, b] = gathered(dot(score_grad, keys, ((0,), (0,)))).astype(gq_ref.dtype)
        grad_keys = dot(score_grad, query, ((1,), (0,)))
        grad_values = dot(low, upstream, ((1,), (0,)))
        for s in range(samples):
            grad[0, listed[s]] += grad_keys[s * cells : (s + 1) * cells]
            grad[1, listed[s]] += grad_values[s * cells : (s + 1) * cells]

    for part in range(2):
        for c in range(cols):
            gown_ref[part, 0, c] = grad[part, c]
            ginter_ref[part, 0, c] = grad[part, 2 * wide + c]
        for c in range(wide):
            gintra_ref[part, 0, c] = grad[part, wide + c].astype(gintra_ref.dtype)
        for side in range(2):
            gside_ref[part, 0, side] = grad[part, cols + side]
    for side in range(2):
        gxk_ref[0, 0, side] = grad[0, 2 * wide + cols + side].astype(gxk_ref.dtype)
    gxwv_ref[0, 0, 0] = grad[1, 2 * wide + cols].astype(gxwv_ref.dtype)
    gxev_ref[0, 0, 0] = grad[1, 2 * wide + cols + 1].astype(gxev_ref.dtype)


def attention(slots, operands):
    queries = operands[0]
    _, cols, cells, width = queries.shape
    wide = cols + 2

    def spec(shape):
        block = tuple(shape[:-1]) + (LANES,)
        lead = (0,) * (len(shape) - 1)
        return pl.BlockSpec(block, lambda g, s: lead + (g,))

    def out(lead, dtype):
        return jax.ShapeDtypeStruct(lead + (cells, width), dtype)

    low, full = jnp.bfloat16, jnp.float32
    outs = [
        out((1, cols), low),
        out((1, cols), low),
        out((2, 1, cols), full),
        out((2, 1, 2), full),
        out((2, 1, wide), low),
        out((2, 1, cols), full),
        out((1, 1, 2), low),
        out((1, 1, 1), low),
        out((1, 1, 1), low),
    ]
    keys = slots.shape[1] * cells
    flops = 2 * 6 * cols * width * GROUP * cells * keys
    moved = sum(x.size * x.dtype.itemsize for x in list(operands) + outs)
    return pl.pallas_call(
        attention_kernel,
        out_shape=outs,
        grid_spec=pltpu.PrefetchScalarGridSpec(
            num_scalar_prefetch=1,
            grid=(width // LANES,),
            in_specs=[spec(x.shape) for x in operands],
            out_specs=[spec(x.shape) for x in outs],
            scratch_shapes=[
                pltpu.VMEM((2, 3 * wide, cells, LANES), low),
                pltpu.VMEM((2, 3 * wide, cells, LANES), full),
            ],
        ),
        cost_estimate=pl.CostEstimate(
            flops=flops, bytes_accessed=moved, transcendentals=cols * width * keys
        ),
        name="attention",
    )(slots, *operands)


def block_slots(blocks, cols):
    sectors = cols * lax.axis_size("lon")
    lat, lon = lax.axis_index("lat"), lax.axis_index("lon")
    down = blocks // sectors - lat
    near = jnp.where(lat % 2 == 0, 1, -1)
    row = jnp.where(down == 0, 0, jnp.where(down == near, 1, 2))
    place = (blocks % sectors - lon * cols + 1) % sectors
    col = jnp.where(place == 0, cols, jnp.where(place <= cols, place - 1, cols + 1))
    return row * (cols + 2) + col


def body(queries, keys_values, cotangent, blocks):
    cols = queries.shape[1]
    slots = block_slots(blocks[0], cols)

    inter = inter_swap(keys_values)
    west = lon_shift(keys_values[:, :, cols - 1 :], 1)
    east = lon_shift(keys_values[:, :, :1], -1)
    intra = intra_swap(keys_values)
    west_values = lon_shift(inter[1:, :, cols - 1 :], 1)
    east_values = lon_shift(inter[1:, :, :1], -1)
    sides = jnp.concatenate([west, east], axis=2)
    corner_keys = inter_swap(sides[:1])
    intra_sides = intra_swap(sides)

    operands = (
        queries,
        cotangent,
        keys_values,
        intra,
        inter,
        west,
        east,
        intra_sides,
        corner_keys,
        west_values,
        east_values,
    )
    attended, grad_queries, own, side, to_intra, to_inter, to_xk, to_xwv, to_xev = attention(
        slots, operands
    )

    low, full = jnp.bfloat16, jnp.float32
    from_xk = inter_swap(to_xk).astype(full)
    from_xwv = lon_shift(to_xwv, -1).astype(full)
    from_xev = lon_shift(to_xev, 1).astype(full)
    from_intra = intra_swap(to_intra).astype(full)
    side = side + from_intra[:, :, cols:]
    side = jnp.concatenate([side[:1] + from_xk, side[1:]], axis=0).astype(low)
    from_east = lon_shift(side[:, :, :1], -1).astype(full)
    from_west = lon_shift(side[:, :, 1:], 1).astype(full)
    to_inter = to_inter.at[1:, :, cols - 1 :].add(from_xwv).at[1:, :, :1].add(from_xev)
    from_inter = inter_swap(to_inter.astype(low)).astype(full)
    own = own + from_intra[:, :, :cols] + from_inter
    own = own.at[:, :, cols - 1 :].add(from_east).at[:, :, :1].add(from_west)
    return (attended, grad_queries, own.astype(low))


def solution(mesh):
    placed = (
        P("lat", "lon", None, None),
        P(None, "lat", "lon", None, None),
        P("lat", "lon", None, None),
        P("lat", "lon", None),
    )
    return jax.shard_map(
        body,
        mesh=mesh,
        in_specs=placed,
        out_specs=(placed[0], placed[0], placed[1]),
        check_vma=False,
    )
```

time: 232 us -> 90.3 us (0.39)
  local copies, waits for them, and re-layouts: 83.5 us -> 2.61 us
  matrix products: 59.7 us -> 0 us
  waiting for transfers between devices: 58.1 us -> 46.1 us
  Pallas kernels: 0 us -> 10.1 us
  starting transfers between devices: 13.7 us -> 22.9 us
  other arithmetic: 13.4 us -> 7.51 us
    dot_general x5 -> x0, matrix products: 52.1 us -> none  [the longest x1 21.4 us: band_attend(): jnp.einsum('bhij,bihe->bjhe', score_grad, query_heads, preferred_element_...]
    slice x22 -> x4, local copies, waits for them, and re-layouts: 25.3 us -> 1.14 us  [the longest x1 1.07 us: body(): east = lon_shift(keys_values[:, :, :1], -1)]
    reshape x2 -> x0, local copies, waits for them, and re-layouts: 17.7 us -> none  [the longest x1 8.88 us: band_attend(): grad_value.reshape(sector_cols, 9, CELLS, D)]
    transpose x2 -> x0, local copies, waits for them, and re-layouts: 17.1 us -> none  [the longest x1 8.53 us: band_attend(): jnp.einsum('bhij,bihe->bjhe', weights_low, upstream_heads, preferred_elem...]
    ppermute x8 -> x15, waiting for transfers between devices: 58.1 us -> 46.1 us  [the longest x8 26.2 us: lon_shift(): lax.ppermute(value, 'lon', [(i, (i + steps) % count) for i in range(count)])]
    concatenate x3 -> x1, local copies, waits for them, and re-layouts: 12 us -> 0.02 us  [body(): sides = jnp.concatenate([west, east], axis=2)]
    pallas_call x0 -> x1, Pallas kernels: none -> 10.1 us  [attention(): pl.pallas_call(attention_kernel, out_shape=outs, grid_spec=pltpu.Prefetch...]
    ppermute x8 -> x15, starting transfers between devices: 13.7 us -> 22.9 us  [the longest x4 13.6 us: inter_swap(): lax.ppermute(value, 'lat', [(i, j) for i, j in pairs if 0 <= j < count])]
  transfers between devices with their start and end apart: 8 -> 15, of which waited for: 6 -> 10; matrix products, arithmetic and copies ran while one was open for 20% -> 7% of each run, Pallas kernels for 0% -> 0%
where the time goes in v1:
time: 90.3 us; the launch traced here: 90 us
  waiting for transfers between devices  46.1 us (51%)
  starting transfers between devices  22.9 us (25%)
  Pallas kernels  10.1 us (11%)
  other arithmetic  7.51 us (8%)
  local copies, waits for them, and re-layouts  2.61 us (3%)
    ppermute x8, waiting for transfers between devices, lon_shift(): lax.ppermute(value, 'lon', [(i, (i + steps) % count) for i in range(count)])  26.2 us
    ppermute x4, waiting for transfers between devices, inter_swap(): lax.ppermute(value, 'lat', [(i, j) for i, j in pairs if 0 <= j < count])  19.8 us
    ppermute x4, starting transfers between devices, inter_swap(): lax.ppermute(value, 'lat', [(i, j) for i, j in pairs if 0 <= j < count])  13.6 us
    pallas_call x1, Pallas kernels, attention(): pl.pallas_call(attention_kernel, out_shape=outs, grid_spec=pltpu.Prefetch...  10.1 us
    ppermute x8, starting transfers between devices, lon_shift(): lax.ppermute(value, 'lon', [(i, (i + steps) % count) for i in range(count)])  8.21 us
    scatter-add x2, other arithmetic, body(): to_inter.at[1:, :, cols - 1:].add(from_xwv).at[1:, :, :1].add(from_xev)  3.35 us
  transfers between devices with their start and end apart: 15, of which 10 were waited for; matrix products, arithmetic and copies ran while one was open for 7% of the time, Pallas kernels for 0%

profile of v1, /device:TPU:3, one launch (start us, length us, event | category | flops | bytes accessed | tf_op | source)
XLA Modules:
  0.0 90.0 jit_solution(2852601751449066323)
XLA Ops:
  0.6 1.1 %fusion.11 = (bf16[2,1,1,64,1024]{4,3,2,1,0:T(8,128)(2,1)S(1)}, bf16[2,1,1,64,1024]{4,3,2,1,0:T(8,128)(2,1)S(1)}) fusion(bf16[2,1,2,64,1024]{4,3,2,1,0:T(8,128)(2,1)} %own_ref.1), kind=kLoop, calls=%fused_computation.38 | loop fusion | bytes 1048576 | tf_op jit(solution)/shard_map/slice | solution.py:193
  1.7 1.3 %collective-permute-start.2 = (bf16[2,1,1,64,1024]{4,3,2,1,0:T(8,128)(2,1)S(1)}, bf16[2,1,1,64,1024]{4,3,2,1,0:T(8,128)(2,1)S(1)}, u32[]{:S(2)}, u32[]{:S(2)}) collective-permute-start(bf16[2,1,1,64,1024]{4,3,2,1,0:T(8,128)(2,1)S(1)} %get-tuple-element.76), channel_id=1, source_target_pairs={{0,1},{1,2},{2,3},{3,0},{4,5},{5,6},{6,7},{7,4},{8,9},{9,10},{10,1... | collective-permute-start | bytes 786440 | tf_op jit(solution)/shard_map/ppermute | solution.py:16
  3.1 4.0 %collective-permute-start.1 = (bf16[2,1,2,64,1024]{4,3,2,1,0:T(8,128)(2,1)}, bf16[2,1,2,64,1024]{4,3,2,1,0:T(8,128)(2,1)S(1)}, u32[]{:S(2)}, u32[]{:S(2)}) collective-permute-start(bf16[2,1,2,64,1024]{4,3,2,1,0:T(8,128)(2,1)} %own_ref.1), channel_id=1, source_target_pairs={{4,8},{8,4},{12,16},{16,12},{20,24},{24,20},{5,9},{9,5},{13,17},{1... | collective-permute-start | bytes 1572872 | tf_op jit(solution)/shard_map/ppermute | solution.py:27
  7.0 2.0 %collective-permute-start.3 = (bf16[2,1,1,64,1024]{4,3,2,1,0:T(8,128)(2,1)S(1)}, bf16[2,1,1,64,1024]{4,3,2,1,0:T(8,128)(2,1)S(1)}, u32[]{:S(2)}, u32[]{:S(2)}) collective-permute-start(bf16[2,1,1,64,1024]{4,3,2,1,0:T(8,128)(2,1)S(1)} %get-tuple-element.75), channel_id=1, source_target_pairs={{0,3},{1,0},{2,1},{3,2},{4,7},{5,4},{6,5},{7,6},{8,11},{9,8},{10,9... | collective-permute-start | bytes 786440 | tf_op jit(solution)/shard_map/ppermute | solution.py:16
  9.0 1.8 %collective-permute-done.2.west_ref = bf16[2,1,1,64,1024]{4,3,2,1,0:T(8,128)(2,1)S(1)} collective-permute-done((bf16[2,1,1,64,1024]{4,3,2,1,0:T(8,128)(2,1)S(1)}, bf16[2,1,1,64,1024]{4,3,2,1,0:T(8,128)(2,1)S(1)}, u32[]{:S(2)}, u32[]{:S(2)}) %collective-permute-start.2) | collective-permute-done | bytes 262176 | tf_op jit(solution)/shard_map/ppermute | solution.py:16
  10.9 6.6 %collective-permute-done.3.east_ref = bf16[2,1,1,64,1024]{4,3,2,1,0:T(8,128)(2,1)S(1)} collective-permute-done((bf16[2,1,1,64,1024]{4,3,2,1,0:T(8,128)(2,1)S(1)}, bf16[2,1,1,64,1024]{4,3,2,1,0:T(8,128)(2,1)S(1)}, u32[]{:S(2)}, u32[]{:S(2)}) %collective-permute-start.3) | collective-permute-done | bytes 262176 | tf_op jit(solution)/shard_map/ppermute | solution.py:16
  18.0 3.2 %collective-permute-start.5 = (bf16[1,1,2,64,1024]{4,3,2,1,0:T(8,128)(2,1)S(1)}, bf16[1,1,2,64,1024]{4,3,2,1,0:T(8,128)(2,1)S(1)}, u32[]{:S(2)}, u32[]{:S(2)}) collective-permute-start(bf16[1,1,2,64,1024]{4,3,2,1,0:T(8,128)(2,1)S(1)} %slice.194), channel_id=1, source_target_pairs={{4,8},{8,4},{12,16},{16,12},{20,24},{24,20},{5,9},{9,5},{13,17},{1... | collective-permute-start | bytes 786440 | tf_op jit(solution)/shard_map/ppermute | solution.py:27
  21.3 1.6 %collective-permute-start.7 = (bf16[1,1,1,64,1024]{4,3,2,1,0:T(8,128)(2,1)S(1)}, bf16[1,1,1,64,1024]{4,3,2,1,0:T(8,128)(2,1)S(1)}, u32[]{:S(2)}, u32[]{:S(2)}) collective-permute-start(bf16[1,1,1,64,1024]{4,3,2,1,0:T(8,128)(2,1)S(1)} %get-tuple-element.73), channel_id=1, source_target_pairs={{0,3},{1,0},{2,1},{3,2},{4,7},{5,4},{6,5},{7,6},{8,11},{9,8},{10,9... | collective-permute-start | bytes 393224 | tf_op jit(solution)/shard_map/ppermute | solution.py:16
  23.5 5.7 %collective-permute-done.5.xk_ref = bf16[1,1,2,64,1024]{4,3,2,1,0:T(8,128)(2,1)S(1)} collective-permute-done((bf16[1,1,2,64,1024]{4,3,2,1,0:T(8,128)(2,1)S(1)}, bf16[1,1,2,64,1024]{4,3,2,1,0:T(8,128)(2,1)S(1)}, u32[]{:S(2)}, u32[]{:S(2)}) %collective-permute-start.5) | collective-permute-done | bytes 262176 | tf_op jit(solution)/shard_map/ppermute | solution.py:27
  31.5 10.1 %attention.1 = (bf16[1,2,64,1024]{3,2,1,0:T(8,128)(2,1)}, bf16[1,2,64,1024]{3,2,1,0:T(8,128)(2,1)}, f32[2,1,2,64,1024]{4,3,2,1,0:T(8,128)}, f32[2,1,2,64,1024]{4...) custom-call(s32[2,6]{1,0:T(2,128)} %fusion.7.slots, ...), custom_call_target="tpu_custom_call" | custom-call | flops 2415919104 | bytes 8912896 | tf_op jit(solution)/shard_map/attention/pallas_call | solution.py:156
  41.6 1.2 %collective-permute-start.9 = (bf16[1,1,1,64,1024]{4,3,2,1,0:T(8,128)(2,1)}, bf16[1,1,1,64,1024]{4,3,2,1,0:T(8,128)(2,1)S(1)}, u32[]{:S(2)}, u32[]{:S(2)}) collective-permute-start(bf16[1,1,1,64,1024]{4,3,2,1,0:T(8,128)(2,1)} %get-tuple-element.65), channel_id=1, source_target_pairs={{0,3},{1,0},{2,1},{3,2},{4,7},{5,4},{6,5},{7,6},{8,11},{9,8},{10,9... | collective-permute-start | bytes 393224 | tf_op jit(solution)/shard_map/ppermute | solution.py:16
  43.9 2.5 %collective-permute-done.9 = bf16[1,1,1,64,1024]{4,3,2,1,0:T(8,128)(2,1)S(1)} collective-permute-done((bf16[1,1,1,64,1024]{4,3,2,1,0:T(8,128)(2,1)}, bf16[1,1,1,64,1024]{4,3,2,1,0:T(8,128)(2,1)S(1)}, u32[]{:S(2)}, u32[]{:S(2)}) %collective-permute-start.9) | collective-permute-done | bytes 131104 | tf_op jit(solution)/shard_map/ppermute | solution.py:16
  46.3 1.7 %add_dynamic-update-slice_fusion = f32[2,1,2,64,1024]{4,3,2,1,0:T(8,128)} fusion(f32[2,1,2,64,1024]{4,3,2,1,0:T(8,128)} %get-tuple-element.64, bf16[1,1,1,64,1024]{4,3,2,1,0:T(8,128)(2,1)S(1)} %collective-permute-done.9), kind=kLoop, calls=%fused_computation.16 | loop fusion | flops 131072 | bytes 655360 | tf_op jit(solution)/shard_map/scatter-add | solution.py:227
  48.0 2.4 %collective-permute-done.10 = bf16[1,1,1,64,1024]{4,3,2,1,0:T(8,128)(2,1)S(1)} collective-permute-done((bf16[1,1,1,64,1024]{4,3,2,1,0:T(8,128)(2,1)}, bf16[1,1,1,64,1024]{4,3,2,1,0:T(8,128)(2,1)S(1)}, u32[]{:S(2)}, u32[]{:S(2)}) %collective-permute-start.10) | collective-permute-done | bytes 131104 | tf_op jit(solution)/shard_map/ppermute | solution.py:16
  50.4 1.7 %fusion.5 = f32[2,1,2,64,1024]{4,3,2,1,0:T(8,128)} fusion(f32[2,1,2,64,1024]{4,3,2,1,0:T(8,128)} %add_dynamic-update-slice_fusion, bf16[1,1,1,64,1024]{4,3,2,1,0:T(8,128)(2,1)S(1)} %collective-permute-done.10), kind=kLoop, calls=%fused_computation.15 | loop fusion | flops 131072 | bytes 655360 | tf_op jit(solution)/shard_map/scatter-add | solution.py:227
  52.1 1.4 %convert_element_type.39 = bf16[2,1,2,64,1024]{4,3,2,1,0:T(8,128)(2,1)S(1)} convert(f32[2,1,2,64,1024]{4,3,2,1,0:T(8,128)} %fusion.5) | non-fusion elementwise | flops 262144 | bytes 1572864 | tf_op jit(solution)/shard_map/convert_element_type | solution.py:228
  53.6 4.3 %collective-permute-start.11 = (bf16[2,1,2,64,1024]{4,3,2,1,0:T(8,128)(2,1)S(1)}, bf16[2,1,2,64,1024]{4,3,2,1,0:T(8,128)(2,1)S(1)}, u32[]{:S(2)}, u32[]{:S(2)}) collective-permute-start(bf16[2,1,2,64,1024]{4,3,2,1,0:T(8,128)(2,1)S(1)} %convert_element_type.39), channel_id=1, source_target_pairs={{4,8},{8,4},{12,16},{16,12},{20,24},{24,20},{5,9},{9,5},{13,17},{1... | collective-permute-start | bytes 1572872 | tf_op jit(solution)/shard_map/ppermute | solution.py:27
  57.9 2.2 %collective-permute-start.12 = (bf16[1,1,2,64,1024]{4,3,2,1,0:T(8,128)(2,1)S(1)}, bf16[1,1,2,64,1024]{4,3,2,1,0:T(8,128)(2,1)S(1)}, u32[]{:S(2)}, u32[]{:S(2)}) collective-permute-start(bf16[1,1,2,64,1024]{4,3,2,1,0:T(8,128)(2,1)S(1)} %copy-done.8), channel_id=1, source_target_pairs={{4,8},{8,4},{12,16},{16,12},{20,24},{24,20},{5,9},{9,5},{13,17},{1... | collective-permute-start | bytes 786440 | tf_op jit(solution)/shard_map/ppermute | solution.py:27
  60.3 10.3 %collective-permute-done.11 = bf16[2,1,2,64,1024]{4,3,2,1,0:T(8,128)(2,1)S(1)} collective-permute-done((bf16[2,1,2,64,1024]{4,3,2,1,0:T(8,128)(2,1)S(1)}, bf16[2,1,2,64,1024]{4,3,2,1,0:T(8,128)(2,1)S(1)}, u32[]{:S(2)}, u32[]{:S(2)}) %collective-permute-start.11) | collective-permute-done | bytes 524320 | tf_op jit(solution)/shard_map/ppermute | solution.py:27
  71.3 3.8 %collective-permute-done.12 = bf16[1,1,2,64,1024]{4,3,2,1,0:T(8,128)(2,1)S(1)} collective-permute-done((bf16[1,1,2,64,1024]{4,3,2,1,0:T(8,128)(2,1)S(1)}, bf16[1,1,2,64,1024]{4,3,2,1,0:T(8,128)(2,1)S(1)}, u32[]{:S(2)}, u32[]{:S(2)}) %collective-permute-start.12) | collective-permute-done | bytes 262176 | tf_op jit(solution)/shard_map/ppermute | solution.py:27
  75.3 1.4 %collective-permute-start.13 = (bf16[2,1,1,64,1024]{4,3,2,1,0:T(8,128)(2,1)S(1)}, bf16[2,1,1,64,1024]{4,3,2,1,0:T(8,128)(2,1)S(1)}, u32[]{:S(2)}, u32[]{:S(2)}) collective-permute-start(bf16[2,1,1,64,1024]{4,3,2,1,0:T(8,128)(2,1)S(1)} %get-tuple-element.72), channel_id=1, source_target_pairs={{0,3},{1,0},{2,1},{3,2},{4,7},{5,4},{6,5},{7,6},{8,11},{9,8},{10,9... | collective-permute-start | bytes 786440 | tf_op jit(solution)/shard_map/ppermute | solution.py:16
  76.8 6.0 %collective-permute-done.13 = bf16[2,1,1,64,1024]{4,3,2,1,0:T(8,128)(2,1)S(1)} collective-permute-done((bf16[2,1,1,64,1024]{4,3,2,1,0:T(8,128)(2,1)S(1)}, bf16[2,1,1,64,1024]{4,3,2,1,0:T(8,128)(2,1)S(1)}, u32[]{:S(2)}, u32[]{:S(2)}) %collective-permute-start.13) | collective-permute-done | bytes 262176 | tf_op jit(solution)/shard_map/ppermute | solution.py:16
  82.9 6.1 %collective-permute-done.14 = bf16[2,1,1,64,1024]{4,3,2,1,0:T(8,128)(2,1)S(1)} collective-permute-done((bf16[2,1,1,64,1024]{4,3,2,1,0:T(8,128)(2,1)S(1)}, bf16[2,1,1,64,1024]{4,3,2,1,0:T(8,128)(2,1)S(1)}, u32[]{:S(2)}, u32[]{:S(2)}) %collective-permute-start.14) | collective-permute-done | bytes 262176 | tf_op jit(solution)/shard_map/ppermute | solution.py:16
  89.1 0.9 convert_element_type.44
  (48 shorter events, 6.0 us)
Async XLA Ops:
  0.6 22.2 %copy-start.5 = (s32[1,2,6]{2,1,0:T(2,128)S(1)}, s32[1,2,6]{2,1,0:T(2,128)}, u32[]{:S(2)}) copy-start(s32[1,2,6]{2,1,0:T(2,128)} %param.15) | copy-start | bytes 148
  1.7 9.2 %collective-permute-start.2 = (bf16[2,1,1,64,1024]{4,3,2,1,0:T(8,128)(2,1)S(1)}, bf16[2,1,1,64,1024]{4,3,2,1,0:T(8,128)(2,1)S(1)}, u32[]{:S(2)}, u32[]{:S(2)}) collective-permute-start(bf16[2,1,1,64,1024]{4,3,2,1,0:T(8,128)(2,1)S(1)} %get-tuple-element.76), channel_id=1, source_target_pairs={{0,1},{1,2},{2,3},{3,0},{4,5},{5,6},{6,7},{7,4},{8,9},{9,10},{10,1... | collective-permute-start | bytes 786440 | tf_op jit(solution)/shard_map/ppermute | solution.py:16
  3.1 18.1 %collective-permute-start.1 = (bf16[2,1,2,64,1024]{4,3,2,1,0:T(8,128)(2,1)}, bf16[2,1,2,64,1024]{4,3,2,1,0:T(8,128)(2,1)S(1)}, u32[]{:S(2)}, u32[]{:S(2)}) collective-permute-start(bf16[2,1,2,64,1024]{4,3,2,1,0:T(8,128)(2,1)} %own_ref.1), channel_id=1, source_target_pairs={{4,8},{8,4},{12,16},{16,12},{20,24},{24,20},{5,9},{9,5},{13,17},{1... | collective-permute-start | bytes 1572872 | tf_op jit(solution)/shard_map/ppermute | solution.py:27
  7.0 10.5 %collective-permute-start.3 = (bf16[2,1,1,64,1024]{4,3,2,1,0:T(8,128)(2,1)S(1)}, bf16[2,1,1,64,1024]{4,3,2,1,0:T(8,128)(2,1)S(1)}, u32[]{:S(2)}, u32[]{:S(2)}) collective-permute-start(bf16[2,1,1,64,1024]{4,3,2,1,0:T(8,128)(2,1)S(1)} %get-tuple-element.75), channel_id=1, source_target_pairs={{0,3},{1,0},{2,1},{3,2},{4,7},{5,4},{6,5},{7,6},{8,11},{9,8},{10,9... | collective-permute-start | bytes 786440 | tf_op jit(solution)/shard_map/ppermute | solution.py:16
  9.0 20.1 %collective-permute-start = (bf16[2,1,2,64,1024]{4,3,2,1,0:T(8,128)(2,1)}, bf16[2,1,2,64,1024]{4,3,2,1,0:T(8,128)(2,1)S(1)}, u32[]{:S(2)}, u32[]{:S(2)}) collective-permute-start(bf16[2,1,2,64,1024]{4,3,2,1,0:T(8,128)(2,1)} %own_ref.1), channel_id=1, source_target_pairs={{0,4},{4,0},{8,12},{12,8},{16,20},{20,16},{24,28},{28,24},{1,5},{5... | collective-permute-start | bytes 1572872 | tf_op jit(solution)/shard_map/ppermute | solution.py:21
  10.9 19.2 %copy-start.2 = (bf16[2,1,1,64,1024]{4,3,2,1,0:T(8,128)(2,1)}, bf16[2,1,1,64,1024]{4,3,2,1,0:T(8,128)(2,1)S(1)}, u32[]{:S(2)}) copy-start(bf16[2,1,1,64,1024]{4,3,2,1,0:T(8,128)(2,1)S(1)} %collective-permute-done.2.west_ref) | copy-start | bytes 786436
  17.5 12.5 %copy-start.3 = (bf16[2,1,1,64,1024]{4,3,2,1,0:T(8,128)(2,1)}, bf16[2,1,1,64,1024]{4,3,2,1,0:T(8,128)(2,1)S(1)}, u32[]{:S(2)}) copy-start(bf16[2,1,1,64,1024]{4,3,2,1,0:T(8,128)(2,1)S(1)} %collective-permute-done.3.east_ref) | copy-start | bytes 786436
  17.5 12.5 %collective-permute-start.4 = (bf16[2,1,2,64,1024]{4,3,2,1,0:T(8,128)(2,1)S(1)}, bf16[2,1,2,64,1024]{4,3,2,1,0:T(8,128)(2,1)S(1)}, u32[]{:S(2)}, u32[]{:S(2)}) collective-permute-start(bf16[2,1,2,64,1024]{4,3,2,1,0:T(8,128)(2,1)S(1)} %constant_dynamic-update-slice_fusion), channel_id=1, source_target_pairs={{0,4},{4,0},{8,12},{12,8},{16,20},{20,16},{24,28},{28,24},{1,5},{5... | collective-permute-start | bytes 1572872 | tf_op jit(solution)/shard_map/ppermute | solution.py:21
  18.0 11.2 %collective-permute-start.5 = (bf16[1,1,2,64,1024]{4,3,2,1,0:T(8,128)(2,1)S(1)}, bf16[1,1,2,64,1024]{4,3,2,1,0:T(8,128)(2,1)S(1)}, u32[]{:S(2)}, u32[]{:S(2)}) collective-permute-start(bf16[1,1,2,64,1024]{4,3,2,1,0:T(8,128)(2,1)S(1)} %slice.194), channel_id=1, source_target_pairs={{4,8},{8,4},{12,16},{16,12},{20,24},{24,20},{5,9},{9,5},{13,17},{1... | collective-permute-start | bytes 786440 | tf_op jit(solution)/shard_map/ppermute | solution.py:27
  21.2 8.8 %copy-start.4 = (bf16[2,1,2,64,1024]{4,3,2,1,0:T(8,128)(2,1)}, bf16[2,1,2,64,1024]{4,3,2,1,0:T(8,128)(2,1)S(1)}, u32[]{:S(2)}) copy-start(bf16[2,1,2,64,1024]{4,3,2,1,0:T(8,128)(2,1)S(1)} %collective-permute-done.1.inter_ref) | copy-start | bytes 1572868
  21.3 7.9 %collective-permute-start.7 = (bf16[1,1,1,64,1024]{4,3,2,1,0:T(8,128)(2,1)S(1)}, bf16[1,1,1,64,1024]{4,3,2,1,0:T(8,128)(2,1)S(1)}, u32[]{:S(2)}, u32[]{:S(2)}) collective-permute-start(bf16[1,1,1,64,1024]{4,3,2,1,0:T(8,128)(2,1)S(1)} %get-tuple-element.73), channel_id=1, source_target_pairs={{0,3},{1,0},{2,1},{3,2},{4,7},{5,4},{6,5},{7,6},{8,11},{9,8},{10,9... | collective-permute-start | bytes 393224 | tf_op jit(solution)/shard_map/ppermute | solution.py:16
  22.9 7.2 %collective-permute-start.6 = (bf16[1,1,1,64,1024]{4,3,2,1,0:T(8,128)(2,1)S(1)}, bf16[1,1,1,64,1024]{4,3,2,1,0:T(8,128)(2,1)S(1)}, u32[]{:S(2)}, u32[]{:S(2)}) collective-permute-start(bf16[1,1,1,64,1024]{4,3,2,1,0:T(8,128)(2,1)S(1)} %get-tuple-element.74), channel_id=1, source_target_pairs={{0,1},{1,2},{2,3},{3,0},{4,5},{5,6},{6,7},{7,4},{8,9},{9,10},{10,1... | collective-permute-start | bytes 393224 | tf_op jit(solution)/shard_map/ppermute | solution.py:16
  29.2 0.9 copy-start.6
  29.2 0.9 copy-start.10
  41.6 16.3 %copy-start.8 = (bf16[1,1,2,64,1024]{4,3,2,1,0:T(8,128)(2,1)S(1)}, bf16[1,1,2,64,1024]{4,3,2,1,0:T(8,128)(2,1)}, u32[]{:S(2)}) copy-start(bf16[1,1,2,64,1024]{4,3,2,1,0:T(8,128)(2,1)} %get-tuple-element.68) | copy-start | bytes 786436
  41.6 4.8 %collective-permute-start.9 = (bf16[1,1,1,64,1024]{4,3,2,1,0:T(8,128)(2,1)}, bf16[1,1,1,64,1024]{4,3,2,1,0:T(8,128)(2,1)S(1)}, u32[]{:S(2)}, u32[]{:S(2)}) collective-permute-start(bf16[1,1,1,64,1024]{4,3,2,1,0:T(8,128)(2,1)} %get-tuple-element.65), channel_id=1, source_target_pairs={{0,3},{1,0},{2,1},{3,2},{4,7},{5,4},{6,5},{7,6},{8,11},{9,8},{10,9... | collective-permute-start | bytes 393224 | tf_op jit(solution)/shard_map/ppermute | solution.py:16
  42.8 17.3 %collective-permute-start.8 = (bf16[2,1,4,64,1024]{4,3,2,1,0:T(8,128)(2,1)}, bf16[2,1,4,64,1024]{4,3,2,1,0:T(8,128)(2,1)S(1)}, u32[]{:S(2)}, u32[]{:S(2)}) collective-permute-start(bf16[2,1,4,64,1024]{4,3,2,1,0:T(8,128)(2,1)} %get-tuple-element.63), channel_id=1, source_target_pairs={{0,4},{4,0},{8,12},{12,8},{16,20},{20,16},{24,28},{28,24},{1,5},{5... | collective-permute-start | bytes 3145736 | tf_op jit(solution)/shard_map/ppermute | solution.py:21
  43.4 7.1 %collective-permute-start.10 = (bf16[1,1,1,64,1024]{4,3,2,1,0:T(8,128)(2,1)}, bf16[1,1,1,64,1024]{4,3,2,1,0:T(8,128)(2,1)S(1)}, u32[]{:S(2)}, u32[]{:S(2)}) collective-permute-start(bf16[1,1,1,64,1024]{4,3,2,1,0:T(8,128)(2,1)} %get-tuple-element.66), channel_id=1, source_target_pairs={{0,1},{1,2},{2,3},{3,0},{4,5},{5,6},{6,7},{7,4},{8,9},{9,10},{10,1... | collective-permute-start | bytes 393224 | tf_op jit(solution)/shard_map/ppermute | solution.py:16
  52.1 18.5 %copy-start = (f32[2,1,2,64,1024]{4,3,2,1,0:T(8,128)S(1)}, f32[2,1,2,64,1024]{4,3,2,1,0:T(8,128)}, u32[]{:S(2)}) copy-start(f32[2,1,2,64,1024]{4,3,2,1,0:T(8,128)} %get-tuple-element.62) | copy-start | bytes 3145732
  52.1 18.5 %copy-start.1 = (f32[2,1,2,64,1024]{4,3,2,1,0:T(8,128)S(1)}, f32[2,1,2,64,1024]{4,3,2,1,0:T(8,128)}, u32[]{:S(2)}) copy-start(f32[2,1,2,64,1024]{4,3,2,1,0:T(8,128)} %get-tuple-element.67) | copy-start | bytes 3145732
  53.6 17.0 %collective-permute-start.11 = (bf16[2,1,2,64,1024]{4,3,2,1,0:T(8,128)(2,1)S(1)}, bf16[2,1,2,64,1024]{4,3,2,1,0:T(8,128)(2,1)S(1)}, u32[]{:S(2)}, u32[]{:S(2)}) collective-permute-start(bf16[2,1,2,64,1024]{4,3,2,1,0:T(8,128)(2,1)S(1)} %convert_element_type.39), channel_id=1, source_target_pairs={{4,8},{8,4},{12,16},{16,12},{20,24},{24,20},{5,9},{9,5},{13,17},{1... | collective-permute-start | bytes 1572872 | tf_op jit(solution)/shard_map/ppermute | solution.py:27
  57.9 17.3 %collective-permute-start.12 = (bf16[1,1,2,64,1024]{4,3,2,1,0:T(8,128)(2,1)S(1)}, bf16[1,1,2,64,1024]{4,3,2,1,0:T(8,128)(2,1)S(1)}, u32[]{:S(2)}, u32[]{:S(2)}) collective-permute-start(bf16[1,1,2,64,1024]{4,3,2,1,0:T(8,128)(2,1)S(1)} %copy-done.8), channel_id=1, source_target_pairs={{4,8},{8,4},{12,16},{16,12},{20,24},{24,20},{5,9},{9,5},{13,17},{1... | collective-permute-start | bytes 786440 | tf_op jit(solution)/shard_map/ppermute | solution.py:27
  75.3 7.5 %collective-permute-start.13 = (bf16[2,1,1,64,1024]{4,3,2,1,0:T(8,128)(2,1)S(1)}, bf16[2,1,1,64,1024]{4,3,2,1,0:T(8,128)(2,1)S(1)}, u32[]{:S(2)}, u32[]{:S(2)}) collective-permute-start(bf16[2,1,1,64,1024]{4,3,2,1,0:T(8,128)(2,1)S(1)} %get-tuple-element.72), channel_id=1, source_target_pairs={{0,3},{1,0},{2,1},{3,2},{4,7},{5,4},{6,5},{7,6},{8,11},{9,8},{10,9... | collective-permute-start | bytes 786440 | tf_op jit(solution)/shard_map/ppermute | solution.py:16
  76.6 12.3 %collective-permute-start.14 = (bf16[2,1,1,64,1024]{4,3,2,1,0:T(8,128)(2,1)S(1)}, bf16[2,1,1,64,1024]{4,3,2,1,0:T(8,128)(2,1)S(1)}, u32[]{:S(2)}, u32[]{:S(2)}) collective-permute-start(bf16[2,1,1,64,1024]{4,3,2,1,0:T(8,128)(2,1)S(1)} %get-tuple-element.71), channel_id=1, source_target_pairs={{0,1},{1,2},{2,3},{3,0},{4,5},{5,6},{6,7},{7,4},{8,9},{9,10},{10,1... | collective-permute-start | bytes 786440 | tf_op jit(solution)/shard_map/ppermute | solution.py:16
  (3 other events, 2.3 us)

commit v2 on v1

--- a/solution.py
+++ b/solution.py
@@ -49,7 +49,8 @@
     gown_ref,
     gside_ref,
     gintra_ref,
-    ginter_ref,
+    gnk_ref,
+    gnv_ref,
     gxk_ref,
     gxwv_ref,
     gxev_ref,
@@ -111,10 +112,12 @@
             grad[0, listed[s]] += grad_keys[s * cells : (s + 1) * cells]
             grad[1, listed[s]] += grad_values[s * cells : (s + 1) * cells]
 
+    for c in range(cols):
+        gnk_ref[0, 0, c] = grad[0, 2 * wide + c].astype(gnk_ref.dtype)
+        gnv_ref[0, 0, c] = grad[1, 2 * wide + c]
     for part in range(2):
         for c in range(cols):
             gown_ref[part, 0, c] = grad[part, c]
-            ginter_ref[part, 0, c] = grad[part, 2 * wide + c]
         for c in range(wide):
             gintra_ref[part, 0, c] = grad[part, wide + c].astype(gintra_ref.dtype)
         for side in range(2):
@@ -145,7 +148,8 @@
         out((2, 1, cols), full),
         out((2, 1, 2), full),
         out((2, 1, wide), low),
-        out((2, 1, cols), full),
+        out((1, 1, cols), low),
+        out((1, 1, cols), full),
         out((1, 1, 2), low),
         out((1, 1, 1), low),
         out((1, 1, 1), low),
@@ -169,6 +173,7 @@
         cost_estimate=pl.CostEstimate(
             flops=flops, bytes_accessed=moved, transcendentals=cols * width * keys
         ),
+        compiler_params=pltpu.CompilerParams(vmem_limit_bytes=67043328),
         name="attention",
     )(slots, *operands)
 
@@ -184,19 +189,31 @@
     return row * (cols + 2) + col
 
 
+def edges(first, last, cols):
+    still = ((0, 0, 0),)
+    return lax.pad(first, jnp.zeros((), first.dtype), still * 2 + ((0, cols - 1, 0),) + still * 2) + lax.pad(
+        last, jnp.zeros((), last.dtype), still * 2 + ((cols - 1, 0, 0),) + still * 2
+    )
+
+
+def named(scope, move, *args):
+    with jax.named_scope(scope):
+        return move(*args)
+
+
 def body(queries, keys_values, cotangent, blocks):
     cols = queries.shape[1]
     slots = block_slots(blocks[0], cols)
 
-    inter = inter_swap(keys_values)
-    west = lon_shift(keys_values[:, :, cols - 1 :], 1)
-    east = lon_shift(keys_values[:, :, :1], -1)
-    intra = intra_swap(keys_values)
-    west_values = lon_shift(inter[1:, :, cols - 1 :], 1)
-    east_values = lon_shift(inter[1:, :, :1], -1)
+    west = named("in_west", lon_shift, keys_values[:, :, cols - 1 :], 1)
+    east = named("in_east", lon_shift, keys_values[:, :, :1], -1)
+    inter = named("in_inter", inter_swap, keys_values)
+    intra = named("in_intra", intra_swap, keys_values)
     sides = jnp.concatenate([west, east], axis=2)
-    corner_keys = inter_swap(sides[:1])
-    intra_sides = intra_swap(sides)
+    intra_sides = named("in_side", intra_swap, sides)
+    corner_keys = named("in_xk", inter_swap, sides[:1])
+    west_values = named("in_xwv", lon_shift, inter[1:, :, cols - 1 :], 1)
+    east_values = named("in_xev", lon_shift, inter[1:, :, :1], -1)
 
     operands = (
         queries,
@@ -211,23 +228,26 @@
         west_values,
         east_values,
     )
-    attended, grad_queries, own, side, to_intra, to_inter, to_xk, to_xwv, to_xev = attention(
-        slots, operands
-    )
+    outs = attention(slots, operands)
+    attended, grad_queries, own, side, to_intra, near_k, near_v, to_xk, to_xwv, to_xev = outs
 
     low, full = jnp.bfloat16, jnp.float32
-    from_xk = inter_swap(to_xk).astype(full)
-    from_xwv = lon_shift(to_xwv, -1).astype(full)
-    from_xev = lon_shift(to_xev, 1).astype(full)
-    from_intra = intra_swap(to_intra).astype(full)
+    from_xk = named("out_xk", inter_swap, to_xk).astype(full)
+    from_xwv = named("out_xwv", lon_shift, to_xwv, -1).astype(full)
+    from_xev = named("out_xev", lon_shift, to_xev, 1).astype(full)
+    from_intra = named("out_intra", intra_swap, to_intra).astype(full)
     side = side + from_intra[:, :, cols:]
-    side = jnp.concatenate([side[:1] + from_xk, side[1:]], axis=0).astype(low)
-    from_east = lon_shift(side[:, :, :1], -1).astype(full)
-    from_west = lon_shift(side[:, :, 1:], 1).astype(full)
-    to_inter = to_inter.at[1:, :, cols - 1 :].add(from_xwv).at[1:, :, :1].add(from_xev)
-    from_inter = inter_swap(to_inter.astype(low)).astype(full)
-    own = own + from_intra[:, :, :cols] + from_inter
-    own = own.at[:, :, cols - 1 :].add(from_east).at[:, :, :1].add(from_west)
+    side_k, side_v = (side[:1] + from_xk).astype(low), side[1:].astype(low)
+    from_east = named(
+        "out_east", lon_shift, jnp.concatenate([side_k[:, :, :1], side_v[:, :, :1]], axis=0), -1
+    )
+    from_west = named(
+        "out_west", lon_shift, jnp.concatenate([side_k[:, :, 1:], side_v[:, :, 1:]], axis=0), 1
+    )
+    near_v = (near_v + edges(from_xev, from_xwv, cols)).astype(low)
+    from_inter = named("out_inter", inter_swap, jnp.concatenate([near_k, near_v], axis=0))
+    own = own + from_intra[:, :, :cols] + from_inter.astype(full)
+    own = own + edges(from_west.astype(full), from_east.astype(full), cols)
     return (attended, grad_queries, own.astype(low))
 
 

time: 90.3 us -> 73.1 us (0.81)
  waiting for transfers between devices: 46.1 us -> 28.5 us
  starting transfers between devices: 22.9 us -> 26.6 us
  other arithmetic: 7.51 us -> 4.5 us
    ppermute x8, waiting for transfers between devices: 26.2 us -> 13.7 us  [lon_shift(): lax.ppermute(value, 'lon', [(i, (i + steps) % count) for i in range(count)])]
    ppermute x4, waiting for transfers between devices: 19.8 us -> 14.8 us  [inter_swap(): lax.ppermute(value, 'lat', [(i, j) for i, j in pairs if 0 <= j < count])]
    scatter-add x4 -> x0, other arithmetic: 3.59 us -> none  [the longest x2 3.35 us: body(): to_inter.at[1:, :, cols - 1:].add(from_xwv).at[1:, :, :1].add(from_xev)]
    ppermute x8, starting transfers between devices: 8.21 us -> 10.2 us  [lon_shift(): lax.ppermute(value, 'lon', [(i, (i + steps) % count) for i in range(count)])]
    ppermute x4, starting transfers between devices: 13.6 us -> 15.5 us  [inter_swap(): lax.ppermute(value, 'lat', [(i, j) for i, j in pairs if 0 <= j < count])]
    concatenate x1 -> x3, other arithmetic: 0.05 us -> 1.14 us  [the longest x1 1.09 us: body(): jnp.concatenate([near_k, near_v], axis=0)]
  transfers between devices with their start and end apart: 15 -> 15, of which waited for: 10 -> 8; matrix products, arithmetic and copies ran while one was open for 7% -> 5% of each run, Pallas kernels for 0% -> 0%
where the time goes in v2:
time: 73.1 us; the launch traced here: 72.8 us
  waiting for transfers between devices  28.5 us (39%)
  starting transfers between devices  26.6 us (36%)
  Pallas kernels  10 us (14%)
  other arithmetic  4.5 us (6%)
  local copies, waits for them, and re-layouts  2.19 us (3%)
  between operations  0.87 us (1%)
    ppermute x4, starting transfers between devices, inter_swap(): lax.ppermute(value, 'lat', [(i, j) for i, j in pairs if 0 <= j < count])  15.5 us
    ppermute x4, waiting for transfers between devices, inter_swap(): lax.ppermute(value, 'lat', [(i, j) for i, j in pairs if 0 <= j < count])  14.8 us
    ppermute x8, waiting for transfers between devices, lon_shift(): lax.ppermute(value, 'lon', [(i, (i + steps) % count) for i in range(count)])  13.7 us
    ppermute x8, starting transfers between devices, lon_shift(): lax.ppermute(value, 'lon', [(i, (i + steps) % count) for i in range(count)])  10.2 us
    pallas_call x1, Pallas kernels, attention(): pl.pallas_call(attention_kernel, out_shape=outs, grid_spec=pltpu.Prefetch...  10 us
  transfers between devices with their start and end apart: 15, of which 8 were waited for; matrix products, arithmetic and copies ran while one was open for 5% of the time, Pallas kernels for 0%

profile of v2, /device:TPU:3, one launch (start us, length us, event | category | flops | bytes accessed | tf_op | source)
XLA Modules:
  0.0 72.8 jit_solution(9236097415718974609)
XLA Ops:
  0.6 1.1 %fusion.11 = (bf16[2,1,1,64,1024]{4,3,2,1,0:T(8,128)(2,1)S(1)}, bf16[2,1,1,64,1024]{4,3,2,1,0:T(8,128)(2,1)S(1)}) fusion(bf16[2,1,2,64,1024]{4,3,2,1,0:T(8,128)(2,1)} %own_ref.1), kind=kLoop, calls=%fused_computation.34 | loop fusion | bytes 1048576 | tf_op jit(solution)/shard_map/slice | solution.py:209
  1.7 1.3 %collective-permute-start.2 = (bf16[2,1,1,64,1024]{4,3,2,1,0:T(8,128)(2,1)S(1)}, bf16[2,1,1,64,1024]{4,3,2,1,0:T(8,128)(2,1)S(1)}, u32[]{:S(2)}, u32[]{:S(2)}) collective-permute-start(bf16[2,1,1,64,1024]{4,3,2,1,0:T(8,128)(2,1)S(1)} %get-tuple-element.30), channel_id=1, source_target_pairs={{0,1},{1,2},{2,3},{3,0},{4,5},{5,6},{6,7},{7,4},{8,9},{9,10},{10,1... | collective-permute-start | bytes 786440 | tf_op jit(solution)/shard_map/in_west/ppermute | solution.py:16
  3.1 4.0 %collective-permute-start.1 = (bf16[2,1,2,64,1024]{4,3,2,1,0:T(8,128)(2,1)}, bf16[2,1,2,64,1024]{4,3,2,1,0:T(8,128)(2,1)S(1)}, u32[]{:S(2)}, u32[]{:S(2)}) collective-permute-start(bf16[2,1,2,64,1024]{4,3,2,1,0:T(8,128)(2,1)} %own_ref.1), channel_id=1, source_target_pairs={{4,8},{8,4},{12,16},{16,12},{20,24},{24,20},{5,9},{9,5},{13,17},{1... | collective-permute-start | bytes 1572872 | tf_op jit(solution)/shard_map/in_inter/ppermute | solution.py:27
  7.0 2.0 %collective-permute-start.3 = (bf16[2,1,1,64,1024]{4,3,2,1,0:T(8,128)(2,1)S(1)}, bf16[2,1,1,64,1024]{4,3,2,1,0:T(8,128)(2,1)S(1)}, u32[]{:S(2)}, u32[]{:S(2)}) collective-permute-start(bf16[2,1,1,64,1024]{4,3,2,1,0:T(8,128)(2,1)S(1)} %get-tuple-element.29), channel_id=1, source_target_pairs={{0,3},{1,0},{2,1},{3,2},{4,7},{5,4},{6,5},{7,6},{8,11},{9,8},{10,9... | collective-permute-start | bytes 786440 | tf_op jit(solution)/shard_map/in_east/ppermute | solution.py:16
  9.0 1.8 %collective-permute-done.2.west_ref = bf16[2,1,1,64,1024]{4,3,2,1,0:T(8,128)(2,1)S(1)} collective-permute-done((bf16[2,1,1,64,1024]{4,3,2,1,0:T(8,128)(2,1)S(1)}, bf16[2,1,1,64,1024]{4,3,2,1,0:T(8,128)(2,1)S(1)}, u32[]{:S(2)}, u32[]{:S(2)}) %collective-permute-start.2) | collective-permute-done | bytes 262176 | tf_op jit(solution)/shard_map/in_west/ppermute | solution.py:16
  10.9 6.6 %collective-permute-done.3.east_ref = bf16[2,1,1,64,1024]{4,3,2,1,0:T(8,128)(2,1)S(1)} collective-permute-done((bf16[2,1,1,64,1024]{4,3,2,1,0:T(8,128)(2,1)S(1)}, bf16[2,1,1,64,1024]{4,3,2,1,0:T(8,128)(2,1)S(1)}, u32[]{:S(2)}, u32[]{:S(2)}) %collective-permute-start.3) | collective-permute-done | bytes 262176 | tf_op jit(solution)/shard_map/in_east/ppermute | solution.py:16
  18.3 3.5 %collective-permute-start.5 = (bf16[1,1,2,64,1024]{4,3,2,1,0:T(8,128)(2,1)S(1)}, bf16[1,1,2,64,1024]{4,3,2,1,0:T(8,128)(2,1)S(1)}, u32[]{:S(2)}, u32[]{:S(2)}) collective-permute-start(bf16[1,1,2,64,1024]{4,3,2,1,0:T(8,128)(2,1)S(1)} %slice.52), channel_id=1, source_target_pairs={{4,8},{8,4},{12,16},{16,12},{20,24},{24,20},{5,9},{9,5},{13,17},{1... | collective-permute-start | bytes 786440 | tf_op jit(solution)/shard_map/in_xk/ppermute | solution.py:27
  21.8 1.7 %collective-permute-start.7 = (bf16[1,1,1,64,1024]{4,3,2,1,0:T(8,128)(2,1)S(1)}, bf16[1,1,1,64,1024]{4,3,2,1,0:T(8,128)(2,1)S(1)}, u32[]{:S(2)}, u32[]{:S(2)}) collective-permute-start(bf16[1,1,1,64,1024]{4,3,2,1,0:T(8,128)(2,1)S(1)} %get-tuple-element.27), channel_id=1, source_target_pairs={{0,3},{1,0},{2,1},{3,2},{4,7},{5,4},{6,5},{7,6},{8,11},{9,8},{10,9... | collective-permute-start | bytes 393224 | tf_op jit(solution)/shard_map/in_xev/ppermute | solution.py:16
  23.4 0.6 fusion.5.slots
  24.0 5.7 %collective-permute-done.5.xk_ref = bf16[1,1,2,64,1024]{4,3,2,1,0:T(8,128)(2,1)S(1)} collective-permute-done((bf16[1,1,2,64,1024]{4,3,2,1,0:T(8,128)(2,1)S(1)}, bf16[1,1,2,64,1024]{4,3,2,1,0:T(8,128)(2,1)S(1)}, u32[]{:S(2)}, u32[]{:S(2)}) %collective-permute-start.5) | collective-permute-done | bytes 262176 | tf_op jit(solution)/shard_map/in_xk/ppermute | solution.py:27
  29.8 0.8 %collective-permute-done.6.xwv_ref = bf16[1,1,1,64,1024]{4,3,2,1,0:T(8,128)(2,1)S(1)} collective-permute-done((bf16[1,1,1,64,1024]{4,3,2,1,0:T(8,128)(2,1)S(1)}, bf16[1,1,1,64,1024]{4,3,2,1,0:T(8,128)(2,1)S(1)}, u32[]{:S(2)}, u32[]{:S(2)}) %collective-permute-start.6) | collective-permute-done | bytes 131104 | tf_op jit(solution)/shard_map/in_xwv/ppermute | solution.py:16
  30.7 0.6 copy-done.9
  31.3 10.0 %attention.1 = (bf16[1,2,64,1024]{3,2,1,0:T(8,128)(2,1)}, bf16[1,2,64,1024]{3,2,1,0:T(8,128)(2,1)}, f32[2,1,2,64,1024]{4,3,2,1,0:T(8,128)}, f32[2,1,2,64,1024]{4...) custom-call(s32[2,6]{1,0:T(2,128)} %fusion.5.slots, ...), custom_call_target="tpu_custom_call" | custom-call | flops 2415919104 | bytes 8650752 | tf_op jit(solution)/shard_map/attention/pallas_call | solution.py:160
  41.9 0.8 %collective-permute-start.9 = (bf16[1,1,1,64,1024]{4,3,2,1,0:T(8,128)(2,1)}, bf16[1,1,1,64,1024]{4,3,2,1,0:T(8,128)(2,1)S(1)}, u32[]{:S(2)}, u32[]{:S(2)}) collective-permute-start(bf16[1,1,1,64,1024]{4,3,2,1,0:T(8,128)(2,1)} %get-tuple-element.19), channel_id=1, source_target_pairs={{0,1},{1,2},{2,3},{3,0},{4,5},{5,6},{6,7},{7,4},{8,9},{9,10},{10,1... | collective-permute-start | bytes 393224 | tf_op jit(solution)/shard_map/out_xev/ppermute | solution.py:16
  42.7 2.5 %collective-permute-start.10 = (bf16[1,1,1,64,1024]{4,3,2,1,0:T(8,128)(2,1)}, bf16[1,1,1,64,1024]{4,3,2,1,0:T(8,128)(2,1)S(1)}, u32[]{:S(2)}, u32[]{:S(2)}) collective-permute-start(bf16[1,1,1,64,1024]{4,3,2,1,0:T(8,128)(2,1)} %get-tuple-element.20), channel_id=1, source_target_pairs={{0,3},{1,0},{2,1},{3,2},{4,7},{5,4},{6,5},{7,6},{8,11},{9,8},{10,9... | collective-permute-start | bytes 393224 | tf_op jit(solution)/shard_map/out_xwv/ppermute | solution.py:16
  45.2 3.6 %collective-permute-start.12 = (bf16[1,1,2,64,1024]{4,3,2,1,0:T(8,128)(2,1)}, bf16[1,1,2,64,1024]{4,3,2,1,0:T(8,128)(2,1)S(1)}, u32[]{:S(2)}, u32[]{:S(2)}) collective-permute-start(bf16[1,1,2,64,1024]{4,3,2,1,0:T(8,128)(2,1)} %get-tuple-element.22), channel_id=1, source_target_pairs={{4,8},{8,4},{12,16},{16,12},{20,24},{24,20},{5,9},{9,5},{13,17},{1... | collective-permute-start | bytes 786440 | tf_op jit(solution)/shard_map/out_xk/ppermute | solution.py:27
  48.9 1.4 %collective-permute-done.10 = bf16[1,1,1,64,1024]{4,3,2,1,0:T(8,128)(2,1)S(1)} collective-permute-done((bf16[1,1,1,64,1024]{4,3,2,1,0:T(8,128)(2,1)}, bf16[1,1,1,64,1024]{4,3,2,1,0:T(8,128)(2,1)S(1)}, u32[]{:S(2)}, u32[]{:S(2)}) %collective-permute-start.10) | collective-permute-done | bytes 131104 | tf_op jit(solution)/shard_map/out_xwv/ppermute | solution.py:16
  50.4 1.1 %add_convert_fusion = bf16[1,1,2,64,1024]{4,3,2,1,0:T(8,128)(2,1)S(1)} fusion(f32[1,1,2,64,1024]{4,3,2,1,0:T(8,128)} %get-tuple-element.18, bf16[1,1,1,64,1024]{4,3,2,1,0:T(8,128)(2,1)S(1)} %collective-permute-done.10, bf16[1,1,1,64,1024]{4,3,2,1,0:T(8,128)(2,1)S(1)} %collective-permute-done.9), kind=kLoop, calls=%fused_computation.8 | loop fusion | flops 655360 | bytes 1048576 | tf_op jit(solution)/shard_map/convert_element_type | solution.py:247
  51.5 1.1 %pad_maximum_fusion = bf16[2,1,2,64,1024]{4,3,2,1,0:T(8,128)(2,1)S(1)} fusion(bf16[1,1,2,64,1024]{4,3,2,1,0:T(8,128)(2,1)S(1)} %add_convert_fusion, bf16[1,1,2,64,1024]{4,3,2,1,0:T(8,128)(2,1)} %get-tuple-element.17), kind=kLoop, calls=%fused_computation.7 | loop fusion | flops 262144 | bytes 1048576 | tf_op jit(solution)/shard_map/concatenate | solution.py:248
  52.6 4.5 %collective-permute-start.11 = (bf16[2,1,2,64,1024]{4,3,2,1,0:T(8,128)(2,1)S(1)}, bf16[2,1,2,64,1024]{4,3,2,1,0:T(8,128)(2,1)S(1)}, u32[]{:S(2)}, u32[]{:S(2)}) collective-permute-start(bf16[2,1,2,64,1024]{4,3,2,1,0:T(8,128)(2,1)S(1)} %pad_maximum_fusion), channel_id=1, source_target_pairs={{4,8},{8,4},{12,16},{16,12},{20,24},{24,20},{5,9},{9,5},{13,17},{1... | collective-permute-start | bytes 1572872 | tf_op jit(solution)/shard_map/out_inter/ppermute | solution.py:27
  57.7 1.9 %collective-permute-start.14 = (bf16[2,1,1,64,1024]{4,3,2,1,0:T(8,128)(2,1)S(1)}, bf16[2,1,1,64,1024]{4,3,2,1,0:T(8,128)(2,1)S(1)}, u32[]{:S(2)}, u32[]{:S(2)}) collective-permute-start(bf16[2,1,1,64,1024]{4,3,2,1,0:T(8,128)(2,1)S(1)} %pad_maximum_fusion.2), channel_id=1, source_target_pairs={{0,3},{1,0},{2,1},{3,2},{4,7},{5,4},{6,5},{7,6},{8,11},{9,8},{10,9... | collective-permute-start | bytes 786440 | tf_op jit(solution)/shard_map/out_east/ppermute | solution.py:16
  59.7 9.1 %collective-permute-done.11 = bf16[2,1,2,64,1024]{4,3,2,1,0:T(8,128)(2,1)S(1)} collective-permute-done((bf16[2,1,2,64,1024]{4,3,2,1,0:T(8,128)(2,1)S(1)}, bf16[2,1,2,64,1024]{4,3,2,1,0:T(8,128)(2,1)S(1)}, u32[]{:S(2)}, u32[]{:S(2)}) %collective-permute-start.11) | collective-permute-done | bytes 524320 | tf_op jit(solution)/shard_map/out_inter/ppermute | solution.py:27
  68.8 2.8 %collective-permute-done.13 = bf16[2,1,1,64,1024]{4,3,2,1,0:T(8,128)(2,1)S(1)} collective-permute-done((bf16[2,1,1,64,1024]{4,3,2,1,0:T(8,128)(2,1)S(1)}, bf16[2,1,1,64,1024]{4,3,2,1,0:T(8,128)(2,1)S(1)}, u32[]{:S(2)}, u32[]{:S(2)}) %collective-permute-start.13) | collective-permute-done | bytes 262176 | tf_op jit(solution)/shard_map/out_west/ppermute | solution.py:16
  71.6 1.1 %fusion.2 = bf16[2,1,2,64,1024]{4,3,2,1,0:T(8,128)(2,1)} fusion(f32[2,1,2,64,1024]{4,3,2,1,0:T(8,128)S(1)} %copy-done, f32[2,1,4,64,1024]{4,3,2,1,0:T(8,128)S(1)} %convert_element_type.23, bf16[2,1,2,64,1024]{4,3,2,1,0:T(8,128)(2,1)S(1)} %collective-permute-done.11, bf16[2,1,1,64,1024]{4,3,2,1,0:T(8,128)(2,1)S(1)} %collective-permute-done.14, ...), kind=kLoop, calls=%fused_computation.4 | loop fusion | flops 2097152 | bytes 3670016 | tf_op jit(solution)/shard_map/convert_element_type | solution.py:251
  (43 shorter events, 2.3 us)
Async XLA Ops:
  0.6 22.8 %copy-start.5 = (s32[1,2,6]{2,1,0:T(2,128)S(1)}, s32[1,2,6]{2,1,0:T(2,128)}, u32[]{:S(2)}) copy-start(s32[1,2,6]{2,1,0:T(2,128)} %param.7) | copy-start | bytes 148
  1.7 9.2 %collective-permute-start.2 = (bf16[2,1,1,64,1024]{4,3,2,1,0:T(8,128)(2,1)S(1)}, bf16[2,1,1,64,1024]{4,3,2,1,0:T(8,128)(2,1)S(1)}, u32[]{:S(2)}, u32[]{:S(2)}) collective-permute-start(bf16[2,1,1,64,1024]{4,3,2,1,0:T(8,128)(2,1)S(1)} %get-tuple-element.30), channel_id=1, source_target_pairs={{0,1},{1,2},{2,3},{3,0},{4,5},{5,6},{6,7},{7,4},{8,9},{9,10},{10,1... | collective-permute-start | bytes 786440 | tf_op jit(solution)/shard_map/in_west/ppermute | solution.py:16
  3.1 18.7 %collective-permute-start.1 = (bf16[2,1,2,64,1024]{4,3,2,1,0:T(8,128)(2,1)}, bf16[2,1,2,64,1024]{4,3,2,1,0:T(8,128)(2,1)S(1)}, u32[]{:S(2)}, u32[]{:S(2)}) collective-permute-start(bf16[2,1,2,64,1024]{4,3,2,1,0:T(8,128)(2,1)} %own_ref.1), channel_id=1, source_target_pairs={{4,8},{8,4},{12,16},{16,12},{20,24},{24,20},{5,9},{9,5},{13,17},{1... | collective-permute-start | bytes 1572872 | tf_op jit(solution)/shard_map/in_inter/ppermute | solution.py:27
  7.0 10.5 %collective-permute-start.3 = (bf16[2,1,1,64,1024]{4,3,2,1,0:T(8,128)(2,1)S(1)}, bf16[2,1,1,64,1024]{4,3,2,1,0:T(8,128)(2,1)S(1)}, u32[]{:S(2)}, u32[]{:S(2)}) collective-permute-start(bf16[2,1,1,64,1024]{4,3,2,1,0:T(8,128)(2,1)S(1)} %get-tuple-element.29), channel_id=1, source_target_pairs={{0,3},{1,0},{2,1},{3,2},{4,7},{5,4},{6,5},{7,6},{8,11},{9,8},{10,9... | collective-permute-start | bytes 786440 | tf_op jit(solution)/shard_map/in_east/ppermute | solution.py:16
  9.0 20.7 %collective-permute-start = (bf16[2,1,2,64,1024]{4,3,2,1,0:T(8,128)(2,1)}, bf16[2,1,2,64,1024]{4,3,2,1,0:T(8,128)(2,1)S(1)}, u32[]{:S(2)}, u32[]{:S(2)}) collective-permute-start(bf16[2,1,2,64,1024]{4,3,2,1,0:T(8,128)(2,1)} %own_ref.1), channel_id=1, source_target_pairs={{0,4},{4,0},{8,12},{12,8},{16,20},{20,16},{24,28},{28,24},{1,5},{5... | collective-permute-start | bytes 1572872 | tf_op jit(solution)/shard_map/in_intra/ppermute | solution.py:21
  10.9 6.7 %copy-start.2 = (bf16[2,1,1,64,1024]{4,3,2,1,0:T(8,128)(2,1)}, bf16[2,1,1,64,1024]{4,3,2,1,0:T(8,128)(2,1)S(1)}, u32[]{:S(2)}) copy-start(bf16[2,1,1,64,1024]{4,3,2,1,0:T(8,128)(2,1)S(1)} %collective-permute-done.2.west_ref) | copy-start | bytes 786436
  17.5 0.7 copy-start.3
  17.5 13.8 %collective-permute-start.4 = (bf16[2,1,2,64,1024]{4,3,2,1,0:T(8,128)(2,1)S(1)}, bf16[2,1,2,64,1024]{4,3,2,1,0:T(8,128)(2,1)}, u32[]{:S(2)}, u32[]{:S(2)}) collective-permute-start(bf16[2,1,2,64,1024]{4,3,2,1,0:T(8,128)(2,1)S(1)} %constant_dynamic-update-slice_fusion), channel_id=1, source_target_pairs={{0,4},{4,0},{8,12},{12,8},{16,20},{20,16},{24,28},{28,24},{1,5},{5... | collective-permute-start | bytes 1572872 | tf_op jit(solution)/shard_map/in_side/ppermute | solution.py:21
  18.3 11.5 %collective-permute-start.5 = (bf16[1,1,2,64,1024]{4,3,2,1,0:T(8,128)(2,1)S(1)}, bf16[1,1,2,64,1024]{4,3,2,1,0:T(8,128)(2,1)S(1)}, u32[]{:S(2)}, u32[]{:S(2)}) collective-permute-start(bf16[1,1,2,64,1024]{4,3,2,1,0:T(8,128)(2,1)S(1)} %slice.52), channel_id=1, source_target_pairs={{4,8},{8,4},{12,16},{16,12},{20,24},{24,20},{5,9},{9,5},{13,17},{1... | collective-permute-start | bytes 786440 | tf_op jit(solution)/shard_map/in_xk/ppermute | solution.py:27
  21.7 8.0 %copy-start.4 = (bf16[2,1,2,64,1024]{4,3,2,1,0:T(8,128)(2,1)}, bf16[2,1,2,64,1024]{4,3,2,1,0:T(8,128)(2,1)S(1)}, u32[]{:S(2)}) copy-start(bf16[2,1,2,64,1024]{4,3,2,1,0:T(8,128)(2,1)S(1)} %collective-permute-done.1.inter_ref) | copy-start | bytes 1572868
  21.8 8.0 %collective-permute-start.7 = (bf16[1,1,1,64,1024]{4,3,2,1,0:T(8,128)(2,1)S(1)}, bf16[1,1,1,64,1024]{4,3,2,1,0:T(8,128)(2,1)S(1)}, u32[]{:S(2)}, u32[]{:S(2)}) collective-permute-start(bf16[1,1,1,64,1024]{4,3,2,1,0:T(8,128)(2,1)S(1)} %get-tuple-element.27), channel_id=1, source_target_pairs={{0,3},{1,0},{2,1},{3,2},{4,7},{5,4},{6,5},{7,6},{8,11},{9,8},{10,9... | collective-permute-start | bytes 393224 | tf_op jit(solution)/shard_map/in_xev/ppermute | solution.py:16
  23.4 7.2 %collective-permute-start.6 = (bf16[1,1,1,64,1024]{4,3,2,1,0:T(8,128)(2,1)S(1)}, bf16[1,1,1,64,1024]{4,3,2,1,0:T(8,128)(2,1)S(1)}, u32[]{:S(2)}, u32[]{:S(2)}) collective-permute-start(bf16[1,1,1,64,1024]{4,3,2,1,0:T(8,128)(2,1)S(1)} %get-tuple-element.28), channel_id=1, source_target_pairs={{0,1},{1,2},{2,3},{3,0},{4,5},{5,6},{6,7},{7,4},{8,9},{9,10},{10,1... | collective-permute-start | bytes 393224 | tf_op jit(solution)/shard_map/in_xwv/ppermute | solution.py:16
  29.8 0.8 %copy-start.7 = (bf16[1,1,2,64,1024]{4,3,2,1,0:T(8,128)(2,1)}, bf16[1,1,2,64,1024]{4,3,2,1,0:T(8,128)(2,1)S(1)}, u32[]{:S(2)}) copy-start(bf16[1,1,2,64,1024]{4,3,2,1,0:T(8,128)(2,1)S(1)} %collective-permute-done.5.xk_ref) | copy-start | bytes 786436
  29.8 0.9 %copy-start.6 = (bf16[2,1,2,64,1024]{4,3,2,1,0:T(8,128)(2,1)}, bf16[2,1,2,64,1024]{4,3,2,1,0:T(8,128)(2,1)S(1)}, u32[]{:S(2)}) copy-start(bf16[2,1,2,64,1024]{4,3,2,1,0:T(8,128)(2,1)S(1)} %collective-permute-done.intra_ref) | copy-start | bytes 1572868
  29.8 0.9 %copy-start.8 = (bf16[1,1,1,64,1024]{4,3,2,1,0:T(8,128)(2,1)}, bf16[1,1,1,64,1024]{4,3,2,1,0:T(8,128)(2,1)S(1)}, u32[]{:S(2)}) copy-start(bf16[1,1,1,64,1024]{4,3,2,1,0:T(8,128)(2,1)S(1)} %collective-permute-done.7.xev_ref) | copy-start | bytes 393220
  41.4 15.7 %collective-permute-start.8 = (bf16[2,1,4,64,1024]{4,3,2,1,0:T(8,128)(2,1)}, bf16[2,1,4,64,1024]{4,3,2,1,0:T(8,128)(2,1)S(1)}, u32[]{:S(2)}, u32[]{:S(2)}) collective-permute-start(bf16[2,1,4,64,1024]{4,3,2,1,0:T(8,128)(2,1)} %get-tuple-element.16), channel_id=1, source_target_pairs={{0,4},{4,0},{8,12},{12,8},{16,20},{20,16},{24,28},{28,24},{1,5},{5... | collective-permute-start | bytes 3145736 | tf_op jit(solution)/shard_map/out_intra/ppermute | solution.py:21
  41.9 7.0 %collective-permute-start.9 = (bf16[1,1,1,64,1024]{4,3,2,1,0:T(8,128)(2,1)}, bf16[1,1,1,64,1024]{4,3,2,1,0:T(8,128)(2,1)S(1)}, u32[]{:S(2)}, u32[]{:S(2)}) collective-permute-start(bf16[1,1,1,64,1024]{4,3,2,1,0:T(8,128)(2,1)} %get-tuple-element.19), channel_id=1, source_target_pairs={{0,1},{1,2},{2,3},{3,0},{4,5},{5,6},{6,7},{7,4},{8,9},{9,10},{10,1... | collective-permute-start | bytes 393224 | tf_op jit(solution)/shard_map/out_xev/ppermute | solution.py:16
  42.7 7.7 %collective-permute-start.10 = (bf16[1,1,1,64,1024]{4,3,2,1,0:T(8,128)(2,1)}, bf16[1,1,1,64,1024]{4,3,2,1,0:T(8,128)(2,1)S(1)}, u32[]{:S(2)}, u32[]{:S(2)}) collective-permute-start(bf16[1,1,1,64,1024]{4,3,2,1,0:T(8,128)(2,1)} %get-tuple-element.20), channel_id=1, source_target_pairs={{0,3},{1,0},{2,1},{3,2},{4,7},{5,4},{6,5},{7,6},{8,11},{9,8},{10,9... | collective-permute-start | bytes 393224 | tf_op jit(solution)/shard_map/out_xwv/ppermute | solution.py:16
  45.2 12.5 %collective-permute-start.12 = (bf16[1,1,2,64,1024]{4,3,2,1,0:T(8,128)(2,1)}, bf16[1,1,2,64,1024]{4,3,2,1,0:T(8,128)(2,1)S(1)}, u32[]{:S(2)}, u32[]{:S(2)}) collective-permute-start(bf16[1,1,2,64,1024]{4,3,2,1,0:T(8,128)(2,1)} %get-tuple-element.22), channel_id=1, source_target_pairs={{4,8},{8,4},{12,16},{16,12},{20,24},{24,20},{5,9},{9,5},{13,17},{1... | collective-permute-start | bytes 786440 | tf_op jit(solution)/shard_map/out_xk/ppermute | solution.py:27
  51.5 5.9 %copy-start.1 = (f32[2,1,2,64,1024]{4,3,2,1,0:T(8,128)S(1)}, f32[2,1,2,64,1024]{4,3,2,1,0:T(8,128)}, u32[]{:S(2)}) copy-start(f32[2,1,2,64,1024]{4,3,2,1,0:T(8,128)} %get-tuple-element.21) | copy-start | bytes 3145732
  52.6 16.2 %collective-permute-start.11 = (bf16[2,1,2,64,1024]{4,3,2,1,0:T(8,128)(2,1)S(1)}, bf16[2,1,2,64,1024]{4,3,2,1,0:T(8,128)(2,1)S(1)}, u32[]{:S(2)}, u32[]{:S(2)}) collective-permute-start(bf16[2,1,2,64,1024]{4,3,2,1,0:T(8,128)(2,1)S(1)} %pad_maximum_fusion), channel_id=1, source_target_pairs={{4,8},{8,4},{12,16},{16,12},{20,24},{24,20},{5,9},{9,5},{13,17},{1... | collective-permute-start | bytes 1572872 | tf_op jit(solution)/shard_map/out_inter/ppermute | solution.py:27
  57.6 14.1 %copy-start = (f32[2,1,2,64,1024]{4,3,2,1,0:T(8,128)S(1)}, f32[2,1,2,64,1024]{4,3,2,1,0:T(8,128)}, u32[]{:S(2)}) copy-start(f32[2,1,2,64,1024]{4,3,2,1,0:T(8,128)} %get-tuple-element.15) | copy-start | bytes 3145732
  57.7 11.1 %collective-permute-start.14 = (bf16[2,1,1,64,1024]{4,3,2,1,0:T(8,128)(2,1)S(1)}, bf16[2,1,1,64,1024]{4,3,2,1,0:T(8,128)(2,1)S(1)}, u32[]{:S(2)}, u32[]{:S(2)}) collective-permute-start(bf16[2,1,1,64,1024]{4,3,2,1,0:T(8,128)(2,1)S(1)} %pad_maximum_fusion.2), channel_id=1, source_target_pairs={{0,3},{1,0},{2,1},{3,2},{4,7},{5,4},{6,5},{7,6},{8,11},{9,8},{10,9... | collective-permute-start | bytes 786440 | tf_op jit(solution)/shard_map/out_east/ppermute | solution.py:16
  59.6 12.0 %collective-permute-start.13 = (bf16[2,1,1,64,1024]{4,3,2,1,0:T(8,128)(2,1)S(1)}, bf16[2,1,1,64,1024]{4,3,2,1,0:T(8,128)(2,1)S(1)}, u32[]{:S(2)}, u32[]{:S(2)}) collective-permute-start(bf16[2,1,1,64,1024]{4,3,2,1,0:T(8,128)(2,1)S(1)} %pad_maximum_fusion.1), channel_id=1, source_target_pairs={{0,1},{1,2},{2,3},{3,0},{4,5},{5,6},{6,7},{7,4},{8,9},{9,10},{10,1... | collective-permute-start | bytes 786440 | tf_op jit(solution)/shard_map/out_west/ppermute | solution.py:16
  (1 other events, 0.6 us)

commit v3 on v1

v3 whole, which is shorter than its diff:
```python
import jax
import jax.numpy as jnp
from jax import lax
from jax.experimental import pallas as pl
from jax.experimental.pallas import tpu as pltpu
from jax.sharding import PartitionSpec as P


HEAD_DIM = 64
GROUP = 4
LANES = GROUP * HEAD_DIM
LOG2E = 1.4426950408889634


def lon_shift(value, steps):
    count = lax.axis_size("lon")
    return lax.ppermute(value, "lon", [(i, (i + steps) % count) for i in range(count)])


def intra_swap(value):
    count = lax.axis_size("lat")
    return lax.ppermute(value, "lat", [(i, i ^ 1) for i in range(count) if i ^ 1 < count])


def inter_swap(value):
    count = lax.axis_size("lat")
    pairs = [(i, i + 1 if i % 2 else i - 1) for i in range(count)]
    return lax.ppermute(value, "lat", [(i, j) for i, j in pairs if 0 <= j < count])


def dot(a, b, dims):
    return lax.dot_general(a, b, (dims, ((), ())), preferred_element_type=jnp.float32)


def attention_kernel(
    slots,
    places,
    q_ref,
    c_ref,
    own_ref,
    intra_ref,
    ik_ref,
    iv_ref,
    wk_ref,
    ek_ref,
    wv_ref,
    ev_ref,
    sk_ref,
    sw_ref,
    se_ref,
    ck_ref,
    cw_ref,
    ce_ref,
    att_ref,
    gq_ref,
    gown_ref,
    gsk_ref,
    gsv_ref,
    gintra_ref,
    gik_ref,
    giv_ref,
    gck_ref,
    gcw_ref,
    gce_ref,
    kv,
    grad,
    sems,
):
    _, cols, cells, width = q_ref.shape
    wide = cols + 2
    samples = slots.shape[1]
    groups = width // LANES
    scale = HEAD_DIM**-0.5
    low = jnp.bfloat16

    near, far = pl.ds(0, cols), pl.ds(2 * wide, cols)
    moves = (
        (own_ref, slice(None), 0, near),
        (intra_ref, slice(None), 0, pl.ds(wide, cols)),
        (ik_ref, pl.ds(0, 1), 0, far),
        (iv_ref, pl.ds(1, 1), 0, far),
        (wk_ref, pl.ds(0, 1), 0, pl.ds(cols, 1)),
        (ek_ref, pl.ds(0, 1), 0, pl.ds(cols + 1, 1)),
        (wv_ref, pl.ds(1, 1), 0, pl.ds(cols, 1)),
        (ev_ref, pl.ds(1, 1), 0, pl.ds(cols + 1, 1)),
        (sk_ref, pl.ds(0, 1), 0, pl.ds(wide + cols, 2)),
        (sw_ref, pl.ds(1, 1), 0, pl.ds(wide + cols, 1)),
        (se_ref, pl.ds(1, 1), 0, pl.ds(wide + cols + 1, 1)),
        (ck_ref, pl.ds(0, 1), 0, pl.ds(2 * wide + cols, 2)),
        (cw_ref, pl.ds(1, 1), 0, pl.ds(2 * wide + cols, 1)),
        (ce_ref, pl.ds(1, 1), 0, pl.ds(2 * wide + cols + 1, 1)),
    )

    def copies(g):
        lanes = pl.ds(0, LANES) if g == 0 else pl.ds(LANES, width - LANES)
        return [
            pltpu.make_async_copy(
                ref.at[:, row, :, :, lanes], kv.at[part, place, :, lanes], sems.at[g, i]
            )
            for i, (ref, part, row, place) in enumerate(moves)
        ]

    pieces = range(min(groups, 2))
    for piece in pieces:
        for copy in copies(piece):
            copy.start()
    for b in range(cols):
        for part in range(2):
            grad[b, part, samples] = jnp.zeros((cells, LANES), jnp.float32)

    head = lax.broadcasted_iota(jnp.int32, (cells, LANES), 1) // HEAD_DIM
    masks = [head == h for h in range(GROUP)]

    def spread(rows):
        zero = jnp.zeros_like(rows)
        return jnp.concatenate([jnp.where(m, rows, zero) for m in masks], axis=0)

    def gathered(rows):
        out = rows[:cells]
        for h in range(1, GROUP):
            out = jnp.where(masks[h], rows[h * cells : (h + 1) * cells], out)
        return out

    def step(g):
        lanes = pl.ds(g * LANES, LANES)
        if g in pieces:
            for copy in copies(g):
                copy.wait()
        spans = range(cols)
        listed = [[slots[b, s] for s in range(samples)] for b in spans]
        query = [spread(q_ref[0, b, :, lanes]) for b in spans]
        upstream = [spread(c_ref[0, b, :, lanes]) for b in spans]
        keys = [jnp.concatenate([kv[0, s, :, lanes] for s in x], axis=0) for x in listed]
        values = [jnp.concatenate([kv[1, s, :, lanes] for s in x], axis=0) for x in listed]
        scores = [dot(keys[b], query[b], ((1,), (1,))) for b in spans]
        pressure = [dot(values[b], upstream[b], ((1,), (1,))) for b in spans]
        for b in spans:
            highest = jnp.max(scores[b], axis=0, keepdims=True)
            raised = jnp.exp2((scores[b] - highest) * (scale * LOG2E))
            weights = raised * (1.0 / jnp.sum(raised, axis=0, keepdims=True))
            weights_low = weights.astype(low)
            inner = jnp.sum(weights * pressure[b], axis=0, keepdims=True)
            score_grad = (weights * (pressure[b] - inner) * scale).astype(low)
            grad_values = dot(weights_low, upstream[b], ((1,), (0,)))
            grad_keys = dot(score_grad, query[b], ((1,), (0,)))
            att_ref[0, b, :, lanes] = gathered(dot(weights_low, values[b], ((0,), (0,)))).astype(low)
            gq_ref[0, b, :, lanes] = gathered(dot(score_grad, keys[b], ((0,), (0,)))).astype(low)
            for s in range(samples):
                grad[b, 0, s] = grad_keys[s * cells : (s + 1) * cells]
                grad[b, 1, s] = grad_values[s * cells : (s + 1) * cells]

        def merged(part, row, col):
            place = {cols: -1, cols + 1: cols}.get(col, col)
            slot = row * wide + col
            terms = [
                grad[b, part, places[b, slot]] for b in range(cols) if abs(b - place) <= 1
            ]
            return sum(terms[1:], terms[0])

        for c in range(cols):
            gik_ref[0, 0, c, :, lanes] = merged(0, 2, c).astype(low)
            giv_ref[0, 0, c, :, lanes] = merged(1, 2, c)
        for part in range(2):
            for c in range(cols):
                gown_ref[part, 0, c, :, lanes] = merged(part, 0, c)
            for c in range(wide):
                gintra_ref[part, 0, c, :, lanes] = merged(part, 1, c).astype(low)
        for side in range(2):
            gsk_ref[0, 0, side, :, lanes] = merged(0, 0, cols + side)
            gsv_ref[0, 0, side, :, lanes] = merged(1, 0, cols + side)
            gck_ref[0, 0, side, :, lanes] = merged(0, 2, cols + side).astype(low)
        gcw_ref[0, 0, 0, :, lanes] = merged(1, 2, cols).astype(low)
        gce_ref[0, 0, 0, :, lanes] = merged(1, 2, cols + 1).astype(low)

    for g in range(groups):
        step(g)


def attention(slots, places, operands):
    queries = operands[0]
    _, cols, cells, width = queries.shape
    wide = cols + 2
    samples = slots.shape[1]

    def out(lead, dtype):
        return jax.ShapeDtypeStruct(lead + (cells, width), dtype)

    low, full = jnp.bfloat16, jnp.float32
    outs = [
        out((1, cols), low),
        out((1, cols), low),
        out((2, 1, cols), full),
        out((1, 1, 2), full),
        out((1, 1, 2), full),
        out((2, 1, wide), low),
        out((1, 1, cols), low),
        out((1, 1, cols), full),
        out((1, 1, 2), low),
        out((1, 1, 1), low),
        out((1, 1, 1), low),
    ]
    keys = samples * cells
    flops = 2 * 6 * cols * width * GROUP * cells * keys
    moved = sum(x.size * x.dtype.itemsize for x in list(operands) + outs)
    scalar, vector, anywhere = (
        pl.BlockSpec(memory_space=space) for space in (pltpu.SMEM, pltpu.VMEM, pl.ANY)
    )
    return pl.pallas_call(
        attention_kernel,
        out_shape=outs,
        in_specs=[scalar] * 2 + [vector] * 2 + [anywhere] * (len(operands) - 2),
        out_specs=[vector] * len(outs),
        scratch_shapes=[
            pltpu.VMEM((2, 3 * wide, cells, width), low),
            pltpu.VMEM((cols, 2, samples + 1, cells, LANES), full),
            pltpu.SemaphoreType.DMA((2, len(operands) - 2)),
        ],
        cost_estimate=pl.CostEstimate(
            flops=flops, bytes_accessed=moved, transcendentals=cols * width * keys
        ),
        compiler_params=pltpu.CompilerParams(vmem_limit_bytes=20 * 1024 * 1024),
        name="attention",
    )(slots, places, *operands)


def block_slots(blocks, cols):
    sectors = cols * lax.axis_size("lon")
    lat, lon = lax.axis_index("lat"), lax.axis_index("lon")
    down = blocks // sectors - lat
    near = jnp.where(lat % 2 == 0, 1, -1)
    row = jnp.where(down == 0, 0, jnp.where(down == near, 1, 2))
    place = (blocks % sectors - lon * cols + 1) % sectors
    col = jnp.where(place == 0, cols, jnp.where(place <= cols, place - 1, cols + 1))
    slots = row * (cols + 2) + col
    samples = blocks.shape[-1]
    listed = slots[:, :, None] == jnp.arange(3 * (cols + 2), dtype=jnp.int32)
    order = jnp.arange(samples, dtype=jnp.int32)[None, :, None]
    places = samples + jnp.sum(jnp.where(listed, order - samples, 0), axis=1, dtype=jnp.int32)
    return slots, places


def edges(first, last, cols):
    still = ((0, 0, 0),)
    return lax.pad(first, jnp.zeros((), first.dtype), still * 2 + ((0, cols - 1, 0),) + still * 2) + lax.pad(
        last, jnp.zeros((), last.dtype), still * 2 + ((cols - 1, 0, 0),) + still * 2
    )


def body(queries, keys_values, cotangent, blocks):
    cols = queries.shape[1]
    slots, places = block_slots(blocks[0], cols)

    keys, values = keys_values[:1], keys_values[1:]
    west_keys = lon_shift(keys[:, :, cols - 1 :], 1)
    east_keys = lon_shift(keys[:, :, :1], -1)
    inter_values = inter_swap(values)
    west_values = lon_shift(values[:, :, cols - 1 :], 1)
    east_values = lon_shift(values[:, :, :1], -1)
    inter_keys = inter_swap(keys)
    intra = intra_swap(keys_values)
    side_keys = jnp.concatenate([west_keys, east_keys], axis=2)
    corner_keys = inter_swap(side_keys)
    corner_west = lon_shift(inter_values[:, :, cols - 1 :], 1)
    corner_east = lon_shift(inter_values[:, :, :1], -1)
    intra_side_keys = intra_swap(side_keys)
    intra_west = intra_swap(west_values)
    intra_east = intra_swap(east_values)

    operands = (
        queries,
        cotangent,
        keys_values,
        intra,
        inter_keys,
        inter_values,
        west_keys,
        east_keys,
        west_values,
        east_values,
        intra_side_keys,
        intra_west,
        intra_east,
        corner_keys,
        corner_west,
        corner_east,
    )
    outs = attention(slots, places, operands)
    attended, grad_queries, own, side_k, side_v, to_intra, near_k, near_v, far_k, far_w, far_e = outs

    low, full = jnp.bfloat16, jnp.float32
    from_k = inter_swap(far_k)
    from_w = lon_shift(far_w, -1)
    from_e = lon_shift(far_e, 1)
    from_intra = intra_swap(to_intra)
    from_inter_k = inter_swap(near_k)
    side_v = (side_v + from_intra[1:, :, cols:].astype(full)).astype(low)
    from_east_v = lon_shift(side_v[:, :, :1], -1)
    from_west_v = lon_shift(side_v[:, :, 1:], 1)
    side_k = (side_k + from_intra[:1, :, cols:].astype(full) + from_k.astype(full)).astype(low)
    from_east_k = lon_shift(side_k[:, :, :1], -1)
    from_west_k = lon_shift(side_k[:, :, 1:], 1)
    near_v = (near_v + edges(from_e.astype(full), from_w.astype(full), cols)).astype(low)
    from_inter_v = inter_swap(near_v)

    def total(part, inter, first, last):
        piece = own[part : part + 1] + from_intra[part : part + 1, :, :cols].astype(full)
        piece = piece + inter.astype(full) + edges(first.astype(full), last.astype(full), cols)
        return piece.astype(low)

    grads = jnp.concatenate(
        [
            total(0, from_inter_k, from_west_k, from_east_k),
            total(1, from_inter_v, from_west_v, from_east_v),
        ],
        axis=0,
    )
    return (attended, grad_queries, grads)


def solution(mesh):
    placed = (
        P("lat", "lon", None, None),
        P(None, "lat", "lon", None, None),
        P("lat", "lon", None, None),
        P("lat", "lon", None),
    )
    return jax.shard_map(
        body,
        mesh=mesh,
        in_specs=placed,
        out_specs=(placed[0], placed[0], placed[1]),
        check_vma=False,
    )
```

time: 90.3 us -> 70.6 us (0.78)
  waiting for transfers between devices: 46.1 us -> 19.4 us
  starting transfers between devices: 22.9 us -> 39.7 us
  other arithmetic: 7.51 us -> 1.56 us
  Pallas kernels: 10.1 us -> 6.85 us
    ppermute x8 -> x12, waiting for transfers between devices: 26.2 us -> 6.72 us  [lon_shift(): lax.ppermute(value, 'lon', [(i, (i + steps) % count) for i in range(count)])]
    ppermute x4 -> x6, waiting for transfers between devices: 19.8 us -> 11.4 us  [inter_swap(): lax.ppermute(value, 'lat', [(i, j) for i, j in pairs if 0 <= j < count])]
    ppermute x8 -> x12, starting transfers between devices: 8.21 us -> 16.5 us  [lon_shift(): lax.ppermute(value, 'lon', [(i, (i + steps) % count) for i in range(count)])]
    ppermute x4 -> x6, starting transfers between devices: 13.6 us -> 20.4 us  [inter_swap(): lax.ppermute(value, 'lat', [(i, j) for i, j in pairs if 0 <= j < count])]
    scatter-add x4 -> x0, other arithmetic: 3.59 us -> none  [the longest x2 3.35 us: body(): to_inter.at[1:, :, cols - 1:].add(from_xwv).at[1:, :, :1].add(from_xev)]
    pallas_call x1, Pallas kernels: 10.1 us -> 6.85 us  [attention(): pl.pallas_call(attention_kernel, out_shape=outs, in_specs=[scalar] * 2 +...]
    convert_element_type x3, other arithmetic: 2.54 us -> 0.6 us  [the longest x1 0.34 us: total(): return piece.astype(low)]
    ppermute x3 -> x5, starting transfers between devices: 1.07 us -> 2.73 us  [intra_swap(): lax.ppermute(value, 'lat', [(i, i ^ 1) for i in range(count) if i ^ 1 < c...]
  transfers between devices with their start and end apart: 15 -> 23, of which waited for: 10 -> 9; matrix products, arithmetic and copies ran while one was open for 7% -> 2% of each run, Pallas kernels for 0% -> 0%
where the time goes in v3:
time: 70.6 us; the launch traced here: 70.3 us
  starting transfers between devices  39.7 us (56%)
  waiting for transfers between devices  19.4 us (27%)
  Pallas kernels  6.85 us (10%)
  local copies, waits for them, and re-layouts  2.02 us (3%)
  other arithmetic  1.56 us (2%)
  between operations  0.9 us (1%)
    ppermute x6, starting transfers between devices, inter_swap(): lax.ppermute(value, 'lat', [(i, j) for i, j in pairs if 0 <= j < count])  20.4 us
    ppermute x12, starting transfers between devices, lon_shift(): lax.ppermute(value, 'lon', [(i, (i + steps) % count) for i in range(count)])  16.5 us
    ppermute x6, waiting for transfers between devices, inter_swap(): lax.ppermute(value, 'lat', [(i, j) for i, j in pairs if 0 <= j < count])  11.4 us
    pallas_call x1, Pallas kernels, attention(): pl.pallas_call(attention_kernel, out_shape=outs, in_specs=[scalar] * 2 +...  6.85 us
    ppermute x12, waiting for transfers between devices, lon_shift(): lax.ppermute(value, 'lon', [(i, (i + steps) % count) for i in range(count)])  6.72 us
    ppermute x5, starting transfers between devices, intra_swap(): lax.ppermute(value, 'lat', [(i, i ^ 1) for i in range(count) if i ^ 1 < c...  2.73 us
  transfers between devices with their start and end apart: 23, of which 9 were waited for; matrix products, arithmetic and copies ran while one was open for 2% of the time, Pallas kernels for 0%

profile of v3, /device:TPU:3, one launch (start us, length us, event | category | flops | bytes accessed | tf_op | source)
XLA Modules:
  0.0 70.3 jit_solution(16367053146415318976)
XLA Ops:
  1.4 1.1 %fusion.5 = (bf16[1,1,1,64,1024]{4,3,2,1,0:T(8,128)(2,1)S(1)}, bf16[1,1,1,64,1024]{4,3,2,1,0:T(8,128)(2,1)S(1)}, bf16[1,1,1,64,1024]{4,3,2,1,0:T(8,128)(2,1)S(1)}, bf16[1,1,1,64,1024]{4,3,2,1,0:T(8,128)(2,1)S(1)}) fusion(bf16[2,1,2,64,1024]{4,3,2,1,0:T(8,128)(2,1)} %own_ref.1), kind=kLoop, calls=%fused_computation.30 | loop fusion | bytes 1048576 | tf_op jit(solution)/shard_map/slice | solution.py:258
  2.5 3.4 %collective-permute-start.6 = (bf16[1,1,1,64,1024]{4,3,2,1,0:T(8,128)(2,1)S(1)}, bf16[1,1,1,64,1024]{4,3,2,1,0:T(8,128)(2,1)S(1)}, u32[]{:S(2)}, u32[]{:S(2)}) collective-permute-start(bf16[1,1,1,64,1024]{4,3,2,1,0:T(8,128)(2,1)S(1)} %get-tuple-element.29), channel_id=1, source_target_pairs={{0,3},{1,0},{2,1},{3,2},{4,7},{5,4},{6,5},{7,6},{8,11},{9,8},{10,9... | collective-permute-start | bytes 393224 | tf_op jit(solution)/shard_map/ppermute | solution.py:17
  6.1 1.3 %collective-permute-start.3 = (bf16[1,1,1,64,1024]{4,3,2,1,0:T(8,128)(2,1)S(1)}, bf16[1,1,1,64,1024]{4,3,2,1,0:T(8,128)(2,1)S(1)}, u32[]{:S(2)}, u32[]{:S(2)}) collective-permute-start(bf16[1,1,1,64,1024]{4,3,2,1,0:T(8,128)(2,1)S(1)} %get-tuple-element.32), channel_id=1, source_target_pairs={{0,1},{1,2},{2,3},{3,0},{4,5},{5,6},{6,7},{7,4},{8,9},{9,10},{10,1... | collective-permute-start | bytes 393224 | tf_op jit(solution)/shard_map/ppermute | solution.py:17
  7.4 3.9 %collective-permute-start.2 = (bf16[1,1,2,64,1024]{4,3,2,1,0:T(8,128)(2,1)S(1)}, bf16[1,1,2,64,1024]{4,3,2,1,0:T(8,128)(2,1)S(1)}, u32[]{:S(2)}, u32[]{:S(2)}) collective-permute-start(bf16[1,1,2,64,1024]{4,3,2,1,0:T(8,128)(2,1)S(1)} %get-tuple-element.33), channel_id=1, source_target_pairs={{4,8},{8,4},{12,16},{16,12},{20,24},{24,20},{5,9},{9,5},{13,17},{1... | collective-permute-start | bytes 786440 | tf_op jit(solution)/shard_map/ppermute | solution.py:28
  12.3 2.9 %collective-permute-done.3.wk_ref = bf16[1,1,1,64,1024]{4,3,2,1,0:T(8,128)(2,1)S(1)} collective-permute-done((bf16[1,1,1,64,1024]{4,3,2,1,0:T(8,128)(2,1)S(1)}, bf16[1,1,1,64,1024]{4,3,2,1,0:T(8,128)(2,1)S(1)}, u32[]{:S(2)}, u32[]{:S(2)}) %collective-permute-start.3) | collective-permute-done | bytes 131104 | tf_op jit(solution)/shard_map/ppermute | solution.py:17
  15.2 0.9 %collective-permute-start.9 = (bf16[1,1,1,64,1024]{4,3,2,1,0:T(8,128)(2,1)S(1)}, bf16[1,1,1,64,1024]{4,3,2,1,0:T(8,128)(2,1)S(1)}, u32[]{:S(2)}, u32[]{:S(2)}) collective-permute-start(bf16[1,1,1,64,1024]{4,3,2,1,0:T(8,128)(2,1)S(1)} %collective-permute-done.6.ev_ref), channel_id=1, source_target_pairs={{0,4},{4,0},{8,12},{12,8},{16,20},{20,16},{24,28},{28,24},{1,5},{5... | collective-permute-start | bytes 393224 | tf_op jit(solution)/shard_map/ppermute | solution.py:22
  16.1 3.0 %collective-permute-start.1 = (bf16[1,1,2,64,1024]{4,3,2,1,0:T(8,128)(2,1)S(1)}, bf16[1,1,2,64,1024]{4,3,2,1,0:T(8,128)(2,1)S(1)}, u32[]{:S(2)}, u32[]{:S(2)}) collective-permute-start(bf16[1,1,2,64,1024]{4,3,2,1,0:T(8,128)(2,1)S(1)} %get-tuple-element.34), channel_id=1, source_target_pairs={{4,8},{8,4},{12,16},{16,12},{20,24},{24,20},{5,9},{9,5},{13,17},{1... | collective-permute-start | bytes 786440 | tf_op jit(solution)/shard_map/ppermute | solution.py:28
  19.2 3.8 %collective-permute-start.10 = (bf16[1,1,2,64,1024]{4,3,2,1,0:T(8,128)(2,1)S(1)}, bf16[1,1,2,64,1024]{4,3,2,1,0:T(8,128)(2,1)S(1)}, u32[]{:S(2)}, u32[]{:S(2)}) collective-permute-start(bf16[1,1,2,64,1024]{4,3,2,1,0:T(8,128)(2,1)S(1)} %constant_dynamic-update-slice_fusion), channel_id=1, source_target_pairs={{4,8},{8,4},{12,16},{16,12},{20,24},{24,20},{5,9},{9,5},{13,17},{1... | collective-permute-start | bytes 786440 | tf_op jit(solution)/shard_map/ppermute | solution.py:28
  23.6 1.2 %collective-permute-done.8.sw_ref = bf16[1,1,1,64,1024]{4,3,2,1,0:T(8,128)(2,1)S(1)} collective-permute-done((bf16[1,1,1,64,1024]{4,3,2,1,0:T(8,128)(2,1)S(1)}, bf16[1,1,1,64,1024]{4,3,2,1,0:T(8,128)(2,1)S(1)}, u32[]{:S(2)}, u32[]{:S(2)}) %collective-permute-start.8) | collective-permute-done | bytes 131104 | tf_op jit(solution)/shard_map/ppermute | solution.py:22
  24.8 1.8 %collective-permute-start.12 = (bf16[1,1,1,64,1024]{4,3,2,1,0:T(8,128)(2,1)S(1)}, bf16[1,1,1,64,1024]{4,3,2,1,0:T(8,128)(2,1)S(1)}, u32[]{:S(2)}, u32[]{:S(2)}) collective-permute-start(bf16[1,1,1,64,1024]{4,3,2,1,0:T(8,128)(2,1)S(1)} %get-tuple-element.39), channel_id=1, source_target_pairs={{0,3},{1,0},{2,1},{3,2},{4,7},{5,4},{6,5},{7,6},{8,11},{9,8},{10,9... | collective-permute-start | bytes 393224 | tf_op jit(solution)/shard_map/ppermute | solution.py:17
  27.5 1.9 %collective-permute-start.11 = (bf16[1,1,1,64,1024]{4,3,2,1,0:T(8,128)(2,1)S(1)}, bf16[1,1,1,64,1024]{4,3,2,1,0:T(8,128)(2,1)S(1)}, u32[]{:S(2)}, u32[]{:S(2)}) collective-permute-start(bf16[1,1,1,64,1024]{4,3,2,1,0:T(8,128)(2,1)S(1)} %get-tuple-element.40), channel_id=1, source_target_pairs={{0,1},{1,2},{2,3},{3,0},{4,5},{5,6},{6,7},{7,4},{8,9},{9,10},{10,1... | collective-permute-start | bytes 393224 | tf_op jit(solution)/shard_map/ppermute | solution.py:17
  29.4 3.9 %collective-permute-done.10.ck_ref = bf16[1,1,2,64,1024]{4,3,2,1,0:T(8,128)(2,1)S(1)} collective-permute-done((bf16[1,1,2,64,1024]{4,3,2,1,0:T(8,128)(2,1)S(1)}, bf16[1,1,2,64,1024]{4,3,2,1,0:T(8,128)(2,1)S(1)}, u32[]{:S(2)}, u32[]{:S(2)}) %collective-permute-start.10) | collective-permute-done | bytes 262176 | tf_op jit(solution)/shard_map/ppermute | solution.py:28
  33.4 1.5 %collective-permute-done.11.cw_ref = bf16[1,1,1,64,1024]{4,3,2,1,0:T(8,128)(2,1)S(1)} collective-permute-done((bf16[1,1,1,64,1024]{4,3,2,1,0:T(8,128)(2,1)S(1)}, bf16[1,1,1,64,1024]{4,3,2,1,0:T(8,128)(2,1)S(1)}, u32[]{:S(2)}, u32[]{:S(2)}) %collective-permute-start.11) | collective-permute-done | bytes 131104 | tf_op jit(solution)/shard_map/ppermute | solution.py:17
  34.9 6.8 %attention.1 = (bf16[1,2,64,1024]{3,2,1,0:T(8,128)(2,1)}, bf16[1,2,64,1024]{3,2,1,0:T(8,128)(2,1)}, f32[2,1,2,64,1024]{4,3,2,1,0:T(8,128)S(1)}, f32[1,1,2,64,102...) custom-call(s32[2,6]{1,0:T(2,128)S(1)} %fusion.2.slots, ...), custom_call_target="tpu_custom_call" | custom-call | flops 2415919104 | bytes 8650752 | tf_op jit(solution)/shard_map/attention/pallas_call | solution.py:208
  42.3 3.2 %collective-permute-start.19 = (bf16[1,1,1,64,1024]{4,3,2,1,0:T(8,128)(2,1)S(1)}, bf16[1,1,1,64,1024]{4,3,2,1,0:T(8,128)(2,1)S(1)}, u32[]{:S(2)}, u32[]{:S(2)}) collective-permute-start(bf16[1,1,1,64,1024]{4,3,2,1,0:T(8,128)(2,1)S(1)} %get-tuple-element.23), channel_id=1, source_target_pairs={{0,3},{1,0},{2,1},{3,2},{4,7},{5,4},{6,5},{7,6},{8,11},{9,8},{10,9... | collective-permute-start | bytes 393224 | tf_op jit(solution)/shard_map/ppermute | solution.py:17
  45.5 3.3 %collective-permute-start.15 = (bf16[1,1,2,64,1024]{4,3,2,1,0:T(8,128)(2,1)S(1)}, bf16[1,1,2,64,1024]{4,3,2,1,0:T(8,128)(2,1)S(1)}, u32[]{:S(2)}, u32[]{:S(2)}) collective-permute-start(bf16[1,1,2,64,1024]{4,3,2,1,0:T(8,128)(2,1)S(1)} %get-tuple-element.20), channel_id=1, source_target_pairs={{4,8},{8,4},{12,16},{16,12},{20,24},{24,20},{5,9},{9,5},{13,17},{1... | collective-permute-start | bytes 786440 | tf_op jit(solution)/shard_map/ppermute | solution.py:28
  48.8 3.2 %collective-permute-start.14 = (bf16[1,1,2,64,1024]{4,3,2,1,0:T(8,128)(2,1)S(1)}, bf16[1,1,2,64,1024]{4,3,2,1,0:T(8,128)(2,1)S(1)}, u32[]{:S(2)}, u32[]{:S(2)}) collective-permute-start(bf16[1,1,2,64,1024]{4,3,2,1,0:T(8,128)(2,1)S(1)} %get-tuple-element.18), channel_id=1, source_target_pairs={{4,8},{8,4},{12,16},{16,12},{20,24},{24,20},{5,9},{9,5},{13,17},{1... | collective-permute-start | bytes 786440 | tf_op jit(solution)/shard_map/ppermute | solution.py:28
  52.0 3.3 %collective-permute-start.20 = (bf16[1,1,2,64,1024]{4,3,2,1,0:T(8,128)(2,1)S(1)}, bf16[1,1,2,64,1024]{4,3,2,1,0:T(8,128)(2,1)S(1)}, u32[]{:S(2)}, u32[]{:S(2)}) collective-permute-start(bf16[1,1,2,64,1024]{4,3,2,1,0:T(8,128)(2,1)S(1)} %add_convert_fusion.2), channel_id=1, source_target_pairs={{4,8},{8,4},{12,16},{16,12},{20,24},{24,20},{5,9},{9,5},{13,17},{1... | collective-permute-start | bytes 786440 | tf_op jit(solution)/shard_map/ppermute | solution.py:28
  55.3 1.6 %collective-permute-done.15 = bf16[1,1,2,64,1024]{4,3,2,1,0:T(8,128)(2,1)S(1)} collective-permute-done((bf16[1,1,2,64,1024]{4,3,2,1,0:T(8,128)(2,1)S(1)}, bf16[1,1,2,64,1024]{4,3,2,1,0:T(8,128)(2,1)S(1)}, u32[]{:S(2)}, u32[]{:S(2)}) %collective-permute-start.15) | collective-permute-done | bytes 262176 | tf_op jit(solution)/shard_map/ppermute | solution.py:28
  57.2 3.3 %collective-permute-start.17 = (bf16[1,1,1,64,1024]{4,3,2,1,0:T(8,128)(2,1)S(1)}, bf16[1,1,1,64,1024]{4,3,2,1,0:T(8,128)(2,1)S(1)}, u32[]{:S(2)}, u32[]{:S(2)}) collective-permute-start(bf16[1,1,1,64,1024]{4,3,2,1,0:T(8,128)(2,1)S(1)} %get-tuple-element.36), channel_id=1, source_target_pairs={{0,3},{1,0},{2,1},{3,2},{4,7},{5,4},{6,5},{7,6},{8,11},{9,8},{10,9... | collective-permute-start | bytes 393224 | tf_op jit(solution)/shard_map/ppermute | solution.py:17
  60.5 2.0 %collective-permute-done.14 = bf16[1,1,2,64,1024]{4,3,2,1,0:T(8,128)(2,1)S(1)} collective-permute-done((bf16[1,1,2,64,1024]{4,3,2,1,0:T(8,128)(2,1)S(1)}, bf16[1,1,2,64,1024]{4,3,2,1,0:T(8,128)(2,1)S(1)}, u32[]{:S(2)}, u32[]{:S(2)}) %collective-permute-start.14) | collective-permute-done | bytes 262176 | tf_op jit(solution)/shard_map/ppermute | solution.py:28
  62.5 1.3 %collective-permute-start.22 = (bf16[1,1,1,64,1024]{4,3,2,1,0:T(8,128)(2,1)S(1)}, bf16[1,1,1,64,1024]{4,3,2,1,0:T(8,128)(2,1)S(1)}, u32[]{:S(2)}, u32[]{:S(2)}) collective-permute-start(bf16[1,1,1,64,1024]{4,3,2,1,0:T(8,128)(2,1)S(1)} %get-tuple-element.38), channel_id=1, source_target_pairs={{0,3},{1,0},{2,1},{3,2},{4,7},{5,4},{6,5},{7,6},{8,11},{9,8},{10,9... | collective-permute-start | bytes 393224 | tf_op jit(solution)/shard_map/ppermute | solution.py:17
  63.8 3.1 %collective-permute-done.20 = bf16[1,1,2,64,1024]{4,3,2,1,0:T(8,128)(2,1)S(1)} collective-permute-done((bf16[1,1,2,64,1024]{4,3,2,1,0:T(8,128)(2,1)S(1)}, bf16[1,1,2,64,1024]{4,3,2,1,0:T(8,128)(2,1)S(1)}, u32[]{:S(2)}, u32[]{:S(2)}) %collective-permute-start.20) | collective-permute-done | bytes 262176 | tf_op jit(solution)/shard_map/ppermute | solution.py:28
  66.9 2.3 %collective-permute-done.21 = bf16[1,1,1,64,1024]{4,3,2,1,0:T(8,128)(2,1)S(1)} collective-permute-done((bf16[1,1,1,64,1024]{4,3,2,1,0:T(8,128)(2,1)S(1)}, bf16[1,1,1,64,1024]{4,3,2,1,0:T(8,128)(2,1)S(1)}, u32[]{:S(2)}, u32[]{:S(2)}) %collective-permute-start.21) | collective-permute-done | bytes 131104 | tf_op jit(solution)/shard_map/ppermute | solution.py:17
  (47 shorter events, 5.6 us)
Async XLA Ops:
  0.6 34.2 %collective-permute-start = (bf16[2,1,2,64,1024]{4,3,2,1,0:T(8,128)(2,1)}, bf16[2,1,2,64,1024]{4,3,2,1,0:T(8,128)(2,1)S(1)}, u32[]{:S(2)}, u32[]{:S(2)}) collective-permute-start(bf16[2,1,2,64,1024]{4,3,2,1,0:T(8,128)(2,1)} %own_ref.1), channel_id=1, source_target_pairs={{0,4},{4,0},{8,12},{12,8},{16,20},{20,16},{24,28},{28,24},{1,5},{5... | collective-permute-start | bytes 1572872 | tf_op jit(solution)/shard_map/ppermute | solution.py:22
  2.5 9.7 %collective-permute-start.6 = (bf16[1,1,1,64,1024]{4,3,2,1,0:T(8,128)(2,1)S(1)}, bf16[1,1,1,64,1024]{4,3,2,1,0:T(8,128)(2,1)S(1)}, u32[]{:S(2)}, u32[]{:S(2)}) collective-permute-start(bf16[1,1,1,64,1024]{4,3,2,1,0:T(8,128)(2,1)S(1)} %get-tuple-element.29), channel_id=1, source_target_pairs={{0,3},{1,0},{2,1},{3,2},{4,7},{5,4},{6,5},{7,6},{8,11},{9,8},{10,9... | collective-permute-start | bytes 393224 | tf_op jit(solution)/shard_map/ppermute | solution.py:17
  5.9 10.2 %collective-permute-start.4 = (bf16[1,1,1,64,1024]{4,3,2,1,0:T(8,128)(2,1)S(1)}, bf16[1,1,1,64,1024]{4,3,2,1,0:T(8,128)(2,1)S(1)}, u32[]{:S(2)}, u32[]{:S(2)}) collective-permute-start(bf16[1,1,1,64,1024]{4,3,2,1,0:T(8,128)(2,1)S(1)} %get-tuple-element.31), channel_id=1, source_target_pairs={{0,3},{1,0},{2,1},{3,2},{4,7},{5,4},{6,5},{7,6},{8,11},{9,8},{10,9... | collective-permute-start | bytes 393224 | tf_op jit(solution)/shard_map/ppermute | solution.py:17
  6.1 9.1 %collective-permute-start.3 = (bf16[1,1,1,64,1024]{4,3,2,1,0:T(8,128)(2,1)S(1)}, bf16[1,1,1,64,1024]{4,3,2,1,0:T(8,128)(2,1)S(1)}, u32[]{:S(2)}, u32[]{:S(2)}) collective-permute-start(bf16[1,1,1,64,1024]{4,3,2,1,0:T(8,128)(2,1)S(1)} %get-tuple-element.32), channel_id=1, source_target_pairs={{0,1},{1,2},{2,3},{3,0},{4,5},{5,6},{6,7},{7,4},{8,9},{9,10},{10,1... | collective-permute-start | bytes 393224 | tf_op jit(solution)/shard_map/ppermute | solution.py:17
  7.4 15.7 %collective-permute-start.2 = (bf16[1,1,2,64,1024]{4,3,2,1,0:T(8,128)(2,1)S(1)}, bf16[1,1,2,64,1024]{4,3,2,1,0:T(8,128)(2,1)S(1)}, u32[]{:S(2)}, u32[]{:S(2)}) collective-permute-start(bf16[1,1,2,64,1024]{4,3,2,1,0:T(8,128)(2,1)S(1)} %get-tuple-element.33), channel_id=1, source_target_pairs={{4,8},{8,4},{12,16},{16,12},{20,24},{24,20},{5,9},{9,5},{13,17},{1... | collective-permute-start | bytes 786440 | tf_op jit(solution)/shard_map/ppermute | solution.py:28
  12.2 7.0 %collective-permute-start.5 = (bf16[1,1,1,64,1024]{4,3,2,1,0:T(8,128)(2,1)S(1)}, bf16[1,1,1,64,1024]{4,3,2,1,0:T(8,128)(2,1)S(1)}, u32[]{:S(2)}, u32[]{:S(2)}) collective-permute-start(bf16[1,1,1,64,1024]{4,3,2,1,0:T(8,128)(2,1)S(1)} %get-tuple-element.30), channel_id=1, source_target_pairs={{0,1},{1,2},{2,3},{3,0},{4,5},{5,6},{6,7},{7,4},{8,9},{9,10},{10,1... | collective-permute-start | bytes 393224 | tf_op jit(solution)/shard_map/ppermute | solution.py:17
  15.2 7.8 %collective-permute-start.9 = (bf16[1,1,1,64,1024]{4,3,2,1,0:T(8,128)(2,1)S(1)}, bf16[1,1,1,64,1024]{4,3,2,1,0:T(8,128)(2,1)S(1)}, u32[]{:S(2)}, u32[]{:S(2)}) collective-permute-start(bf16[1,1,1,64,1024]{4,3,2,1,0:T(8,128)(2,1)S(1)} %collective-permute-done.6.ev_ref), channel_id=1, source_target_pairs={{0,4},{4,0},{8,12},{12,8},{16,20},{20,16},{24,28},{28,24},{1,5},{5... | collective-permute-start | bytes 393224 | tf_op jit(solution)/shard_map/ppermute | solution.py:22
  16.1 11.4 %collective-permute-start.1 = (bf16[1,1,2,64,1024]{4,3,2,1,0:T(8,128)(2,1)S(1)}, bf16[1,1,2,64,1024]{4,3,2,1,0:T(8,128)(2,1)S(1)}, u32[]{:S(2)}, u32[]{:S(2)}) collective-permute-start(bf16[1,1,2,64,1024]{4,3,2,1,0:T(8,128)(2,1)S(1)} %get-tuple-element.34), channel_id=1, source_target_pairs={{4,8},{8,4},{12,16},{16,12},{20,24},{24,20},{5,9},{9,5},{13,17},{1... | collective-permute-start | bytes 786440 | tf_op jit(solution)/shard_map/ppermute | solution.py:28
  19.2 15.7 %copy-start.1 = (bf16[1,2,64,1024]{3,2,1,0:T(8,128)(2,1)S(1)}, bf16[1,2,64,1024]{3,2,1,0:T(8,128)(2,1)}, u32[]{:S(2)}) copy-start(bf16[1,2,64,1024]{3,2,1,0:T(8,128)(2,1)} %q_ref.1) | copy-start | bytes 786436
  19.2 14.1 %collective-permute-start.10 = (bf16[1,1,2,64,1024]{4,3,2,1,0:T(8,128)(2,1)S(1)}, bf16[1,1,2,64,1024]{4,3,2,1,0:T(8,128)(2,1)S(1)}, u32[]{:S(2)}, u32[]{:S(2)}) collective-permute-start(bf16[1,1,2,64,1024]{4,3,2,1,0:T(8,128)(2,1)S(1)} %constant_dynamic-update-slice_fusion), channel_id=1, source_target_pairs={{4,8},{8,4},{12,16},{16,12},{20,24},{24,20},{5,9},{9,5},{13,17},{1... | collective-permute-start | bytes 786440 | tf_op jit(solution)/shard_map/ppermute | solution.py:28
  23.0 10.3 %collective-permute-start.7 = (bf16[1,1,2,64,1024]{4,3,2,1,0:T(8,128)(2,1)S(1)}, bf16[1,1,2,64,1024]{4,3,2,1,0:T(8,128)(2,1)S(1)}, u32[]{:S(2)}, u32[]{:S(2)}) collective-permute-start(bf16[1,1,2,64,1024]{4,3,2,1,0:T(8,128)(2,1)S(1)} %constant_dynamic-update-slice_fusion), channel_id=1, source_target_pairs={{0,4},{4,0},{8,12},{12,8},{16,20},{20,16},{24,28},{28,24},{1,5},{5... | collective-permute-start | bytes 786440 | tf_op jit(solution)/shard_map/ppermute | solution.py:22
  23.1 1.7 %collective-permute-start.8 = (bf16[1,1,1,64,1024]{4,3,2,1,0:T(8,128)(2,1)S(1)}, bf16[1,1,1,64,1024]{4,3,2,1,0:T(8,128)(2,1)S(1)}, u32[]{:S(2)}, u32[]{:S(2)}) collective-permute-start(bf16[1,1,1,64,1024]{4,3,2,1,0:T(8,128)(2,1)S(1)} %collective-permute-done.5.wv_ref), channel_id=1, source_target_pairs={{0,4},{4,0},{8,12},{12,8},{16,20},{20,16},{24,28},{28,24},{1,5},{5... | collective-permute-start | bytes 393224 | tf_op jit(solution)/shard_map/ppermute | solution.py:22
  24.8 8.6 %collective-permute-start.12 = (bf16[1,1,1,64,1024]{4,3,2,1,0:T(8,128)(2,1)S(1)}, bf16[1,1,1,64,1024]{4,3,2,1,0:T(8,128)(2,1)S(1)}, u32[]{:S(2)}, u32[]{:S(2)}) collective-permute-start(bf16[1,1,1,64,1024]{4,3,2,1,0:T(8,128)(2,1)S(1)} %get-tuple-element.39), channel_id=1, source_target_pairs={{0,3},{1,0},{2,1},{3,2},{4,7},{5,4},{6,5},{7,6},{8,11},{9,8},{10,9... | collective-permute-start | bytes 393224 | tf_op jit(solution)/shard_map/ppermute | solution.py:17
  27.5 7.3 %collective-permute-start.11 = (bf16[1,1,1,64,1024]{4,3,2,1,0:T(8,128)(2,1)S(1)}, bf16[1,1,1,64,1024]{4,3,2,1,0:T(8,128)(2,1)S(1)}, u32[]{:S(2)}, u32[]{:S(2)}) collective-permute-start(bf16[1,1,1,64,1024]{4,3,2,1,0:T(8,128)(2,1)S(1)} %get-tuple-element.40), channel_id=1, source_target_pairs={{0,1},{1,2},{2,3},{3,0},{4,5},{5,6},{6,7},{7,4},{8,9},{9,10},{10,1... | collective-permute-start | bytes 393224 | tf_op jit(solution)/shard_map/ppermute | solution.py:17
  41.7 15.2 %collective-permute-start.13 = (bf16[2,1,4,64,1024]{4,3,2,1,0:T(8,128)(2,1)S(1)}, bf16[2,1,4,64,1024]{4,3,2,1,0:T(8,128)(2,1)S(1)}, u32[]{:S(2)}, u32[]{:S(2)}) collective-permute-start(bf16[2,1,4,64,1024]{4,3,2,1,0:T(8,128)(2,1)S(1)} %get-tuple-element.17), channel_id=1, source_target_pairs={{0,4},{4,0},{8,12},{12,8},{16,20},{20,16},{24,28},{28,24},{1,5},{5... | collective-permute-start | bytes 3145736 | tf_op jit(solution)/shard_map/ppermute | solution.py:22
  42.2 9.7 %collective-permute-start.18 = (bf16[1,1,1,64,1024]{4,3,2,1,0:T(8,128)(2,1)S(1)}, bf16[1,1,1,64,1024]{4,3,2,1,0:T(8,128)(2,1)S(1)}, u32[]{:S(2)}, u32[]{:S(2)}) collective-permute-start(bf16[1,1,1,64,1024]{4,3,2,1,0:T(8,128)(2,1)S(1)} %get-tuple-element.22), channel_id=1, source_target_pairs={{0,1},{1,2},{2,3},{3,0},{4,5},{5,6},{6,7},{7,4},{8,9},{9,10},{10,1... | collective-permute-start | bytes 393224 | tf_op jit(solution)/shard_map/ppermute | solution.py:17
  42.3 9.7 %collective-permute-start.19 = (bf16[1,1,1,64,1024]{4,3,2,1,0:T(8,128)(2,1)S(1)}, bf16[1,1,1,64,1024]{4,3,2,1,0:T(8,128)(2,1)S(1)}, u32[]{:S(2)}, u32[]{:S(2)}) collective-permute-start(bf16[1,1,1,64,1024]{4,3,2,1,0:T(8,128)(2,1)S(1)} %get-tuple-element.23), channel_id=1, source_target_pairs={{0,3},{1,0},{2,1},{3,2},{4,7},{5,4},{6,5},{7,6},{8,11},{9,8},{10,9... | collective-permute-start | bytes 393224 | tf_op jit(solution)/shard_map/ppermute | solution.py:17
  45.5 11.4 %collective-permute-start.15 = (bf16[1,1,2,64,1024]{4,3,2,1,0:T(8,128)(2,1)S(1)}, bf16[1,1,2,64,1024]{4,3,2,1,0:T(8,128)(2,1)S(1)}, u32[]{:S(2)}, u32[]{:S(2)}) collective-permute-start(bf16[1,1,2,64,1024]{4,3,2,1,0:T(8,128)(2,1)S(1)} %get-tuple-element.20), channel_id=1, source_target_pairs={{4,8},{8,4},{12,16},{16,12},{20,24},{24,20},{5,9},{9,5},{13,17},{1... | collective-permute-start | bytes 786440 | tf_op jit(solution)/shard_map/ppermute | solution.py:28
  48.8 13.7 %collective-permute-start.14 = (bf16[1,1,2,64,1024]{4,3,2,1,0:T(8,128)(2,1)S(1)}, bf16[1,1,2,64,1024]{4,3,2,1,0:T(8,128)(2,1)S(1)}, u32[]{:S(2)}, u32[]{:S(2)}) collective-permute-start(bf16[1,1,2,64,1024]{4,3,2,1,0:T(8,128)(2,1)S(1)} %get-tuple-element.18), channel_id=1, source_target_pairs={{4,8},{8,4},{12,16},{16,12},{20,24},{24,20},{5,9},{9,5},{13,17},{1... | collective-permute-start | bytes 786440 | tf_op jit(solution)/shard_map/ppermute | solution.py:28
  52.0 14.8 %collective-permute-start.20 = (bf16[1,1,2,64,1024]{4,3,2,1,0:T(8,128)(2,1)S(1)}, bf16[1,1,2,64,1024]{4,3,2,1,0:T(8,128)(2,1)S(1)}, u32[]{:S(2)}, u32[]{:S(2)}) collective-permute-start(bf16[1,1,2,64,1024]{4,3,2,1,0:T(8,128)(2,1)S(1)} %add_convert_fusion.2), channel_id=1, source_target_pairs={{4,8},{8,4},{12,16},{16,12},{20,24},{24,20},{5,9},{9,5},{13,17},{1... | collective-permute-start | bytes 786440 | tf_op jit(solution)/shard_map/ppermute | solution.py:28
  57.1 9.7 %collective-permute-start.16 = (bf16[1,1,1,64,1024]{4,3,2,1,0:T(8,128)(2,1)S(1)}, bf16[1,1,1,64,1024]{4,3,2,1,0:T(8,128)(2,1)S(1)}, u32[]{:S(2)}, u32[]{:S(2)}) collective-permute-start(bf16[1,1,1,64,1024]{4,3,2,1,0:T(8,128)(2,1)S(1)} %get-tuple-element.35), channel_id=1, source_target_pairs={{0,1},{1,2},{2,3},{3,0},{4,5},{5,6},{6,7},{7,4},{8,9},{9,10},{10,1... | collective-permute-start | bytes 393224 | tf_op jit(solution)/shard_map/ppermute | solution.py:17
  57.2 9.7 %collective-permute-start.17 = (bf16[1,1,1,64,1024]{4,3,2,1,0:T(8,128)(2,1)S(1)}, bf16[1,1,1,64,1024]{4,3,2,1,0:T(8,128)(2,1)S(1)}, u32[]{:S(2)}, u32[]{:S(2)}) collective-permute-start(bf16[1,1,1,64,1024]{4,3,2,1,0:T(8,128)(2,1)S(1)} %get-tuple-element.36), channel_id=1, source_target_pairs={{0,3},{1,0},{2,1},{3,2},{4,7},{5,4},{6,5},{7,6},{8,11},{9,8},{10,9... | collective-permute-start | bytes 393224 | tf_op jit(solution)/shard_map/ppermute | solution.py:17
  60.5 8.7 %collective-permute-start.21 = (bf16[1,1,1,64,1024]{4,3,2,1,0:T(8,128)(2,1)S(1)}, bf16[1,1,1,64,1024]{4,3,2,1,0:T(8,128)(2,1)S(1)}, u32[]{:S(2)}, u32[]{:S(2)}) collective-permute-start(bf16[1,1,1,64,1024]{4,3,2,1,0:T(8,128)(2,1)S(1)} %get-tuple-element.37), channel_id=1, source_target_pairs={{0,1},{1,2},{2,3},{3,0},{4,5},{5,6},{6,7},{7,4},{8,9},{9,10},{10,1... | collective-permute-start | bytes 393224 | tf_op jit(solution)/shard_map/ppermute | solution.py:17
  62.5 6.7 %collective-permute-start.22 = (bf16[1,1,1,64,1024]{4,3,2,1,0:T(8,128)(2,1)S(1)}, bf16[1,1,1,64,1024]{4,3,2,1,0:T(8,128)(2,1)S(1)}, u32[]{:S(2)}, u32[]{:S(2)}) collective-permute-start(bf16[1,1,1,64,1024]{4,3,2,1,0:T(8,128)(2,1)S(1)} %get-tuple-element.38), channel_id=1, source_target_pairs={{0,3},{1,0},{2,1},{3,2},{4,7},{5,4},{6,5},{7,6},{8,11},{9,8},{10,9... | collective-permute-start | bytes 393224 | tf_op jit(solution)/shard_map/ppermute | solution.py:17
  (3 other events, 23.1 us)

commit v4 on v3

--- a/solution.py
+++ b/solution.py
@@ -39,8 +39,7 @@
     c_ref,
     own_ref,
     intra_ref,
-    ik_ref,
-    iv_ref,
+    inter_ref,
     wk_ref,
     ek_ref,
     wv_ref,
@@ -51,8 +50,8 @@
     ck_ref,
     cw_ref,
     ce_ref,
-    att_ref,
-    gq_ref,
+    kv,
+    shares,
     gown_ref,
     gsk_ref,
     gsv_ref,
@@ -62,7 +61,6 @@
     gck_ref,
     gcw_ref,
     gce_ref,
-    kv,
     grad,
     sems,
 ):
@@ -77,8 +75,7 @@
     moves = (
         (own_ref, slice(None), 0, near),
         (intra_ref, slice(None), 0, pl.ds(wide, cols)),
-        (ik_ref, pl.ds(0, 1), 0, far),
-        (iv_ref, pl.ds(1, 1), 0, far),
+        (inter_ref, slice(None), 0, far),
         (wk_ref, pl.ds(0, 1), 0, pl.ds(cols, 1)),
         (ek_ref, pl.ds(0, 1), 0, pl.ds(cols + 1, 1)),
         (wv_ref, pl.ds(1, 1), 0, pl.ds(cols, 1)),
@@ -114,12 +111,6 @@
     def spread(rows):
         zero = jnp.zeros_like(rows)
         return jnp.concatenate([jnp.where(m, rows, zero) for m in masks], axis=0)
-
-    def gathered(rows):
-        out = rows[:cells]
-        for h in range(1, GROUP):
-            out = jnp.where(masks[h], rows[h * cells : (h + 1) * cells], out)
-        return out
 
     def step(g):
         lanes = pl.ds(g * LANES, LANES)
@@ -143,8 +134,8 @@
             score_grad = (weights * (pressure[b] - inner) * scale).astype(low)
             grad_values = dot(weights_low, upstream[b], ((1,), (0,)))
             grad_keys = dot(score_grad, query[b], ((1,), (0,)))
-            att_ref[0, b, :, lanes] = gathered(dot(weights_low, values[b], ((0,), (0,)))).astype(low)
-            gq_ref[0, b, :, lanes] = gathered(dot(score_grad, keys[b], ((0,), (0,)))).astype(low)
+            shares[0, b, g] = score_grad
+            shares[1, b, g] = weights_low
             for s in range(samples):
                 grad[b, 0, s] = grad_keys[s * cells : (s + 1) * cells]
                 grad[b, 1, s] = grad_values[s * cells : (s + 1) * cells]
@@ -186,9 +177,10 @@
         return jax.ShapeDtypeStruct(lead + (cells, width), dtype)
 
     low, full = jnp.bfloat16, jnp.float32
+    keys = samples * cells
     outs = [
-        out((1, cols), low),
-        out((1, cols), low),
+        out((2, 3 * wide), low),
+        jax.ShapeDtypeStruct((2, cols, width // LANES, keys, LANES), low),
         out((2, 1, cols), full),
         out((1, 1, 2), full),
         out((1, 1, 2), full),
@@ -199,8 +191,7 @@
         out((1, 1, 1), low),
         out((1, 1, 1), low),
     ]
-    keys = samples * cells
-    flops = 2 * 6 * cols * width * GROUP * cells * keys
+    flops = 2 * 4 * cols * width * GROUP * cells * keys
     moved = sum(x.size * x.dtype.itemsize for x in list(operands) + outs)
     scalar, vector, anywhere = (
         pl.BlockSpec(memory_space=space) for space in (pltpu.SMEM, pltpu.VMEM, pl.ANY)
@@ -211,7 +202,6 @@
         in_specs=[scalar] * 2 + [vector] * 2 + [anywhere] * (len(operands) - 2),
         out_specs=[vector] * len(outs),
         scratch_shapes=[
-            pltpu.VMEM((2, 3 * wide, cells, width), low),
             pltpu.VMEM((cols, 2, samples + 1, cells, LANES), full),
             pltpu.SemaphoreType.DMA((2, len(operands) - 2)),
         ],
@@ -221,6 +211,64 @@
         compiler_params=pltpu.CompilerParams(vmem_limit_bytes=20 * 1024 * 1024),
         name="attention",
     )(slots, places, *operands)
+
+
+def stage_kernel(*refs):
+    sems = refs[-1]
+    count = len(refs) // 2
+    copies = [
+        pltpu.make_async_copy(refs[i], refs[count + i], sems.at[i]) for i in range(count)
+    ]
+    for copy in copies:
+        copy.start()
+    for copy in copies:
+        copy.wait()
+
+
+def stage(*arrays):
+    return pl.pallas_call(
+        stage_kernel,
+        out_shape=[jax.ShapeDtypeStruct(x.shape, x.dtype) for x in arrays],
+        in_specs=[pl.BlockSpec(memory_space=pl.ANY) for _ in arrays],
+        out_specs=[pl.BlockSpec(memory_space=pltpu.VMEM) for _ in arrays],
+        scratch_shapes=[pltpu.SemaphoreType.DMA((len(arrays),))],
+        compiler_params=pltpu.CompilerParams(vmem_limit_bytes=8 * 1024 * 1024),
+        name="stage",
+    )(*arrays)
+
+
+def finish_kernel(slots, kv, shares, gq_ref, att_ref):
+    _, cols, cells, width = att_ref.shape
+    samples = slots.shape[1]
+    head = lax.broadcasted_iota(jnp.int32, (cells, LANES), 1) // HEAD_DIM
+    for g in range(width // LANES):
+        lanes = pl.ds(g * LANES, LANES)
+        for b in range(cols):
+            for part, ref in enumerate((gq_ref, att_ref)):
+                rows = jnp.concatenate(
+                    [kv[part, slots[b, s], :, lanes] for s in range(samples)], axis=0
+                )
+                sums = dot(shares[part, b, g], rows, ((0,), (0,)))
+                out = sums[:cells]
+                for h in range(1, GROUP):
+                    out = jnp.where(head == h, sums[h * cells : (h + 1) * cells], out)
+                ref[0, b, :, lanes] = out.astype(ref.dtype)
+
+
+def finish(slots, kv, shares, like):
+    scalar, vector = (pl.BlockSpec(memory_space=space) for space in (pltpu.SMEM, pltpu.VMEM))
+    shape = jax.ShapeDtypeStruct(like.shape, like.dtype)
+    return pl.pallas_call(
+        finish_kernel,
+        out_shape=[shape, shape],
+        in_specs=[scalar, vector, vector],
+        out_specs=[vector, vector],
+        cost_estimate=pl.CostEstimate(
+            flops=4 * shares.size * LANES, bytes_accessed=2 * shares.size, transcendentals=0
+        ),
+        compiler_params=pltpu.CompilerParams(vmem_limit_bytes=16 * 1024 * 1024),
+        name="finish",
+    )(slots, kv, shares)
 
 
 def block_slots(blocks, cols):
@@ -235,7 +283,7 @@
     samples = blocks.shape[-1]
     listed = slots[:, :, None] == jnp.arange(3 * (cols + 2), dtype=jnp.int32)
     order = jnp.arange(samples, dtype=jnp.int32)[None, :, None]
-    places = samples + jnp.sum(jnp.where(listed, order - samples, 0), axis=1, dtype=jnp.int32)
+    places = jnp.min(jnp.where(listed, order, samples), axis=1)
     return slots, places
 
 
@@ -253,26 +301,25 @@
     keys, values = keys_values[:1], keys_values[1:]
     west_keys = lon_shift(keys[:, :, cols - 1 :], 1)
     east_keys = lon_shift(keys[:, :, :1], -1)
-    inter_values = inter_swap(values)
     west_values = lon_shift(values[:, :, cols - 1 :], 1)
     east_values = lon_shift(values[:, :, :1], -1)
-    inter_keys = inter_swap(keys)
+    inter = inter_swap(keys_values)
     intra = intra_swap(keys_values)
     side_keys = jnp.concatenate([west_keys, east_keys], axis=2)
     corner_keys = inter_swap(side_keys)
-    corner_west = lon_shift(inter_values[:, :, cols - 1 :], 1)
-    corner_east = lon_shift(inter_values[:, :, :1], -1)
+    corner_west = lon_shift(inter[1:, :, cols - 1 :], 1)
+    corner_east = lon_shift(inter[1:, :, :1], -1)
     intra_side_keys = intra_swap(side_keys)
     intra_west = intra_swap(west_values)
     intra_east = intra_swap(east_values)
 
+    queries_near, cotangent_near, own_near = stage(queries, cotangent, keys_values)
     operands = (
-        queries,
-        cotangent,
-        keys_values,
+        queries_near,
+        cotangent_near,
+        own_near,
         intra,
-        inter_keys,
-        inter_values,
+        inter,
         west_keys,
         east_keys,
         west_values,
@@ -285,7 +332,7 @@
         corner_east,
     )
     outs = attention(slots, places, operands)
-    attended, grad_queries, own, side_k, side_v, to_intra, near_k, near_v, far_k, far_w, far_e = outs
+    kv, shares, own, side_k, side_v, to_intra, near_k, near_v, far_k, far_w, far_e = outs
 
     low, full = jnp.bfloat16, jnp.float32
     from_k = inter_swap(far_k)
@@ -302,6 +349,8 @@
     near_v = (near_v + edges(from_e.astype(full), from_w.astype(full), cols)).astype(low)
     from_inter_v = inter_swap(near_v)
 
+    grad_queries, attended = finish(slots, kv, shares, queries)
+
     def total(part, inter, first, last):
         piece = own[part : part + 1] + from_intra[part : part + 1, :, :cols].astype(full)
         piece = piece + inter.astype(full) + edges(first.astype(full), last.astype(full), cols)

time: 70.6 us -> 68 us (0.963)
  starting transfers between devices: 39.7 us -> 34.4 us
  local copies, waits for them, and re-layouts: 2.02 us -> 4.24 us
  waiting for transfers between devices: 19.4 us -> 17.9 us
  Pallas kernels: 6.85 us -> 8.13 us
    ppermute x6 -> x5, waiting for transfers between devices: 11.4 us -> 3.35 us  [inter_swap(): lax.ppermute(value, 'lat', [(i, j) for i, j in pairs if 0 <= j < count])]
    ppermute x12, waiting for transfers between devices: 6.72 us -> 13.7 us  [lon_shift(): lax.ppermute(value, 'lon', [(i, (i + steps) % count) for i in range(count)])]
    ppermute x6 -> x5, starting transfers between devices: 20.4 us -> 17.5 us  [inter_swap(): lax.ppermute(value, 'lat', [(i, j) for i, j in pairs if 0 <= j < count])]
    pallas_call x0 -> x2, Pallas kernels: none -> 2.79 us  [the longest x1 2.69 us: finish(): pl.pallas_call(finish_kernel, out_shape=[shape, shape], in_specs=[scalar,...]
    unnamed x9 -> x7, local copies, waits for them, and re-layouts: 0.7 us -> 2.95 us
    pallas_call x1, Pallas kernels: 6.85 us -> 5.34 us  [attention(): pl.pallas_call(attention_kernel, out_shape=outs, in_specs=[scalar] * 2 +...]
    ppermute x12, starting transfers between devices: 16.5 us -> 15.2 us  [lon_shift(): lax.ppermute(value, 'lon', [(i, (i + steps) % count) for i in range(count)])]
    ppermute x5, starting transfers between devices: 2.73 us -> 1.65 us  [intra_swap(): lax.ppermute(value, 'lat', [(i, i ^ 1) for i in range(count) if i ^ 1 < c...]
  transfers between devices with their start and end apart: 23 -> 22, of which waited for: 9 -> 8; matrix products, arithmetic and copies ran while one was open for 2% -> 3% of each run, Pallas kernels for 0% -> 4%
where the time goes in v4:
time: 68 us; the launch traced here: 67.7 us
  starting transfers between devices  34.4 us (51%)
  waiting for transfers between devices  17.9 us (26%)
  Pallas kernels  8.13 us (12%)
  local copies, waits for them, and re-layouts  4.24 us (6%)
  other arithmetic  2.23 us (3%)
  between operations  0.84 us (1%)
    ppermute x5, starting transfers between devices, inter_swap(): lax.ppermute(value, 'lat', [(i, j) for i, j in pairs if 0 <= j < count])  17.5 us
    ppermute x12, starting transfers between devices, lon_shift(): lax.ppermute(value, 'lon', [(i, (i + steps) % count) for i in range(count)])  15.2 us
    ppermute x12, waiting for transfers between devices, lon_shift(): lax.ppermute(value, 'lon', [(i, (i + steps) % count) for i in range(count)])  13.7 us
    pallas_call x1, Pallas kernels, attention(): pl.pallas_call(attention_kernel, out_shape=outs, in_specs=[scalar] * 2 +...  5.34 us
    ppermute x5, waiting for transfers between devices, inter_swap(): lax.ppermute(value, 'lat', [(i, j) for i, j in pairs if 0 <= j < count])  3.35 us
    unnamed x7, local copies, waits for them, and re-layouts  2.95 us
    pallas_call x1, Pallas kernels, finish(): pl.pallas_call(finish_kernel, out_shape=[shape, shape], in_specs=[scalar,...  2.69 us
    ppermute x5, starting transfers between devices, intra_swap(): lax.ppermute(value, 'lat', [(i, i ^ 1) for i in range(count) if i ^ 1 < c...  1.65 us
  transfers between devices with their start and end apart: 22, of which 8 were waited for; matrix products, arithmetic and copies ran while one was open for 3% of the time, Pallas kernels for 4%

profile of v4, /device:TPU:3, one launch (start us, length us, event | category | flops | bytes accessed | tf_op | source)
XLA Modules:
  0.0 67.7 jit_solution(4391057673724224414)
XLA Ops:
  0.6 3.7 %collective-permute-start.1 = (bf16[2,1,2,64,1024]{4,3,2,1,0:T(8,128)(2,1)}, bf16[2,1,2,64,1024]{4,3,2,1,0:T(8,128)(2,1)S(1)}, u32[]{:S(2)}, u32[]{:S(2)}) collective-permute-start(bf16[2,1,2,64,1024]{4,3,2,1,0:T(8,128)(2,1)} %refs_2_.1), channel_id=1, source_target_pairs={{4,8},{8,4},{12,16},{16,12},{20,24},{24,20},{5,9},{9,5},{13,17},{1... | collective-permute-start | bytes 1572872 | tf_op jit(solution)/shard_map/ppermute | solution.py:28
  4.3 1.1 %fusion.6 = (bf16[1,1,1,64,1024]{4,3,2,1,0:T(8,128)(2,1)S(1)}, bf16[1,1,1,64,1024]{4,3,2,1,0:T(8,128)(2,1)S(1)}, bf16[1,1,1,64,1024]{4,3,2,1,0:T(8,128)(2,1)S(1)}, bf16[1,1,1,64,1024]{4,3,2,1,0:T(8,128)(2,1)S(1)}) fusion(bf16[2,1,2,64,1024]{4,3,2,1,0:T(8,128)(2,1)} %refs_2_.1), kind=kLoop, calls=%fused_computation.29 | loop fusion | bytes 1048576 | tf_op jit(solution)/shard_map/slice | solution.py:305
  5.5 1.3 %collective-permute-start.2 = (bf16[1,1,1,64,1024]{4,3,2,1,0:T(8,128)(2,1)S(1)}, bf16[1,1,1,64,1024]{4,3,2,1,0:T(8,128)(2,1)S(1)}, u32[]{:S(2)}, u32[]{:S(2)}) collective-permute-start(bf16[1,1,1,64,1024]{4,3,2,1,0:T(8,128)(2,1)S(1)} %get-tuple-element.43), channel_id=1, source_target_pairs={{0,1},{1,2},{2,3},{3,0},{4,5},{5,6},{6,7},{7,4},{8,9},{9,10},{10,1... | collective-permute-start | bytes 393224 | tf_op jit(solution)/shard_map/ppermute | solution.py:17
  6.8 2.1 %collective-permute-start.3 = (bf16[1,1,1,64,1024]{4,3,2,1,0:T(8,128)(2,1)S(1)}, bf16[1,1,1,64,1024]{4,3,2,1,0:T(8,128)(2,1)S(1)}, u32[]{:S(2)}, u32[]{:S(2)}) collective-permute-start(bf16[1,1,1,64,1024]{4,3,2,1,0:T(8,128)(2,1)S(1)} %get-tuple-element.42), channel_id=1, source_target_pairs={{0,3},{1,0},{2,1},{3,2},{4,7},{5,4},{6,5},{7,6},{8,11},{9,8},{10,9... | collective-permute-start | bytes 393224 | tf_op jit(solution)/shard_map/ppermute | solution.py:17
  8.9 1.4 %collective-permute-start.5 = (bf16[1,1,1,64,1024]{4,3,2,1,0:T(8,128)(2,1)S(1)}, bf16[1,1,1,64,1024]{4,3,2,1,0:T(8,128)(2,1)S(1)}, u32[]{:S(2)}, u32[]{:S(2)}) collective-permute-start(bf16[1,1,1,64,1024]{4,3,2,1,0:T(8,128)(2,1)S(1)} %get-tuple-element.41), channel_id=1, source_target_pairs={{0,3},{1,0},{2,1},{3,2},{4,7},{5,4},{6,5},{7,6},{8,11},{9,8},{10,9... | collective-permute-start | bytes 393224 | tf_op jit(solution)/shard_map/ppermute | solution.py:17
  10.3 2.3 %collective-permute-done.2.wk_ref = bf16[1,1,1,64,1024]{4,3,2,1,0:T(8,128)(2,1)S(1)} collective-permute-done((bf16[1,1,1,64,1024]{4,3,2,1,0:T(8,128)(2,1)S(1)}, bf16[1,1,1,64,1024]{4,3,2,1,0:T(8,128)(2,1)S(1)}, u32[]{:S(2)}, u32[]{:S(2)}) %collective-permute-start.2) | collective-permute-done | bytes 131104 | tf_op jit(solution)/shard_map/ppermute | solution.py:17
  12.6 2.5 %collective-permute-done.3.ek_ref = bf16[1,1,1,64,1024]{4,3,2,1,0:T(8,128)(2,1)S(1)} collective-permute-done((bf16[1,1,1,64,1024]{4,3,2,1,0:T(8,128)(2,1)S(1)}, bf16[1,1,1,64,1024]{4,3,2,1,0:T(8,128)(2,1)S(1)}, u32[]{:S(2)}, u32[]{:S(2)}) %collective-permute-start.3) | collective-permute-done | bytes 131104 | tf_op jit(solution)/shard_map/ppermute | solution.py:17
  15.1 3.9 %collective-permute-start.9 = (bf16[1,1,2,64,1024]{4,3,2,1,0:T(8,128)(2,1)S(1)}, bf16[1,1,2,64,1024]{4,3,2,1,0:T(8,128)(2,1)S(1)}, u32[]{:S(2)}, u32[]{:S(2)}) collective-permute-start(bf16[1,1,2,64,1024]{4,3,2,1,0:T(8,128)(2,1)S(1)} %constant_dynamic-update-slice_fusion), channel_id=1, source_target_pairs={{4,8},{8,4},{12,16},{16,12},{20,24},{24,20},{5,9},{9,5},{13,17},{1... | collective-permute-start | bytes 786440 | tf_op jit(solution)/shard_map/ppermute | solution.py:28
  19.2 2.4 %collective-permute-done.4.wv_ref = bf16[1,1,1,64,1024]{4,3,2,1,0:T(8,128)(2,1)S(1)} collective-permute-done((bf16[1,1,1,64,1024]{4,3,2,1,0:T(8,128)(2,1)S(1)}, bf16[1,1,1,64,1024]{4,3,2,1,0:T(8,128)(2,1)S(1)}, u32[]{:S(2)}, u32[]{:S(2)}) %collective-permute-start.4) | collective-permute-done | bytes 131104 | tf_op jit(solution)/shard_map/ppermute | solution.py:17
  22.9 2.4 %collective-permute-start.11 = (bf16[1,1,1,64,1024]{4,3,2,1,0:T(8,128)(2,1)S(1)}, bf16[1,1,1,64,1024]{4,3,2,1,0:T(8,128)(2,1)S(1)}, u32[]{:S(2)}, u32[]{:S(2)}) collective-permute-start(bf16[1,1,1,64,1024]{4,3,2,1,0:T(8,128)(2,1)S(1)} %get-tuple-element.39), channel_id=1, source_target_pairs={{0,3},{1,0},{2,1},{3,2},{4,7},{5,4},{6,5},{7,6},{8,11},{9,8},{10,9... | collective-permute-start | bytes 393224 | tf_op jit(solution)/shard_map/ppermute | solution.py:17
  26.1 1.0 %copy-done = bf16[2,1,2,64,1024]{4,3,2,1,0:T(8,128)(2,1)S(1)} copy-done((bf16[2,1,2,64,1024]{4,3,2,1,0:T(8,128)(2,1)S(1)}, bf16[2,1,2,64,1024]{4,3,2,1,0:T(8,128)(2,1)}, u32[]{:S(2)}) %copy-start) | copy-done | bytes 524312
  29.3 4.0 %collective-permute-done.10.cw_ref = bf16[1,1,1,64,1024]{4,3,2,1,0:T(8,128)(2,1)S(1)} collective-permute-done((bf16[1,1,1,64,1024]{4,3,2,1,0:T(8,128)(2,1)S(1)}, bf16[1,1,1,64,1024]{4,3,2,1,0:T(8,128)(2,1)S(1)}, u32[]{:S(2)}, u32[]{:S(2)}) %collective-permute-start.10) | collective-permute-done | bytes 131104 | tf_op jit(solution)/shard_map/ppermute | solution.py:17
  33.3 5.3 %attention.1 = (bf16[2,12,64,1024]{3,2,1,0:T(8,128)(2,1)S(1)}, bf16[2,2,4,384,256]{4,3,2,1,0:T(8,128)(2,1)S(1)}, f32[2,1,2,64,1024]{4,3,2,1,0:T(8,128)S(1)}, f32...) custom-call(s32[2,6]{1,0:T(2,128)S(1)} %fusion.2.slots, ...), custom_call_target="tpu_custom_call" | custom-call | flops 1610612736 | bytes 14417920 | tf_op jit(solution)/shard_map/attention/pallas_call | solution.py:199
  38.7 1.1 %collective-permute-start.12 = (bf16[2,1,4,64,1024]{4,3,2,1,0:T(8,128)(2,1)S(1)}, bf16[2,1,4,64,1024]{4,3,2,1,0:T(8,128)(2,1)S(1)}, u32[]{:S(2)}, u32[]{:S(2)}) collective-permute-start(bf16[2,1,4,64,1024]{4,3,2,1,0:T(8,128)(2,1)S(1)} %get-tuple-element.27), channel_id=1, source_target_pairs={{0,4},{4,0},{8,12},{12,8},{16,20},{20,16},{24,28},{28,24},{1,5},{5... | collective-permute-start | bytes 3145736 | tf_op jit(solution)/shard_map/ppermute | solution.py:22
  39.7 3.3 %collective-permute-start.18 = (bf16[1,1,1,64,1024]{4,3,2,1,0:T(8,128)(2,1)S(1)}, bf16[1,1,1,64,1024]{4,3,2,1,0:T(8,128)(2,1)S(1)}, u32[]{:S(2)}, u32[]{:S(2)}) collective-permute-start(bf16[1,1,1,64,1024]{4,3,2,1,0:T(8,128)(2,1)S(1)} %get-tuple-element.33), channel_id=1, source_target_pairs={{0,3},{1,0},{2,1},{3,2},{4,7},{5,4},{6,5},{7,6},{8,11},{9,8},{10,9... | collective-permute-start | bytes 393224 | tf_op jit(solution)/shard_map/ppermute | solution.py:17
  43.0 3.4 %collective-permute-start.14 = (bf16[1,1,2,64,1024]{4,3,2,1,0:T(8,128)(2,1)S(1)}, bf16[1,1,2,64,1024]{4,3,2,1,0:T(8,128)(2,1)S(1)}, u32[]{:S(2)}, u32[]{:S(2)}) collective-permute-start(bf16[1,1,2,64,1024]{4,3,2,1,0:T(8,128)(2,1)S(1)} %get-tuple-element.30), channel_id=1, source_target_pairs={{4,8},{8,4},{12,16},{16,12},{20,24},{24,20},{5,9},{9,5},{13,17},{1... | collective-permute-start | bytes 786440 | tf_op jit(solution)/shard_map/ppermute | solution.py:28
  46.5 3.0 %collective-permute-start.13 = (bf16[1,1,2,64,1024]{4,3,2,1,0:T(8,128)(2,1)S(1)}, bf16[1,1,2,64,1024]{4,3,2,1,0:T(8,128)(2,1)S(1)}, u32[]{:S(2)}, u32[]{:S(2)}) collective-permute-start(bf16[1,1,2,64,1024]{4,3,2,1,0:T(8,128)(2,1)S(1)} %get-tuple-element.28), channel_id=1, source_target_pairs={{4,8},{8,4},{12,16},{16,12},{20,24},{24,20},{5,9},{9,5},{13,17},{1... | collective-permute-start | bytes 786440 | tf_op jit(solution)/shard_map/ppermute | solution.py:28
  49.6 3.4 %collective-permute-start.19 = (bf16[1,1,2,64,1024]{4,3,2,1,0:T(8,128)(2,1)S(1)}, bf16[1,1,2,64,1024]{4,3,2,1,0:T(8,128)(2,1)S(1)}, u32[]{:S(2)}, u32[]{:S(2)}) collective-permute-start(bf16[1,1,2,64,1024]{4,3,2,1,0:T(8,128)(2,1)S(1)} %add_convert_fusion.2), channel_id=1, source_target_pairs={{4,8},{8,4},{12,16},{16,12},{20,24},{24,20},{5,9},{9,5},{13,17},{1... | collective-permute-start | bytes 786440 | tf_op jit(solution)/shard_map/ppermute | solution.py:28
  53.0 1.4 %collective-permute-done.14 = bf16[1,1,2,64,1024]{4,3,2,1,0:T(8,128)(2,1)S(1)} collective-permute-done((bf16[1,1,2,64,1024]{4,3,2,1,0:T(8,128)(2,1)S(1)}, bf16[1,1,2,64,1024]{4,3,2,1,0:T(8,128)(2,1)S(1)}, u32[]{:S(2)}, u32[]{:S(2)}) %collective-permute-start.14) | collective-permute-done | bytes 262176 | tf_op jit(solution)/shard_map/ppermute | solution.py:28
  54.7 3.3 %collective-permute-start.16 = (bf16[1,1,1,64,1024]{4,3,2,1,0:T(8,128)(2,1)S(1)}, bf16[1,1,1,64,1024]{4,3,2,1,0:T(8,128)(2,1)S(1)}, u32[]{:S(2)}, u32[]{:S(2)}) collective-permute-start(bf16[1,1,1,64,1024]{4,3,2,1,0:T(8,128)(2,1)S(1)} %get-tuple-element.46), channel_id=1, source_target_pairs={{0,3},{1,0},{2,1},{3,2},{4,7},{5,4},{6,5},{7,6},{8,11},{9,8},{10,9... | collective-permute-start | bytes 393224 | tf_op jit(solution)/shard_map/ppermute | solution.py:17
  58.1 2.0 %collective-permute-done.13 = bf16[1,1,2,64,1024]{4,3,2,1,0:T(8,128)(2,1)S(1)} collective-permute-done((bf16[1,1,2,64,1024]{4,3,2,1,0:T(8,128)(2,1)S(1)}, bf16[1,1,2,64,1024]{4,3,2,1,0:T(8,128)(2,1)S(1)}, u32[]{:S(2)}, u32[]{:S(2)}) %collective-permute-start.13) | collective-permute-done | bytes 262176 | tf_op jit(solution)/shard_map/ppermute | solution.py:28
  60.0 1.3 %collective-permute-start.21 = (bf16[1,1,1,64,1024]{4,3,2,1,0:T(8,128)(2,1)S(1)}, bf16[1,1,1,64,1024]{4,3,2,1,0:T(8,128)(2,1)S(1)}, u32[]{:S(2)}, u32[]{:S(2)}) collective-permute-start(bf16[1,1,1,64,1024]{4,3,2,1,0:T(8,128)(2,1)S(1)} %get-tuple-element.48), channel_id=1, source_target_pairs={{0,3},{1,0},{2,1},{3,2},{4,7},{5,4},{6,5},{7,6},{8,11},{9,8},{10,9... | collective-permute-start | bytes 393224 | tf_op jit(solution)/shard_map/ppermute | solution.py:17
  61.3 2.7 %finish.1 = (bf16[1,2,64,1024]{3,2,1,0:T(8,128)(2,1)}, bf16[1,2,64,1024]{3,2,1,0:T(8,128)(2,1)}) custom-call(s32[2,6]{1,0:T(2,128)S(1)} %fusion.2.slots, bf16[2,12,64,1024]{3,2,1,0:T(8,128)(2,1)S(1)} %get-tuple-element.22.kv, bf16[2,2,4,384,256]{4,3,2,1,0:T(8,128)(2,1)S(1)} %get-tuple-element.23.shares), custom_call_target="tpu_custom_call" | custom-call | flops 1610612736 | bytes 3145728 | tf_op jit(solution)/shard_map/finish/pallas_call | solution.py:261
  64.0 2.5 %collective-permute-done.20 = bf16[1,1,1,64,1024]{4,3,2,1,0:T(8,128)(2,1)S(1)} collective-permute-done((bf16[1,1,1,64,1024]{4,3,2,1,0:T(8,128)(2,1)S(1)}, bf16[1,1,1,64,1024]{4,3,2,1,0:T(8,128)(2,1)S(1)}, u32[]{:S(2)}, u32[]{:S(2)}) %collective-permute-start.20) | collective-permute-done | bytes 131104 | tf_op jit(solution)/shard_map/ppermute | solution.py:17
  (42 shorter events, 6.0 us)
Async XLA Ops:
  0.6 20.9 %collective-permute-start.1 = (bf16[2,1,2,64,1024]{4,3,2,1,0:T(8,128)(2,1)}, bf16[2,1,2,64,1024]{4,3,2,1,0:T(8,128)(2,1)S(1)}, u32[]{:S(2)}, u32[]{:S(2)}) collective-permute-start(bf16[2,1,2,64,1024]{4,3,2,1,0:T(8,128)(2,1)} %refs_2_.1), channel_id=1, source_target_pairs={{4,8},{8,4},{12,16},{16,12},{20,24},{24,20},{5,9},{9,5},{13,17},{1... | collective-permute-start | bytes 1572872 | tf_op jit(solution)/shard_map/ppermute | solution.py:28
  5.5 7.2 %collective-permute-start.2 = (bf16[1,1,1,64,1024]{4,3,2,1,0:T(8,128)(2,1)S(1)}, bf16[1,1,1,64,1024]{4,3,2,1,0:T(8,128)(2,1)S(1)}, u32[]{:S(2)}, u32[]{:S(2)}) collective-permute-start(bf16[1,1,1,64,1024]{4,3,2,1,0:T(8,128)(2,1)S(1)} %get-tuple-element.43), channel_id=1, source_target_pairs={{0,1},{1,2},{2,3},{3,0},{4,5},{5,6},{6,7},{7,4},{8,9},{9,10},{10,1... | collective-permute-start | bytes 393224 | tf_op jit(solution)/shard_map/ppermute | solution.py:17
  6.8 8.3 %collective-permute-start.3 = (bf16[1,1,1,64,1024]{4,3,2,1,0:T(8,128)(2,1)S(1)}, bf16[1,1,1,64,1024]{4,3,2,1,0:T(8,128)(2,1)S(1)}, u32[]{:S(2)}, u32[]{:S(2)}) collective-permute-start(bf16[1,1,1,64,1024]{4,3,2,1,0:T(8,128)(2,1)S(1)} %get-tuple-element.42), channel_id=1, source_target_pairs={{0,3},{1,0},{2,1},{3,2},{4,7},{5,4},{6,5},{7,6},{8,11},{9,8},{10,9... | collective-permute-start | bytes 393224 | tf_op jit(solution)/shard_map/ppermute | solution.py:17
  8.9 20.4 %collective-permute-start = (bf16[2,1,2,64,1024]{4,3,2,1,0:T(8,128)(2,1)}, bf16[2,1,2,64,1024]{4,3,2,1,0:T(8,128)(2,1)S(1)}, u32[]{:S(2)}, u32[]{:S(2)}) collective-permute-start(bf16[2,1,2,64,1024]{4,3,2,1,0:T(8,128)(2,1)} %refs_2_.1), channel_id=1, source_target_pairs={{0,4},{4,0},{8,12},{12,8},{16,20},{20,16},{24,28},{28,24},{1,5},{5... | collective-permute-start | bytes 1572872 | tf_op jit(solution)/shard_map/ppermute | solution.py:22
  8.9 10.2 %collective-permute-start.5 = (bf16[1,1,1,64,1024]{4,3,2,1,0:T(8,128)(2,1)S(1)}, bf16[1,1,1,64,1024]{4,3,2,1,0:T(8,128)(2,1)S(1)}, u32[]{:S(2)}, u32[]{:S(2)}) collective-permute-start(bf16[1,1,1,64,1024]{4,3,2,1,0:T(8,128)(2,1)S(1)} %get-tuple-element.41), channel_id=1, source_target_pairs={{0,3},{1,0},{2,1},{3,2},{4,7},{5,4},{6,5},{7,6},{8,11},{9,8},{10,9... | collective-permute-start | bytes 393224 | tf_op jit(solution)/shard_map/ppermute | solution.py:17
  12.6 8.9 %collective-permute-start.4 = (bf16[1,1,1,64,1024]{4,3,2,1,0:T(8,128)(2,1)S(1)}, bf16[1,1,1,64,1024]{4,3,2,1,0:T(8,128)(2,1)S(1)}, u32[]{:S(2)}, u32[]{:S(2)}) collective-permute-start(bf16[1,1,1,64,1024]{4,3,2,1,0:T(8,128)(2,1)S(1)} %get-tuple-element.44), channel_id=1, source_target_pairs={{0,1},{1,2},{2,3},{3,0},{4,5},{5,6},{6,7},{7,4},{8,9},{9,10},{10,1... | collective-permute-start | bytes 393224 | tf_op jit(solution)/shard_map/ppermute | solution.py:17
  15.1 14.2 %collective-permute-start.9 = (bf16[1,1,2,64,1024]{4,3,2,1,0:T(8,128)(2,1)S(1)}, bf16[1,1,2,64,1024]{4,3,2,1,0:T(8,128)(2,1)S(1)}, u32[]{:S(2)}, u32[]{:S(2)}) collective-permute-start(bf16[1,1,2,64,1024]{4,3,2,1,0:T(8,128)(2,1)S(1)} %constant_dynamic-update-slice_fusion), channel_id=1, source_target_pairs={{4,8},{8,4},{12,16},{16,12},{20,24},{24,20},{5,9},{9,5},{13,17},{1... | collective-permute-start | bytes 786440 | tf_op jit(solution)/shard_map/ppermute | solution.py:28
  19.1 10.2 %collective-permute-start.6 = (bf16[1,1,2,64,1024]{4,3,2,1,0:T(8,128)(2,1)S(1)}, bf16[1,1,2,64,1024]{4,3,2,1,0:T(8,128)(2,1)S(1)}, u32[]{:S(2)}, u32[]{:S(2)}) collective-permute-start(bf16[1,1,2,64,1024]{4,3,2,1,0:T(8,128)(2,1)S(1)} %constant_dynamic-update-slice_fusion), channel_id=1, source_target_pairs={{0,4},{4,0},{8,12},{12,8},{16,20},{20,16},{24,28},{28,24},{1,5},{5... | collective-permute-start | bytes 786440 | tf_op jit(solution)/shard_map/ppermute | solution.py:22
  21.5 1.3 %collective-permute-start.8 = (bf16[1,1,1,64,1024]{4,3,2,1,0:T(8,128)(2,1)S(1)}, bf16[1,1,1,64,1024]{4,3,2,1,0:T(8,128)(2,1)S(1)}, u32[]{:S(2)}, u32[]{:S(2)}) collective-permute-start(bf16[1,1,1,64,1024]{4,3,2,1,0:T(8,128)(2,1)S(1)} %collective-permute-done.5.ev_ref), channel_id=1, source_target_pairs={{0,4},{4,0},{8,12},{12,8},{16,20},{20,16},{24,28},{28,24},{1,5},{5... | collective-permute-start | bytes 393224 | tf_op jit(solution)/shard_map/ppermute | solution.py:22
  21.6 3.8 %collective-permute-start.7 = (bf16[1,1,1,64,1024]{4,3,2,1,0:T(8,128)(2,1)S(1)}, bf16[1,1,1,64,1024]{4,3,2,1,0:T(8,128)(2,1)S(1)}, u32[]{:S(2)}, u32[]{:S(2)}) collective-permute-start(bf16[1,1,1,64,1024]{4,3,2,1,0:T(8,128)(2,1)S(1)} %collective-permute-done.4.wv_ref), channel_id=1, source_target_pairs={{0,4},{4,0},{8,12},{12,8},{16,20},{20,16},{24,28},{28,24},{1,5},{5... | collective-permute-start | bytes 393224 | tf_op jit(solution)/shard_map/ppermute | solution.py:22
  22.9 6.4 %collective-permute-start.11 = (bf16[1,1,1,64,1024]{4,3,2,1,0:T(8,128)(2,1)S(1)}, bf16[1,1,1,64,1024]{4,3,2,1,0:T(8,128)(2,1)S(1)}, u32[]{:S(2)}, u32[]{:S(2)}) collective-permute-start(bf16[1,1,1,64,1024]{4,3,2,1,0:T(8,128)(2,1)S(1)} %get-tuple-element.39), channel_id=1, source_target_pairs={{0,3},{1,0},{2,1},{3,2},{4,7},{5,4},{6,5},{7,6},{8,11},{9,8},{10,9... | collective-permute-start | bytes 393224 | tf_op jit(solution)/shard_map/ppermute | solution.py:17
  25.3 8.0 %collective-permute-start.10 = (bf16[1,1,1,64,1024]{4,3,2,1,0:T(8,128)(2,1)S(1)}, bf16[1,1,1,64,1024]{4,3,2,1,0:T(8,128)(2,1)S(1)}, u32[]{:S(2)}, u32[]{:S(2)}) collective-permute-start(bf16[1,1,1,64,1024]{4,3,2,1,0:T(8,128)(2,1)S(1)} %get-tuple-element.40), channel_id=1, source_target_pairs={{0,1},{1,2},{2,3},{3,0},{4,5},{5,6},{6,7},{7,4},{8,9},{9,10},{10,1... | collective-permute-start | bytes 393224 | tf_op jit(solution)/shard_map/ppermute | solution.py:17
  26.1 1.0 %copy-start = (bf16[2,1,2,64,1024]{4,3,2,1,0:T(8,128)(2,1)S(1)}, bf16[2,1,2,64,1024]{4,3,2,1,0:T(8,128)(2,1)}, u32[]{:S(2)}) copy-start(bf16[2,1,2,64,1024]{4,3,2,1,0:T(8,128)(2,1)} %refs_2_.1) | copy-start | bytes 1572868
  27.2 0.9 %copy-start.1 = (bf16[1,2,64,1024]{3,2,1,0:T(8,128)(2,1)S(1)}, bf16[1,2,64,1024]{3,2,1,0:T(8,128)(2,1)}, u32[]{:S(2)}) copy-start(bf16[1,2,64,1024]{3,2,1,0:T(8,128)(2,1)} %refs_0_.1) | copy-start | bytes 786436
  38.7 15.7 %collective-permute-start.12 = (bf16[2,1,4,64,1024]{4,3,2,1,0:T(8,128)(2,1)S(1)}, bf16[2,1,4,64,1024]{4,3,2,1,0:T(8,128)(2,1)S(1)}, u32[]{:S(2)}, u32[]{:S(2)}) collective-permute-start(bf16[2,1,4,64,1024]{4,3,2,1,0:T(8,128)(2,1)S(1)} %get-tuple-element.27), channel_id=1, source_target_pairs={{0,4},{4,0},{8,12},{12,8},{16,20},{20,16},{24,28},{28,24},{1,5},{5... | collective-permute-start | bytes 3145736 | tf_op jit(solution)/shard_map/ppermute | solution.py:22
  39.7 9.7 %collective-permute-start.17 = (bf16[1,1,1,64,1024]{4,3,2,1,0:T(8,128)(2,1)S(1)}, bf16[1,1,1,64,1024]{4,3,2,1,0:T(8,128)(2,1)S(1)}, u32[]{:S(2)}, u32[]{:S(2)}) collective-permute-start(bf16[1,1,1,64,1024]{4,3,2,1,0:T(8,128)(2,1)S(1)} %get-tuple-element.32), channel_id=1, source_target_pairs={{0,1},{1,2},{2,3},{3,0},{4,5},{5,6},{6,7},{7,4},{8,9},{9,10},{10,1... | collective-permute-start | bytes 393224 | tf_op jit(solution)/shard_map/ppermute | solution.py:17
  39.7 9.7 %collective-permute-start.18 = (bf16[1,1,1,64,1024]{4,3,2,1,0:T(8,128)(2,1)S(1)}, bf16[1,1,1,64,1024]{4,3,2,1,0:T(8,128)(2,1)S(1)}, u32[]{:S(2)}, u32[]{:S(2)}) collective-permute-start(bf16[1,1,1,64,1024]{4,3,2,1,0:T(8,128)(2,1)S(1)} %get-tuple-element.33), channel_id=1, source_target_pairs={{0,3},{1,0},{2,1},{3,2},{4,7},{5,4},{6,5},{7,6},{8,11},{9,8},{10,9... | collective-permute-start | bytes 393224 | tf_op jit(solution)/shard_map/ppermute | solution.py:17
  43.0 11.4 %collective-permute-start.14 = (bf16[1,1,2,64,1024]{4,3,2,1,0:T(8,128)(2,1)S(1)}, bf16[1,1,2,64,1024]{4,3,2,1,0:T(8,128)(2,1)S(1)}, u32[]{:S(2)}, u32[]{:S(2)}) collective-permute-start(bf16[1,1,2,64,1024]{4,3,2,1,0:T(8,128)(2,1)S(1)} %get-tuple-element.30), channel_id=1, source_target_pairs={{4,8},{8,4},{12,16},{16,12},{20,24},{24,20},{5,9},{9,5},{13,17},{1... | collective-permute-start | bytes 786440 | tf_op jit(solution)/shard_map/ppermute | solution.py:28
  46.5 13.6 %collective-permute-start.13 = (bf16[1,1,2,64,1024]{4,3,2,1,0:T(8,128)(2,1)S(1)}, bf16[1,1,2,64,1024]{4,3,2,1,0:T(8,128)(2,1)S(1)}, u32[]{:S(2)}, u32[]{:S(2)}) collective-permute-start(bf16[1,1,2,64,1024]{4,3,2,1,0:T(8,128)(2,1)S(1)} %get-tuple-element.28), channel_id=1, source_target_pairs={{4,8},{8,4},{12,16},{16,12},{20,24},{24,20},{5,9},{9,5},{13,17},{1... | collective-permute-start | bytes 786440 | tf_op jit(solution)/shard_map/ppermute | solution.py:28
  49.6 14.4 %collective-permute-start.19 = (bf16[1,1,2,64,1024]{4,3,2,1,0:T(8,128)(2,1)S(1)}, bf16[1,1,2,64,1024]{4,3,2,1,0:T(8,128)(2,1)S(1)}, u32[]{:S(2)}, u32[]{:S(2)}) collective-permute-start(bf16[1,1,2,64,1024]{4,3,2,1,0:T(8,128)(2,1)S(1)} %add_convert_fusion.2), channel_id=1, source_target_pairs={{4,8},{8,4},{12,16},{16,12},{20,24},{24,20},{5,9},{9,5},{13,17},{1... | collective-permute-start | bytes 786440 | tf_op jit(solution)/shard_map/ppermute | solution.py:28
  54.6 9.4 %collective-permute-start.15 = (bf16[1,1,1,64,1024]{4,3,2,1,0:T(8,128)(2,1)S(1)}, bf16[1,1,1,64,1024]{4,3,2,1,0:T(8,128)(2,1)S(1)}, u32[]{:S(2)}, u32[]{:S(2)}) collective-permute-start(bf16[1,1,1,64,1024]{4,3,2,1,0:T(8,128)(2,1)S(1)} %get-tuple-element.45), channel_id=1, source_target_pairs={{0,1},{1,2},{2,3},{3,0},{4,5},{5,6},{6,7},{7,4},{8,9},{9,10},{10,1... | collective-permute-start | bytes 393224 | tf_op jit(solution)/shard_map/ppermute | solution.py:17
  54.7 9.3 %collective-permute-start.16 = (bf16[1,1,1,64,1024]{4,3,2,1,0:T(8,128)(2,1)S(1)}, bf16[1,1,1,64,1024]{4,3,2,1,0:T(8,128)(2,1)S(1)}, u32[]{:S(2)}, u32[]{:S(2)}) collective-permute-start(bf16[1,1,1,64,1024]{4,3,2,1,0:T(8,128)(2,1)S(1)} %get-tuple-element.46), channel_id=1, source_target_pairs={{0,3},{1,0},{2,1},{3,2},{4,7},{5,4},{6,5},{7,6},{8,11},{9,8},{10,9... | collective-permute-start | bytes 393224 | tf_op jit(solution)/shard_map/ppermute | solution.py:17
  58.0 8.5 %collective-permute-start.20 = (bf16[1,1,1,64,1024]{4,3,2,1,0:T(8,128)(2,1)S(1)}, bf16[1,1,1,64,1024]{4,3,2,1,0:T(8,128)(2,1)S(1)}, u32[]{:S(2)}, u32[]{:S(2)}) collective-permute-start(bf16[1,1,1,64,1024]{4,3,2,1,0:T(8,128)(2,1)S(1)} %get-tuple-element.47), channel_id=1, source_target_pairs={{0,1},{1,2},{2,3},{3,0},{4,5},{5,6},{6,7},{7,4},{8,9},{9,10},{10,1... | collective-permute-start | bytes 393224 | tf_op jit(solution)/shard_map/ppermute | solution.py:17
  60.0 6.5 %collective-permute-start.21 = (bf16[1,1,1,64,1024]{4,3,2,1,0:T(8,128)(2,1)S(1)}, bf16[1,1,1,64,1024]{4,3,2,1,0:T(8,128)(2,1)S(1)}, u32[]{:S(2)}, u32[]{:S(2)}) collective-permute-start(bf16[1,1,1,64,1024]{4,3,2,1,0:T(8,128)(2,1)S(1)} %get-tuple-element.48), channel_id=1, source_target_pairs={{0,3},{1,0},{2,1},{3,2},{4,7},{5,4},{6,5},{7,6},{8,11},{9,8},{10,9... | collective-permute-start | bytes 393224 | tf_op jit(solution)/shard_map/ppermute | solution.py:17
  (1 other events, 0.9 us)

commit v5 on v4

--- a/solution.py
+++ b/solution.py
@@ -35,9 +35,11 @@
 def attention_kernel(
     slots,
     places,
-    q_ref,
-    c_ref,
-    own_ref,
+    qc_ref,
+    fk_ref,
+    lk_ref,
+    fv_ref,
+    lv_ref,
     intra_ref,
     inter_ref,
     wk_ref,
@@ -64,16 +66,19 @@
     grad,
     sems,
 ):
-    _, cols, cells, width = q_ref.shape
+    _, cols, cells, width = qc_ref.shape
     wide = cols + 2
     samples = slots.shape[1]
     groups = width // LANES
     scale = HEAD_DIM**-0.5
     low = jnp.bfloat16
 
-    near, far = pl.ds(0, cols), pl.ds(2 * wide, cols)
+    far = pl.ds(2 * wide, cols)
     moves = (
-        (own_ref, slice(None), 0, near),
+        (fk_ref, pl.ds(0, 1), 0, pl.ds(0, cols - 1)),
+        (lk_ref, pl.ds(0, 1), 0, pl.ds(cols - 1, 1)),
+        (fv_ref, pl.ds(1, 1), 0, pl.ds(0, cols - 1)),
+        (lv_ref, pl.ds(1, 1), 0, pl.ds(cols - 1, 1)),
         (intra_ref, slice(None), 0, pl.ds(wide, cols)),
         (inter_ref, slice(None), 0, far),
         (wk_ref, pl.ds(0, 1), 0, pl.ds(cols, 1)),
@@ -119,8 +124,8 @@
                 copy.wait()
         spans = range(cols)
         listed = [[slots[b, s] for s in range(samples)] for b in spans]
-        query = [spread(q_ref[0, b, :, lanes]) for b in spans]
-        upstream = [spread(c_ref[0, b, :, lanes]) for b in spans]
+        query = [spread(qc_ref[0, b, :, lanes]) for b in spans]
+        upstream = [spread(qc_ref[1, b, :, lanes]) for b in spans]
         keys = [jnp.concatenate([kv[0, s, :, lanes] for s in x], axis=0) for x in listed]
         values = [jnp.concatenate([kv[1, s, :, lanes] for s in x], axis=0) for x in listed]
         scores = [dot(keys[b], query[b], ((1,), (1,))) for b in spans]
@@ -168,8 +173,7 @@
 
 
 def attention(slots, places, operands):
-    queries = operands[0]
-    _, cols, cells, width = queries.shape
+    _, cols, cells, width = operands[0].shape
     wide = cols + 2
     samples = slots.shape[1]
 
@@ -199,11 +203,11 @@
     return pl.pallas_call(
         attention_kernel,
         out_shape=outs,
-        in_specs=[scalar] * 2 + [vector] * 2 + [anywhere] * (len(operands) - 2),
+        in_specs=[scalar] * 2 + [vector] + [anywhere] * (len(operands) - 1),
         out_specs=[vector] * len(outs),
         scratch_shapes=[
             pltpu.VMEM((cols, 2, samples + 1, cells, LANES), full),
-            pltpu.SemaphoreType.DMA((2, len(operands) - 2)),
+            pltpu.SemaphoreType.DMA((2, len(operands) - 1)),
         ],
         cost_estimate=pl.CostEstimate(
             flops=flops, bytes_accessed=moved, transcendentals=cols * width * keys
@@ -211,30 +215,6 @@
         compiler_params=pltpu.CompilerParams(vmem_limit_bytes=20 * 1024 * 1024),
         name="attention",
     )(slots, places, *operands)
-
-
-def stage_kernel(*refs):
-    sems = refs[-1]
-    count = len(refs) // 2
-    copies = [
-        pltpu.make_async_copy(refs[i], refs[count + i], sems.at[i]) for i in range(count)
-    ]
-    for copy in copies:
-        copy.start()
-    for copy in copies:
-        copy.wait()
-
-
-def stage(*arrays):
-    return pl.pallas_call(
-        stage_kernel,
-        out_shape=[jax.ShapeDtypeStruct(x.shape, x.dtype) for x in arrays],
-        in_specs=[pl.BlockSpec(memory_space=pl.ANY) for _ in arrays],
-        out_specs=[pl.BlockSpec(memory_space=pltpu.VMEM) for _ in arrays],
-        scratch_shapes=[pltpu.SemaphoreType.DMA((len(arrays),))],
-        compiler_params=pltpu.CompilerParams(vmem_limit_bytes=8 * 1024 * 1024),
-        name="stage",
-    )(*arrays)
 
 
 def finish_kernel(slots, kv, shares, gq_ref, att_ref):
@@ -313,11 +293,13 @@
     intra_west = intra_swap(west_values)
     intra_east = intra_swap(east_values)
 
-    queries_near, cotangent_near, own_near = stage(queries, cotangent, keys_values)
+    queries_cotangent = jnp.concatenate([queries, cotangent], axis=0)
     operands = (
-        queries_near,
-        cotangent_near,
-        own_near,
+        queries_cotangent,
+        keys[:, :, : cols - 1],
+        keys[:, :, cols - 1 :],
+        values[:, :, : cols - 1],
+        values[:, :, cols - 1 :],
         intra,
         inter,
         west_keys,
@@ -341,11 +323,13 @@
     from_intra = intra_swap(to_intra)
     from_inter_k = inter_swap(near_k)
     side_v = (side_v + from_intra[1:, :, cols:].astype(full)).astype(low)
-    from_east_v = lon_shift(side_v[:, :, :1], -1)
-    from_west_v = lon_shift(side_v[:, :, 1:], 1)
     side_k = (side_k + from_intra[:1, :, cols:].astype(full) + from_k.astype(full)).astype(low)
-    from_east_k = lon_shift(side_k[:, :, :1], -1)
-    from_west_k = lon_shift(side_k[:, :, 1:], 1)
+    to_east = jnp.concatenate([side_k[:, :, :1], side_v[:, :, :1]], axis=0)
+    to_west = jnp.concatenate([side_k[:, :, 1:], side_v[:, :, 1:]], axis=0)
+    from_east = lon_shift(to_east, -1)
+    from_west = lon_shift(to_west, 1)
+    from_east_k, from_east_v = from_east[:1], from_east[1:]
+    from_west_k, from_west_v = from_west[:1], from_west[1:]
     near_v = (near_v + edges(from_e.astype(full), from_w.astype(full), cols)).astype(low)
     from_inter_v = inter_swap(near_v)
 

time: 68 us -> 69.1 us (1.016)
  local copies, waits for them, and re-layouts: 4.24 us -> 1.34 us
  waiting for transfers between devices: 17.9 us -> 20.1 us
  other arithmetic: 2.23 us -> 3.35 us
    ppermute x12 -> x10, waiting for transfers between devices: 13.7 us -> 18 us  [lon_shift(): lax.ppermute(value, 'lon', [(i, (i + steps) % count) for i in range(count)])]
    unnamed x7 -> x1, local copies, waits for them, and re-layouts: 2.95 us -> 0.01 us
    ppermute x5, waiting for transfers between devices: 3.35 us -> 1.07 us  [inter_swap(): lax.ppermute(value, 'lat', [(i, j) for i, j in pairs if 0 <= j < count])]
    ppermute x12 -> x10, starting transfers between devices: 15.2 us -> 13.7 us  [lon_shift(): lax.ppermute(value, 'lon', [(i, (i + steps) % count) for i in range(count)])]
    ppermute x5, starting transfers between devices: 17.5 us -> 19 us  [inter_swap(): lax.ppermute(value, 'lat', [(i, j) for i, j in pairs if 0 <= j < count])]
    concatenate x0 -> x3, other arithmetic: none -> 1.14 us  [the longest x1 1.08 us: body(): queries_cotangent = jnp.concatenate([queries, cotangent], axis=0)]
  transfers between devices with their start and end apart: 22 -> 20, of which waited for: 8 -> 7; matrix products, arithmetic and copies ran while one was open for 3% -> 5% of each run, Pallas kernels for 4% -> 4%
where the time goes in v5:
time: 69.1 us; the launch traced here: 68.7 us
  starting transfers between devices  34.9 us (51%)
  waiting for transfers between devices  20.1 us (29%)
  Pallas kernels  8.11 us (12%)
  other arithmetic  3.35 us (5%)
  local copies, waits for them, and re-layouts  1.34 us (2%)
  between operations  0.83 us (1%)
    ppermute x5, starting transfers between devices, inter_swap(): lax.ppermute(value, 'lat', [(i, j) for i, j in pairs if 0 <= j < count])  19 us
    ppermute x10, waiting for transfers between devices, lon_shift(): lax.ppermute(value, 'lon', [(i, (i + steps) % count) for i in range(count)])  18 us
    ppermute x10, starting transfers between devices, lon_shift(): lax.ppermute(value, 'lon', [(i, (i + steps) % count) for i in range(count)])  13.7 us
    pallas_call x1, Pallas kernels, attention(): pl.pallas_call(attention_kernel, out_shape=outs, in_specs=[scalar] * 2 +...  5.41 us
    pallas_call x1, Pallas kernels, finish(): pl.pallas_call(finish_kernel, out_shape=[shape, shape], in_specs=[scalar,...  2.7 us
    ppermute x5, starting transfers between devices, intra_swap(): lax.ppermute(value, 'lat', [(i, i ^ 1) for i in range(count) if i ^ 1 < c...  2.28 us
  transfers between devices with their start and end apart: 20, of which 7 were waited for; matrix products, arithmetic and copies ran while one was open for 5% of the time, Pallas kernels for 4%

profile of v5, /device:TPU:3, one launch (start us, length us, event | category | flops | bytes accessed | tf_op | source)
XLA Modules:
  0.0 68.7 jit_solution(16853201256894087442)
XLA Ops:
  0.6 3.7 %collective-permute-start.1 = (bf16[2,1,2,64,1024]{4,3,2,1,0:T(8,128)(2,1)}, bf16[2,1,2,64,1024]{4,3,2,1,0:T(8,128)(2,1)S(1)}, u32[]{:S(2)}, u32[]{:S(2)}) collective-permute-start(bf16[2,1,2,64,1024]{4,3,2,1,0:T(8,128)(2,1)} %param.5), channel_id=1, source_target_pairs={{4,8},{8,4},{12,16},{16,12},{20,24},{24,20},{5,9},{9,5},{13,17},{1... | collective-permute-start | bytes 1572872 | tf_op jit(solution)/shard_map/ppermute | solution.py:28
  4.4 1.1 %fusion.6 = (bf16[1,1,1,64,1024]{4,3,2,1,0:T(8,128)(2,1)S(1)}, bf16[1,1,1,64,1024]{4,3,2,1,0:T(8,128)(2,1)S(1)}, bf16[1,1,1,64,1024]{4,3,2,1,0:T(8,128)(2,1)S(1)}, bf16[1,1,1,64,1024]{4,3,2,1,0:T(8,128)(2,1)S(1)}) fusion(bf16[2,1,2,64,1024]{4,3,2,1,0:T(8,128)(2,1)} %param.5), kind=kLoop, calls=%fused_computation.32 | loop fusion | bytes 1048576 | tf_op jit(solution)/shard_map/slice | solution.py:302
  5.5 1.3 %collective-permute-start.4 = (bf16[1,1,1,64,1024]{4,3,2,1,0:T(8,128)(2,1)S(1)}, bf16[1,1,1,64,1024]{4,3,2,1,0:T(8,128)(2,1)S(1)}, u32[]{:S(2)}, u32[]{:S(2)}) collective-permute-start(bf16[1,1,1,64,1024]{4,3,2,1,0:T(8,128)(2,1)S(1)} %get-tuple-element.35.lv_ref), channel_id=1, source_target_pairs={{0,1},{1,2},{2,3},{3,0},{4,5},{5,6},{6,7},{7,4},{8,9},{9,10},{10,1... | collective-permute-start | bytes 393224 | tf_op jit(solution)/shard_map/ppermute | solution.py:17
  6.9 1.3 %collective-permute-start.2 = (bf16[1,1,1,64,1024]{4,3,2,1,0:T(8,128)(2,1)S(1)}, bf16[1,1,1,64,1024]{4,3,2,1,0:T(8,128)(2,1)S(1)}, u32[]{:S(2)}, u32[]{:S(2)}) collective-permute-start(bf16[1,1,1,64,1024]{4,3,2,1,0:T(8,128)(2,1)S(1)} %get-tuple-element.37.lk_ref), channel_id=1, source_target_pairs={{0,1},{1,2},{2,3},{3,0},{4,5},{5,6},{6,7},{7,4},{8,9},{9,10},{10,1... | collective-permute-start | bytes 393224 | tf_op jit(solution)/shard_map/ppermute | solution.py:17
  8.2 2.0 %collective-permute-start.3 = (bf16[1,1,1,64,1024]{4,3,2,1,0:T(8,128)(2,1)S(1)}, bf16[1,1,1,64,1024]{4,3,2,1,0:T(8,128)(2,1)S(1)}, u32[]{:S(2)}, u32[]{:S(2)}) collective-permute-start(bf16[1,1,1,64,1024]{4,3,2,1,0:T(8,128)(2,1)S(1)} %get-tuple-element.38.fk_ref), channel_id=1, source_target_pairs={{0,3},{1,0},{2,1},{3,2},{4,7},{5,4},{6,5},{7,6},{8,11},{9,8},{10,9... | collective-permute-start | bytes 393224 | tf_op jit(solution)/shard_map/ppermute | solution.py:17
  10.9 4.0 %collective-permute-done.2.wk_ref = bf16[1,1,1,64,1024]{4,3,2,1,0:T(8,128)(2,1)S(1)} collective-permute-done((bf16[1,1,1,64,1024]{4,3,2,1,0:T(8,128)(2,1)S(1)}, bf16[1,1,1,64,1024]{4,3,2,1,0:T(8,128)(2,1)S(1)}, u32[]{:S(2)}, u32[]{:S(2)}) %collective-permute-start.2) | collective-permute-done | bytes 131104 | tf_op jit(solution)/shard_map/ppermute | solution.py:17
  14.9 1.6 %collective-permute-start.5 = (bf16[1,1,1,64,1024]{4,3,2,1,0:T(8,128)(2,1)S(1)}, bf16[1,1,1,64,1024]{4,3,2,1,0:T(8,128)(2,1)S(1)}, u32[]{:S(2)}, u32[]{:S(2)}) collective-permute-start(bf16[1,1,1,64,1024]{4,3,2,1,0:T(8,128)(2,1)S(1)} %get-tuple-element.36.fv_ref), channel_id=1, source_target_pairs={{0,3},{1,0},{2,1},{3,2},{4,7},{5,4},{6,5},{7,6},{8,11},{9,8},{10,9... | collective-permute-start | bytes 393224 | tf_op jit(solution)/shard_map/ppermute | solution.py:17
  16.5 2.0 %collective-permute-done.3.ek_ref = bf16[1,1,1,64,1024]{4,3,2,1,0:T(8,128)(2,1)S(1)} collective-permute-done((bf16[1,1,1,64,1024]{4,3,2,1,0:T(8,128)(2,1)S(1)}, bf16[1,1,1,64,1024]{4,3,2,1,0:T(8,128)(2,1)S(1)}, u32[]{:S(2)}, u32[]{:S(2)}) %collective-permute-start.3) | collective-permute-done | bytes 131104 | tf_op jit(solution)/shard_map/ppermute | solution.py:17
  18.5 5.3 %collective-permute-start.9 = (bf16[1,1,2,64,1024]{4,3,2,1,0:T(8,128)(2,1)S(1)}, bf16[1,1,2,64,1024]{4,3,2,1,0:T(8,128)(2,1)S(1)}, u32[]{:S(2)}, u32[]{:S(2)}) collective-permute-start(bf16[1,1,2,64,1024]{4,3,2,1,0:T(8,128)(2,1)S(1)} %constant_dynamic-update-slice_fusion), channel_id=1, source_target_pairs={{4,8},{8,4},{12,16},{16,12},{20,24},{24,20},{5,9},{9,5},{13,17},{1... | collective-permute-start | bytes 786440 | tf_op jit(solution)/shard_map/ppermute | solution.py:28
  24.5 1.1 %collective-permute-done.7.sw_ref = bf16[1,1,1,64,1024]{4,3,2,1,0:T(8,128)(2,1)S(1)} collective-permute-done((bf16[1,1,1,64,1024]{4,3,2,1,0:T(8,128)(2,1)S(1)}, bf16[1,1,1,64,1024]{4,3,2,1,0:T(8,128)(2,1)S(1)}, u32[]{:S(2)}, u32[]{:S(2)}) %collective-permute-start.7) | collective-permute-done | bytes 131104 | tf_op jit(solution)/shard_map/ppermute | solution.py:22
  25.6 2.6 %collective-permute-start.11 = (bf16[1,1,1,64,1024]{4,3,2,1,0:T(8,128)(2,1)S(1)}, bf16[1,1,1,64,1024]{4,3,2,1,0:T(8,128)(2,1)S(1)}, u32[]{:S(2)}, u32[]{:S(2)}) collective-permute-start(bf16[1,1,1,64,1024]{4,3,2,1,0:T(8,128)(2,1)S(1)} %get-tuple-element.33), channel_id=1, source_target_pairs={{0,3},{1,0},{2,1},{3,2},{4,7},{5,4},{6,5},{7,6},{8,11},{9,8},{10,9... | collective-permute-start | bytes 393224 | tf_op jit(solution)/shard_map/ppermute | solution.py:17
  28.3 1.1 %pad_maximum_fusion.qc_ref = bf16[2,2,64,1024]{3,2,1,0:T(8,128)(2,1)S(1)} fusion(bf16[1,2,64,1024]{3,2,1,0:T(8,128)(2,1)} %param.6, bf16[1,2,64,1024]{3,2,1,0:T(8,128)(2,1)} %param.4), kind=kLoop, calls=%fused_computation | loop fusion | flops 262144 | bytes 1048576 | tf_op jit(solution)/shard_map/concatenate | solution.py:296
  29.4 1.1 %collective-permute-done.9.ck_ref = bf16[1,1,2,64,1024]{4,3,2,1,0:T(8,128)(2,1)S(1)} collective-permute-done((bf16[1,1,2,64,1024]{4,3,2,1,0:T(8,128)(2,1)S(1)}, bf16[1,1,2,64,1024]{4,3,2,1,0:T(8,128)(2,1)S(1)}, u32[]{:S(2)}, u32[]{:S(2)}) %collective-permute-start.9) | collective-permute-done | bytes 262176 | tf_op jit(solution)/shard_map/ppermute | solution.py:28
  30.7 3.7 %collective-permute-done.10.cw_ref = bf16[1,1,1,64,1024]{4,3,2,1,0:T(8,128)(2,1)S(1)} collective-permute-done((bf16[1,1,1,64,1024]{4,3,2,1,0:T(8,128)(2,1)S(1)}, bf16[1,1,1,64,1024]{4,3,2,1,0:T(8,128)(2,1)S(1)}, u32[]{:S(2)}, u32[]{:S(2)}) %collective-permute-start.10) | collective-permute-done | bytes 131104 | tf_op jit(solution)/shard_map/ppermute | solution.py:17
  34.4 5.4 %attention.1 = (bf16[2,12,64,1024]{3,2,1,0:T(8,128)(2,1)S(1)}, bf16[2,2,4,384,256]{4,3,2,1,0:T(8,128)(2,1)S(1)}, f32[2,1,2,64,1024]{4,3,2,1,0:T(8,128)S(1)}, f32...) custom-call(s32[2,6]{1,0:T(2,128)S(1)} %fusion.2.slots, ...), custom_call_target="tpu_custom_call" | custom-call | flops 1610612736 | bytes 14417920 | tf_op jit(solution)/shard_map/attention/pallas_call | solution.py:203
  39.8 1.6 %collective-permute-start.12 = (bf16[2,1,4,64,1024]{4,3,2,1,0:T(8,128)(2,1)S(1)}, bf16[2,1,4,64,1024]{4,3,2,1,0:T(8,128)(2,1)S(1)}, u32[]{:S(2)}, u32[]{:S(2)}) collective-permute-start(bf16[2,1,4,64,1024]{4,3,2,1,0:T(8,128)(2,1)S(1)} %get-tuple-element.21), channel_id=1, source_target_pairs={{0,4},{4,0},{8,12},{12,8},{16,20},{20,16},{24,28},{28,24},{1,5},{5... | collective-permute-start | bytes 3145736 | tf_op jit(solution)/shard_map/ppermute | solution.py:22
  41.4 3.0 %collective-permute-start.14 = (bf16[1,1,2,64,1024]{4,3,2,1,0:T(8,128)(2,1)S(1)}, bf16[1,1,2,64,1024]{4,3,2,1,0:T(8,128)(2,1)S(1)}, u32[]{:S(2)}, u32[]{:S(2)}) collective-permute-start(bf16[1,1,2,64,1024]{4,3,2,1,0:T(8,128)(2,1)S(1)} %get-tuple-element.24), channel_id=1, source_target_pairs={{4,8},{8,4},{12,16},{16,12},{20,24},{24,20},{5,9},{9,5},{13,17},{1... | collective-permute-start | bytes 786440 | tf_op jit(solution)/shard_map/ppermute | solution.py:28
  44.4 1.1 %collective-permute-start.17 = (bf16[1,1,1,64,1024]{4,3,2,1,0:T(8,128)(2,1)S(1)}, bf16[1,1,1,64,1024]{4,3,2,1,0:T(8,128)(2,1)S(1)}, u32[]{:S(2)}, u32[]{:S(2)}) collective-permute-start(bf16[1,1,1,64,1024]{4,3,2,1,0:T(8,128)(2,1)S(1)} %get-tuple-element.27), channel_id=1, source_target_pairs={{0,1},{1,2},{2,3},{3,0},{4,5},{5,6},{6,7},{7,4},{8,9},{9,10},{10,1... | collective-permute-start | bytes 393224 | tf_op jit(solution)/shard_map/ppermute | solution.py:17
  45.5 2.3 %collective-permute-start.18 = (bf16[1,1,1,64,1024]{4,3,2,1,0:T(8,128)(2,1)S(1)}, bf16[1,1,1,64,1024]{4,3,2,1,0:T(8,128)(2,1)S(1)}, u32[]{:S(2)}, u32[]{:S(2)}) collective-permute-start(bf16[1,1,1,64,1024]{4,3,2,1,0:T(8,128)(2,1)S(1)} %get-tuple-element.28), channel_id=1, source_target_pairs={{0,3},{1,0},{2,1},{3,2},{4,7},{5,4},{6,5},{7,6},{8,11},{9,8},{10,9... | collective-permute-start | bytes 393224 | tf_op jit(solution)/shard_map/ppermute | solution.py:17
  47.7 4.0 %collective-permute-start.13 = (bf16[1,1,2,64,1024]{4,3,2,1,0:T(8,128)(2,1)S(1)}, bf16[1,1,2,64,1024]{4,3,2,1,0:T(8,128)(2,1)S(1)}, u32[]{:S(2)}, u32[]{:S(2)}) collective-permute-start(bf16[1,1,2,64,1024]{4,3,2,1,0:T(8,128)(2,1)S(1)} %get-tuple-element.22), channel_id=1, source_target_pairs={{4,8},{8,4},{12,16},{16,12},{20,24},{24,20},{5,9},{9,5},{13,17},{1... | collective-permute-start | bytes 786440 | tf_op jit(solution)/shard_map/ppermute | solution.py:28
  51.7 2.7 %finish.1 = (bf16[1,2,64,1024]{3,2,1,0:T(8,128)(2,1)}, bf16[1,2,64,1024]{3,2,1,0:T(8,128)(2,1)}) custom-call(s32[2,6]{1,0:T(2,128)S(1)} %fusion.2.slots, bf16[2,12,64,1024]{3,2,1,0:T(8,128)(2,1)S(1)} %get-tuple-element.16.kv, bf16[2,2,4,384,256]{4,3,2,1,0:T(8,128)(2,1)S(1)} %get-tuple-element.17.shares), custom_call_target="tpu_custom_call" | custom-call | flops 1610612736 | bytes 3145728 | tf_op jit(solution)/shard_map/finish/pallas_call | solution.py:241
  54.8 1.5 %collective-permute-start.15 = (bf16[2,1,1,64,1024]{4,3,2,1,0:T(8,128)(2,1)S(1)}, bf16[2,1,1,64,1024]{4,3,2,1,0:T(8,128)(2,1)S(1)}, u32[]{:S(2)}, u32[]{:S(2)}) collective-permute-start(bf16[2,1,1,64,1024]{4,3,2,1,0:T(8,128)(2,1)S(1)} %pad_maximum_fusion.2), channel_id=1, source_target_pairs={{0,1},{1,2},{2,3},{3,0},{4,5},{5,6},{6,7},{7,4},{8,9},{9,10},{10,1... | collective-permute-start | bytes 786440 | tf_op jit(solution)/shard_map/ppermute | solution.py:17
  56.4 3.0 %collective-permute-start.19 = (bf16[1,1,2,64,1024]{4,3,2,1,0:T(8,128)(2,1)S(1)}, bf16[1,1,2,64,1024]{4,3,2,1,0:T(8,128)(2,1)S(1)}, u32[]{:S(2)}, u32[]{:S(2)}) collective-permute-start(bf16[1,1,2,64,1024]{4,3,2,1,0:T(8,128)(2,1)S(1)} %add_convert_fusion.1), channel_id=1, source_target_pairs={{4,8},{8,4},{12,16},{16,12},{20,24},{24,20},{5,9},{9,5},{13,17},{1... | collective-permute-start | bytes 786440 | tf_op jit(solution)/shard_map/ppermute | solution.py:28
  59.4 8.0 %collective-permute-done.16 = bf16[2,1,1,64,1024]{4,3,2,1,0:T(8,128)(2,1)S(1)} collective-permute-done((bf16[2,1,1,64,1024]{4,3,2,1,0:T(8,128)(2,1)S(1)}, bf16[2,1,1,64,1024]{4,3,2,1,0:T(8,128)(2,1)S(1)}, u32[]{:S(2)}, u32[]{:S(2)}) %collective-permute-start.16) | collective-permute-done | bytes 262176 | tf_op jit(solution)/shard_map/ppermute | solution.py:17
  (35 shorter events, 3.6 us)
Async XLA Ops:
  0.6 23.7 %collective-permute-start.1 = (bf16[2,1,2,64,1024]{4,3,2,1,0:T(8,128)(2,1)}, bf16[2,1,2,64,1024]{4,3,2,1,0:T(8,128)(2,1)S(1)}, u32[]{:S(2)}, u32[]{:S(2)}) collective-permute-start(bf16[2,1,2,64,1024]{4,3,2,1,0:T(8,128)(2,1)} %param.5), channel_id=1, source_target_pairs={{4,8},{8,4},{12,16},{16,12},{20,24},{24,20},{5,9},{9,5},{13,17},{1... | collective-permute-start | bytes 1572872 | tf_op jit(solution)/shard_map/ppermute | solution.py:28
  4.3 26.1 %collective-permute-start = (bf16[2,1,2,64,1024]{4,3,2,1,0:T(8,128)(2,1)}, bf16[2,1,2,64,1024]{4,3,2,1,0:T(8,128)(2,1)S(1)}, u32[]{:S(2)}, u32[]{:S(2)}) collective-permute-start(bf16[2,1,2,64,1024]{4,3,2,1,0:T(8,128)(2,1)} %param.5), channel_id=1, source_target_pairs={{0,4},{4,0},{8,12},{12,8},{16,20},{20,16},{24,28},{28,24},{1,5},{5... | collective-permute-start | bytes 1572872 | tf_op jit(solution)/shard_map/ppermute | solution.py:22
  5.5 18.2 %collective-permute-start.4 = (bf16[1,1,1,64,1024]{4,3,2,1,0:T(8,128)(2,1)S(1)}, bf16[1,1,1,64,1024]{4,3,2,1,0:T(8,128)(2,1)S(1)}, u32[]{:S(2)}, u32[]{:S(2)}) collective-permute-start(bf16[1,1,1,64,1024]{4,3,2,1,0:T(8,128)(2,1)S(1)} %get-tuple-element.35.lv_ref), channel_id=1, source_target_pairs={{0,1},{1,2},{2,3},{3,0},{4,5},{5,6},{6,7},{7,4},{8,9},{9,10},{10,1... | collective-permute-start | bytes 393224 | tf_op jit(solution)/shard_map/ppermute | solution.py:17
  6.9 8.0 %collective-permute-start.2 = (bf16[1,1,1,64,1024]{4,3,2,1,0:T(8,128)(2,1)S(1)}, bf16[1,1,1,64,1024]{4,3,2,1,0:T(8,128)(2,1)S(1)}, u32[]{:S(2)}, u32[]{:S(2)}) collective-permute-start(bf16[1,1,1,64,1024]{4,3,2,1,0:T(8,128)(2,1)S(1)} %get-tuple-element.37.lk_ref), channel_id=1, source_target_pairs={{0,1},{1,2},{2,3},{3,0},{4,5},{5,6},{6,7},{7,4},{8,9},{9,10},{10,1... | collective-permute-start | bytes 393224 | tf_op jit(solution)/shard_map/ppermute | solution.py:17
  8.2 10.3 %collective-permute-start.3 = (bf16[1,1,1,64,1024]{4,3,2,1,0:T(8,128)(2,1)S(1)}, bf16[1,1,1,64,1024]{4,3,2,1,0:T(8,128)(2,1)S(1)}, u32[]{:S(2)}, u32[]{:S(2)}) collective-permute-start(bf16[1,1,1,64,1024]{4,3,2,1,0:T(8,128)(2,1)S(1)} %get-tuple-element.38.fk_ref), channel_id=1, source_target_pairs={{0,3},{1,0},{2,1},{3,2},{4,7},{5,4},{6,5},{7,6},{8,11},{9,8},{10,9... | collective-permute-start | bytes 393224 | tf_op jit(solution)/shard_map/ppermute | solution.py:17
  14.9 8.9 %collective-permute-start.5 = (bf16[1,1,1,64,1024]{4,3,2,1,0:T(8,128)(2,1)S(1)}, bf16[1,1,1,64,1024]{4,3,2,1,0:T(8,128)(2,1)S(1)}, u32[]{:S(2)}, u32[]{:S(2)}) collective-permute-start(bf16[1,1,1,64,1024]{4,3,2,1,0:T(8,128)(2,1)S(1)} %get-tuple-element.36.fv_ref), channel_id=1, source_target_pairs={{0,3},{1,0},{2,1},{3,2},{4,7},{5,4},{6,5},{7,6},{8,11},{9,8},{10,9... | collective-permute-start | bytes 393224 | tf_op jit(solution)/shard_map/ppermute | solution.py:17
  18.5 11.9 %collective-permute-start.9 = (bf16[1,1,2,64,1024]{4,3,2,1,0:T(8,128)(2,1)S(1)}, bf16[1,1,2,64,1024]{4,3,2,1,0:T(8,128)(2,1)S(1)}, u32[]{:S(2)}, u32[]{:S(2)}) collective-permute-start(bf16[1,1,2,64,1024]{4,3,2,1,0:T(8,128)(2,1)S(1)} %constant_dynamic-update-slice_fusion), channel_id=1, source_target_pairs={{4,8},{8,4},{12,16},{16,12},{20,24},{24,20},{5,9},{9,5},{13,17},{1... | collective-permute-start | bytes 786440 | tf_op jit(solution)/shard_map/ppermute | solution.py:28
  23.8 6.6 %collective-permute-start.6 = (bf16[1,1,2,64,1024]{4,3,2,1,0:T(8,128)(2,1)S(1)}, bf16[1,1,2,64,1024]{4,3,2,1,0:T(8,128)(2,1)S(1)}, u32[]{:S(2)}, u32[]{:S(2)}) collective-permute-start(bf16[1,1,2,64,1024]{4,3,2,1,0:T(8,128)(2,1)S(1)} %constant_dynamic-update-slice_fusion), channel_id=1, source_target_pairs={{0,4},{4,0},{8,12},{12,8},{16,20},{20,16},{24,28},{28,24},{1,5},{5... | collective-permute-start | bytes 786440 | tf_op jit(solution)/shard_map/ppermute | solution.py:22
  23.9 1.7 %collective-permute-start.7 = (bf16[1,1,1,64,1024]{4,3,2,1,0:T(8,128)(2,1)S(1)}, bf16[1,1,1,64,1024]{4,3,2,1,0:T(8,128)(2,1)S(1)}, u32[]{:S(2)}, u32[]{:S(2)}) collective-permute-start(bf16[1,1,1,64,1024]{4,3,2,1,0:T(8,128)(2,1)S(1)} %collective-permute-done.4.wv_ref), channel_id=1, source_target_pairs={{0,4},{4,0},{8,12},{12,8},{16,20},{20,16},{24,28},{28,24},{1,5},{5... | collective-permute-start | bytes 393224 | tf_op jit(solution)/shard_map/ppermute | solution.py:22
  24.4 3.8 %collective-permute-start.8 = (bf16[1,1,1,64,1024]{4,3,2,1,0:T(8,128)(2,1)S(1)}, bf16[1,1,1,64,1024]{4,3,2,1,0:T(8,128)(2,1)S(1)}, u32[]{:S(2)}, u32[]{:S(2)}) collective-permute-start(bf16[1,1,1,64,1024]{4,3,2,1,0:T(8,128)(2,1)S(1)} %collective-permute-done.5.ev_ref), channel_id=1, source_target_pairs={{0,4},{4,0},{8,12},{12,8},{16,20},{20,16},{24,28},{28,24},{1,5},{5... | collective-permute-start | bytes 393224 | tf_op jit(solution)/shard_map/ppermute | solution.py:22
  25.6 5.2 %collective-permute-start.11 = (bf16[1,1,1,64,1024]{4,3,2,1,0:T(8,128)(2,1)S(1)}, bf16[1,1,1,64,1024]{4,3,2,1,0:T(8,128)(2,1)S(1)}, u32[]{:S(2)}, u32[]{:S(2)}) collective-permute-start(bf16[1,1,1,64,1024]{4,3,2,1,0:T(8,128)(2,1)S(1)} %get-tuple-element.33), channel_id=1, source_target_pairs={{0,3},{1,0},{2,1},{3,2},{4,7},{5,4},{6,5},{7,6},{8,11},{9,8},{10,9... | collective-permute-start | bytes 393224 | tf_op jit(solution)/shard_map/ppermute | solution.py:17
  28.2 6.2 %collective-permute-start.10 = (bf16[1,1,1,64,1024]{4,3,2,1,0:T(8,128)(2,1)S(1)}, bf16[1,1,1,64,1024]{4,3,2,1,0:T(8,128)(2,1)S(1)}, u32[]{:S(2)}, u32[]{:S(2)}) collective-permute-start(bf16[1,1,1,64,1024]{4,3,2,1,0:T(8,128)(2,1)S(1)} %get-tuple-element.34), channel_id=1, source_target_pairs={{0,1},{1,2},{2,3},{3,0},{4,5},{5,6},{6,7},{7,4},{8,9},{9,10},{10,1... | collective-permute-start | bytes 393224 | tf_op jit(solution)/shard_map/ppermute | solution.py:17
  39.8 14.6 %collective-permute-start.12 = (bf16[2,1,4,64,1024]{4,3,2,1,0:T(8,128)(2,1)S(1)}, bf16[2,1,4,64,1024]{4,3,2,1,0:T(8,128)(2,1)S(1)}, u32[]{:S(2)}, u32[]{:S(2)}) collective-permute-start(bf16[2,1,4,64,1024]{4,3,2,1,0:T(8,128)(2,1)S(1)} %get-tuple-element.21), channel_id=1, source_target_pairs={{0,4},{4,0},{8,12},{12,8},{16,20},{20,16},{24,28},{28,24},{1,5},{5... | collective-permute-start | bytes 3145736 | tf_op jit(solution)/shard_map/ppermute | solution.py:22
  41.4 13.0 %collective-permute-start.14 = (bf16[1,1,2,64,1024]{4,3,2,1,0:T(8,128)(2,1)S(1)}, bf16[1,1,2,64,1024]{4,3,2,1,0:T(8,128)(2,1)S(1)}, u32[]{:S(2)}, u32[]{:S(2)}) collective-permute-start(bf16[1,1,2,64,1024]{4,3,2,1,0:T(8,128)(2,1)S(1)} %get-tuple-element.24), channel_id=1, source_target_pairs={{4,8},{8,4},{12,16},{16,12},{20,24},{24,20},{5,9},{9,5},{13,17},{1... | collective-permute-start | bytes 786440 | tf_op jit(solution)/shard_map/ppermute | solution.py:28
  44.4 11.9 %collective-permute-start.17 = (bf16[1,1,1,64,1024]{4,3,2,1,0:T(8,128)(2,1)S(1)}, bf16[1,1,1,64,1024]{4,3,2,1,0:T(8,128)(2,1)S(1)}, u32[]{:S(2)}, u32[]{:S(2)}) collective-permute-start(bf16[1,1,1,64,1024]{4,3,2,1,0:T(8,128)(2,1)S(1)} %get-tuple-element.27), channel_id=1, source_target_pairs={{0,1},{1,2},{2,3},{3,0},{4,5},{5,6},{6,7},{7,4},{8,9},{9,10},{10,1... | collective-permute-start | bytes 393224 | tf_op jit(solution)/shard_map/ppermute | solution.py:17
  45.5 10.8 %collective-permute-start.18 = (bf16[1,1,1,64,1024]{4,3,2,1,0:T(8,128)(2,1)S(1)}, bf16[1,1,1,64,1024]{4,3,2,1,0:T(8,128)(2,1)S(1)}, u32[]{:S(2)}, u32[]{:S(2)}) collective-permute-start(bf16[1,1,1,64,1024]{4,3,2,1,0:T(8,128)(2,1)S(1)} %get-tuple-element.28), channel_id=1, source_target_pairs={{0,3},{1,0},{2,1},{3,2},{4,7},{5,4},{6,5},{7,6},{8,11},{9,8},{10,9... | collective-permute-start | bytes 393224 | tf_op jit(solution)/shard_map/ppermute | solution.py:17
  47.7 19.8 %collective-permute-start.13 = (bf16[1,1,2,64,1024]{4,3,2,1,0:T(8,128)(2,1)S(1)}, bf16[1,1,2,64,1024]{4,3,2,1,0:T(8,128)(2,1)S(1)}, u32[]{:S(2)}, u32[]{:S(2)}) collective-permute-start(bf16[1,1,2,64,1024]{4,3,2,1,0:T(8,128)(2,1)S(1)} %get-tuple-element.22), channel_id=1, source_target_pairs={{4,8},{8,4},{12,16},{16,12},{20,24},{24,20},{5,9},{9,5},{13,17},{1... | collective-permute-start | bytes 786440 | tf_op jit(solution)/shard_map/ppermute | solution.py:28
  54.7 12.7 %collective-permute-start.16 = (bf16[2,1,1,64,1024]{4,3,2,1,0:T(8,128)(2,1)S(1)}, bf16[2,1,1,64,1024]{4,3,2,1,0:T(8,128)(2,1)S(1)}, u32[]{:S(2)}, u32[]{:S(2)}) collective-permute-start(bf16[2,1,1,64,1024]{4,3,2,1,0:T(8,128)(2,1)S(1)} %pad_maximum_fusion.3), channel_id=1, source_target_pairs={{0,3},{1,0},{2,1},{3,2},{4,7},{5,4},{6,5},{7,6},{8,11},{9,8},{10,9... | collective-permute-start | bytes 786440 | tf_op jit(solution)/shard_map/ppermute | solution.py:17
  54.8 12.6 %collective-permute-start.15 = (bf16[2,1,1,64,1024]{4,3,2,1,0:T(8,128)(2,1)S(1)}, bf16[2,1,1,64,1024]{4,3,2,1,0:T(8,128)(2,1)S(1)}, u32[]{:S(2)}, u32[]{:S(2)}) collective-permute-start(bf16[2,1,1,64,1024]{4,3,2,1,0:T(8,128)(2,1)S(1)} %pad_maximum_fusion.2), channel_id=1, source_target_pairs={{0,1},{1,2},{2,3},{3,0},{4,5},{5,6},{6,7},{7,4},{8,9},{9,10},{10,1... | collective-permute-start | bytes 786440 | tf_op jit(solution)/shard_map/ppermute | solution.py:17
  56.4 11.1 %collective-permute-start.19 = (bf16[1,1,2,64,1024]{4,3,2,1,0:T(8,128)(2,1)S(1)}, bf16[1,1,2,64,1024]{4,3,2,1,0:T(8,128)(2,1)S(1)}, u32[]{:S(2)}, u32[]{:S(2)}) collective-permute-start(bf16[1,1,2,64,1024]{4,3,2,1,0:T(8,128)(2,1)S(1)} %add_convert_fusion.1), channel_id=1, source_target_pairs={{4,8},{8,4},{12,16},{16,12},{20,24},{24,20},{5,9},{9,5},{13,17},{1... | collective-permute-start | bytes 786440 | tf_op jit(solution)/shard_map/ppermute | solution.py:28

commit v6 on v5

--- a/solution.py
+++ b/solution.py
@@ -328,25 +328,18 @@
     to_west = jnp.concatenate([side_k[:, :, 1:], side_v[:, :, 1:]], axis=0)
     from_east = lon_shift(to_east, -1)
     from_west = lon_shift(to_west, 1)
-    from_east_k, from_east_v = from_east[:1], from_east[1:]
-    from_west_k, from_west_v = from_west[:1], from_west[1:]
     near_v = (near_v + edges(from_e.astype(full), from_w.astype(full), cols)).astype(low)
     from_inter_v = inter_swap(near_v)
 
     grad_queries, attended = finish(slots, kv, shares, queries)
 
-    def total(part, inter, first, last):
-        piece = own[part : part + 1] + from_intra[part : part + 1, :, :cols].astype(full)
-        piece = piece + inter.astype(full) + edges(first.astype(full), last.astype(full), cols)
-        return piece.astype(low)
-
-    grads = jnp.concatenate(
-        [
-            total(0, from_inter_k, from_west_k, from_east_k),
-            total(1, from_inter_v, from_west_v, from_east_v),
-        ],
-        axis=0,
-    )
+    still = ((0, 0, 0),) * 4
+    zero = jnp.zeros((), full)
+    grads = own + from_intra[:, :, :cols].astype(full)
+    grads = grads + lax.pad(from_inter_k.astype(full), zero, ((0, 1, 0),) + still)
+    grads = grads + lax.pad(from_inter_v.astype(full), zero, ((1, 0, 0),) + still)
+    grads = grads + edges(from_west.astype(full), from_east.astype(full), cols)
+    grads = grads.astype(low)
     return (attended, grad_queries, grads)
 
 

time: 69.1 us -> 69.8 us (1.010)
  waiting for transfers between devices: 20.1 us -> 21.1 us
    ppermute x5, waiting for transfers between devices: 1.07 us -> 8.11 us  [inter_swap(): lax.ppermute(value, 'lat', [(i, j) for i, j in pairs if 0 <= j < count])]
    ppermute x10, waiting for transfers between devices: 18 us -> 11.9 us  [lon_shift(): lax.ppermute(value, 'lon', [(i, (i + steps) % count) for i in range(count)])]
    concatenate x1 -> x0, other arithmetic: 0.84 us -> none  [body(): jnp.concatenate([total(0, from_inter_k, from_west_k, from_east_k), total(...]
    convert_element_type x1, other arithmetic: 0.34 us -> 1.13 us  [body(): grads = grads.astype(low)]
  transfers between devices with their start and end apart: 20 -> 20, of which waited for: 7 -> 10; matrix products, arithmetic and copies ran while one was open for 5% -> 5% of each run, Pallas kernels for 4% -> 4%
where the time goes in v6:
time: 69.8 us; the launch traced here: 69.5 us
  starting transfers between devices  34.9 us (50%)
  waiting for transfers between devices  21.1 us (30%)
  Pallas kernels  8.11 us (12%)
  other arithmetic  3.3 us (5%)
  local copies, waits for them, and re-layouts  1.3 us (2%)
  between operations  0.81 us (1%)
    ppermute x5, starting transfers between devices, inter_swap(): lax.ppermute(value, 'lat', [(i, j) for i, j in pairs if 0 <= j < count])  19 us
    ppermute x10, starting transfers between devices, lon_shift(): lax.ppermute(value, 'lon', [(i, (i + steps) % count) for i in range(count)])  13.6 us
    ppermute x10, waiting for transfers between devices, lon_shift(): lax.ppermute(value, 'lon', [(i, (i + steps) % count) for i in range(count)])  11.9 us
    ppermute x5, waiting for transfers between devices, inter_swap(): lax.ppermute(value, 'lat', [(i, j) for i, j in pairs if 0 <= j < count])  8.11 us
    pallas_call x1, Pallas kernels, attention(): pl.pallas_call(attention_kernel, out_shape=outs, in_specs=[scalar] * 2 +...  5.41 us
    pallas_call x1, Pallas kernels, finish(): pl.pallas_call(finish_kernel, out_shape=[shape, shape], in_specs=[scalar,...  2.69 us
    ppermute x5, starting transfers between devices, intra_swap(): lax.ppermute(value, 'lat', [(i, i ^ 1) for i in range(count) if i ^ 1 < c...  2.28 us
  transfers between devices with their start and end apart: 20, of which 10 were waited for; matrix products, arithmetic and copies ran while one was open for 5% of the time, Pallas kernels for 4%

profile of v6, /device:TPU:3, one launch (start us, length us, event | category | flops | bytes accessed | tf_op | source)
XLA Modules:
  0.0 69.5 jit_solution(1966399241714984144)
XLA Ops:
  0.6 3.7 %collective-permute-start.1 = (bf16[2,1,2,64,1024]{4,3,2,1,0:T(8,128)(2,1)}, bf16[2,1,2,64,1024]{4,3,2,1,0:T(8,128)(2,1)S(1)}, u32[]{:S(2)}, u32[]{:S(2)}) collective-permute-start(bf16[2,1,2,64,1024]{4,3,2,1,0:T(8,128)(2,1)} %param.5), channel_id=1, source_target_pairs={{4,8},{8,4},{12,16},{16,12},{20,24},{24,20},{5,9},{9,5},{13,17},{1... | collective-permute-start | bytes 1572872 | tf_op jit(solution)/shard_map/ppermute | solution.py:28
  4.4 1.1 %fusion.6 = (bf16[1,1,1,64,1024]{4,3,2,1,0:T(8,128)(2,1)S(1)}, bf16[1,1,1,64,1024]{4,3,2,1,0:T(8,128)(2,1)S(1)}, bf16[1,1,1,64,1024]{4,3,2,1,0:T(8,128)(2,1)S(1)}, bf16[1,1,1,64,1024]{4,3,2,1,0:T(8,128)(2,1)S(1)}) fusion(bf16[2,1,2,64,1024]{4,3,2,1,0:T(8,128)(2,1)} %param.5), kind=kLoop, calls=%fused_computation.30 | loop fusion | bytes 1048576 | tf_op jit(solution)/shard_map/slice | solution.py:302
  5.5 1.3 %collective-permute-start.4 = (bf16[1,1,1,64,1024]{4,3,2,1,0:T(8,128)(2,1)S(1)}, bf16[1,1,1,64,1024]{4,3,2,1,0:T(8,128)(2,1)S(1)}, u32[]{:S(2)}, u32[]{:S(2)}) collective-permute-start(bf16[1,1,1,64,1024]{4,3,2,1,0:T(8,128)(2,1)S(1)} %get-tuple-element.33.lv_ref), channel_id=1, source_target_pairs={{0,1},{1,2},{2,3},{3,0},{4,5},{5,6},{6,7},{7,4},{8,9},{9,10},{10,1... | collective-permute-start | bytes 393224 | tf_op jit(solution)/shard_map/ppermute | solution.py:17
  6.9 1.3 %collective-permute-start.2 = (bf16[1,1,1,64,1024]{4,3,2,1,0:T(8,128)(2,1)S(1)}, bf16[1,1,1,64,1024]{4,3,2,1,0:T(8,128)(2,1)S(1)}, u32[]{:S(2)}, u32[]{:S(2)}) collective-permute-start(bf16[1,1,1,64,1024]{4,3,2,1,0:T(8,128)(2,1)S(1)} %get-tuple-element.35.lk_ref), channel_id=1, source_target_pairs={{0,1},{1,2},{2,3},{3,0},{4,5},{5,6},{6,7},{7,4},{8,9},{9,10},{10,1... | collective-permute-start | bytes 393224 | tf_op jit(solution)/shard_map/ppermute | solution.py:17
  8.2 2.0 %collective-permute-start.3 = (bf16[1,1,1,64,1024]{4,3,2,1,0:T(8,128)(2,1)S(1)}, bf16[1,1,1,64,1024]{4,3,2,1,0:T(8,128)(2,1)S(1)}, u32[]{:S(2)}, u32[]{:S(2)}) collective-permute-start(bf16[1,1,1,64,1024]{4,3,2,1,0:T(8,128)(2,1)S(1)} %get-tuple-element.36.fk_ref), channel_id=1, source_target_pairs={{0,3},{1,0},{2,1},{3,2},{4,7},{5,4},{6,5},{7,6},{8,11},{9,8},{10,9... | collective-permute-start | bytes 393224 | tf_op jit(solution)/shard_map/ppermute | solution.py:17
  10.9 4.0 %collective-permute-done.2.wk_ref = bf16[1,1,1,64,1024]{4,3,2,1,0:T(8,128)(2,1)S(1)} collective-permute-done((bf16[1,1,1,64,1024]{4,3,2,1,0:T(8,128)(2,1)S(1)}, bf16[1,1,1,64,1024]{4,3,2,1,0:T(8,128)(2,1)S(1)}, u32[]{:S(2)}, u32[]{:S(2)}) %collective-permute-start.2) | collective-permute-done | bytes 131104 | tf_op jit(solution)/shard_map/ppermute | solution.py:17
  14.9 1.6 %collective-permute-start.5 = (bf16[1,1,1,64,1024]{4,3,2,1,0:T(8,128)(2,1)S(1)}, bf16[1,1,1,64,1024]{4,3,2,1,0:T(8,128)(2,1)S(1)}, u32[]{:S(2)}, u32[]{:S(2)}) collective-permute-start(bf16[1,1,1,64,1024]{4,3,2,1,0:T(8,128)(2,1)S(1)} %get-tuple-element.34.fv_ref), channel_id=1, source_target_pairs={{0,3},{1,0},{2,1},{3,2},{4,7},{5,4},{6,5},{7,6},{8,11},{9,8},{10,9... | collective-permute-start | bytes 393224 | tf_op jit(solution)/shard_map/ppermute | solution.py:17
  16.5 2.0 %collective-permute-done.3.ek_ref = bf16[1,1,1,64,1024]{4,3,2,1,0:T(8,128)(2,1)S(1)} collective-permute-done((bf16[1,1,1,64,1024]{4,3,2,1,0:T(8,128)(2,1)S(1)}, bf16[1,1,1,64,1024]{4,3,2,1,0:T(8,128)(2,1)S(1)}, u32[]{:S(2)}, u32[]{:S(2)}) %collective-permute-start.3) | collective-permute-done | bytes 131104 | tf_op jit(solution)/shard_map/ppermute | solution.py:17
  18.5 5.3 %collective-permute-start.9 = (bf16[1,1,2,64,1024]{4,3,2,1,0:T(8,128)(2,1)S(1)}, bf16[1,1,2,64,1024]{4,3,2,1,0:T(8,128)(2,1)S(1)}, u32[]{:S(2)}, u32[]{:S(2)}) collective-permute-start(bf16[1,1,2,64,1024]{4,3,2,1,0:T(8,128)(2,1)S(1)} %constant_dynamic-update-slice_fusion), channel_id=1, source_target_pairs={{4,8},{8,4},{12,16},{16,12},{20,24},{24,20},{5,9},{9,5},{13,17},{1... | collective-permute-start | bytes 786440 | tf_op jit(solution)/shard_map/ppermute | solution.py:28
  24.5 1.1 %collective-permute-done.7.sw_ref = bf16[1,1,1,64,1024]{4,3,2,1,0:T(8,128)(2,1)S(1)} collective-permute-done((bf16[1,1,1,64,1024]{4,3,2,1,0:T(8,128)(2,1)S(1)}, bf16[1,1,1,64,1024]{4,3,2,1,0:T(8,128)(2,1)S(1)}, u32[]{:S(2)}, u32[]{:S(2)}) %collective-permute-start.7) | collective-permute-done | bytes 131104 | tf_op jit(solution)/shard_map/ppermute | solution.py:22
  25.6 2.6 %collective-permute-start.11 = (bf16[1,1,1,64,1024]{4,3,2,1,0:T(8,128)(2,1)S(1)}, bf16[1,1,1,64,1024]{4,3,2,1,0:T(8,128)(2,1)S(1)}, u32[]{:S(2)}, u32[]{:S(2)}) collective-permute-start(bf16[1,1,1,64,1024]{4,3,2,1,0:T(8,128)(2,1)S(1)} %get-tuple-element.31), channel_id=1, source_target_pairs={{0,3},{1,0},{2,1},{3,2},{4,7},{5,4},{6,5},{7,6},{8,11},{9,8},{10,9... | collective-permute-start | bytes 393224 | tf_op jit(solution)/shard_map/ppermute | solution.py:17
  30.7 3.7 %collective-permute-done.10.cw_ref = bf16[1,1,1,64,1024]{4,3,2,1,0:T(8,128)(2,1)S(1)} collective-permute-done((bf16[1,1,1,64,1024]{4,3,2,1,0:T(8,128)(2,1)S(1)}, bf16[1,1,1,64,1024]{4,3,2,1,0:T(8,128)(2,1)S(1)}, u32[]{:S(2)}, u32[]{:S(2)}) %collective-permute-start.10) | collective-permute-done | bytes 131104 | tf_op jit(solution)/shard_map/ppermute | solution.py:17
  34.4 5.4 %attention.1 = (bf16[2,12,64,1024]{3,2,1,0:T(8,128)(2,1)S(1)}, bf16[2,2,4,384,256]{4,3,2,1,0:T(8,128)(2,1)S(1)}, f32[2,1,2,64,1024]{4,3,2,1,0:T(8,128)S(1)}, f32...) custom-call(s32[2,6]{1,0:T(2,128)S(1)} %fusion.2.slots, ...), custom_call_target="tpu_custom_call" | custom-call | flops 1610612736 | bytes 14417920 | tf_op jit(solution)/shard_map/attention/pallas_call | solution.py:203
  39.8 1.6 %collective-permute-start.12 = (bf16[2,1,4,64,1024]{4,3,2,1,0:T(8,128)(2,1)S(1)}, bf16[2,1,4,64,1024]{4,3,2,1,0:T(8,128)(2,1)S(1)}, u32[]{:S(2)}, u32[]{:S(2)}) collective-permute-start(bf16[2,1,4,64,1024]{4,3,2,1,0:T(8,128)(2,1)S(1)} %get-tuple-element.21), channel_id=1, source_target_pairs={{0,4},{4,0},{8,12},{12,8},{16,20},{20,16},{24,28},{28,24},{1,5},{5... | collective-permute-start | bytes 3145736 | tf_op jit(solution)/shard_map/ppermute | solution.py:22
  42.4 2.2 %collective-permute-start.15 = (bf16[1,1,1,64,1024]{4,3,2,1,0:T(8,128)(2,1)S(1)}, bf16[1,1,1,64,1024]{4,3,2,1,0:T(8,128)(2,1)S(1)}, u32[]{:S(2)}, u32[]{:S(2)}) collective-permute-start(bf16[1,1,1,64,1024]{4,3,2,1,0:T(8,128)(2,1)S(1)} %get-tuple-element.25), channel_id=1, source_target_pairs={{0,3},{1,0},{2,1},{3,2},{4,7},{5,4},{6,5},{7,6},{8,11},{9,8},{10,9... | collective-permute-start | bytes 393224 | tf_op jit(solution)/shard_map/ppermute | solution.py:17
  44.7 3.6 %collective-permute-start.17 = (bf16[1,1,2,64,1024]{4,3,2,1,0:T(8,128)(2,1)S(1)}, bf16[1,1,2,64,1024]{4,3,2,1,0:T(8,128)(2,1)S(1)}, u32[]{:S(2)}, u32[]{:S(2)}) collective-permute-start(bf16[1,1,2,64,1024]{4,3,2,1,0:T(8,128)(2,1)S(1)} %get-tuple-element.27), channel_id=1, source_target_pairs={{4,8},{8,4},{12,16},{16,12},{20,24},{24,20},{5,9},{9,5},{13,17},{1... | collective-permute-start | bytes 786440 | tf_op jit(solution)/shard_map/ppermute | solution.py:28
  48.3 2.8 %collective-permute-start.13 = (bf16[1,1,2,64,1024]{4,3,2,1,0:T(8,128)(2,1)S(1)}, bf16[1,1,2,64,1024]{4,3,2,1,0:T(8,128)(2,1)S(1)}, u32[]{:S(2)}, u32[]{:S(2)}) collective-permute-start(bf16[1,1,2,64,1024]{4,3,2,1,0:T(8,128)(2,1)S(1)} %get-tuple-element.22), channel_id=1, source_target_pairs={{4,8},{8,4},{12,16},{16,12},{20,24},{24,20},{5,9},{9,5},{13,17},{1... | collective-permute-start | bytes 786440 | tf_op jit(solution)/shard_map/ppermute | solution.py:28
  51.2 3.6 %collective-permute-start.16 = (bf16[1,1,2,64,1024]{4,3,2,1,0:T(8,128)(2,1)S(1)}, bf16[1,1,2,64,1024]{4,3,2,1,0:T(8,128)(2,1)S(1)}, u32[]{:S(2)}, u32[]{:S(2)}) collective-permute-start(bf16[1,1,2,64,1024]{4,3,2,1,0:T(8,128)(2,1)S(1)} %add_convert_fusion.3), channel_id=1, source_target_pairs={{4,8},{8,4},{12,16},{16,12},{20,24},{24,20},{5,9},{9,5},{13,17},{1... | collective-permute-start | bytes 786440 | tf_op jit(solution)/shard_map/ppermute | solution.py:28
  54.8 1.2 %collective-permute-done.17 = bf16[1,1,2,64,1024]{4,3,2,1,0:T(8,128)(2,1)S(1)} collective-permute-done((bf16[1,1,2,64,1024]{4,3,2,1,0:T(8,128)(2,1)S(1)}, bf16[1,1,2,64,1024]{4,3,2,1,0:T(8,128)(2,1)S(1)}, u32[]{:S(2)}, u32[]{:S(2)}) %collective-permute-start.17) | collective-permute-done | bytes 262176 | tf_op jit(solution)/shard_map/ppermute | solution.py:28
  56.4 1.5 %collective-permute-start.18 = (bf16[2,1,1,64,1024]{4,3,2,1,0:T(8,128)(2,1)S(1)}, bf16[2,1,1,64,1024]{4,3,2,1,0:T(8,128)(2,1)S(1)}, u32[]{:S(2)}, u32[]{:S(2)}) collective-permute-start(bf16[2,1,1,64,1024]{4,3,2,1,0:T(8,128)(2,1)S(1)} %pad_maximum_fusion.1), channel_id=1, source_target_pairs={{0,1},{1,2},{2,3},{3,0},{4,5},{5,6},{6,7},{7,4},{8,9},{9,10},{10,1... | collective-permute-start | bytes 786440 | tf_op jit(solution)/shard_map/ppermute | solution.py:17
  57.9 2.7 %finish.1 = (bf16[1,2,64,1024]{3,2,1,0:T(8,128)(2,1)}, bf16[1,2,64,1024]{3,2,1,0:T(8,128)(2,1)}) custom-call(s32[2,6]{1,0:T(2,128)S(1)} %fusion.2.slots, bf16[2,12,64,1024]{3,2,1,0:T(8,128)(2,1)S(1)} %get-tuple-element.16.kv, bf16[2,2,4,384,256]{4,3,2,1,0:T(8,128)(2,1)S(1)} %get-tuple-element.17.shares), custom_call_target="tpu_custom_call" | custom-call | flops 1610612736 | bytes 3145728 | tf_op jit(solution)/shard_map/finish/pallas_call | solution.py:241
  61.7 4.8 %collective-permute-done.16 = bf16[1,1,2,64,1024]{4,3,2,1,0:T(8,128)(2,1)S(1)} collective-permute-done((bf16[1,1,2,64,1024]{4,3,2,1,0:T(8,128)(2,1)S(1)}, bf16[1,1,2,64,1024]{4,3,2,1,0:T(8,128)(2,1)S(1)}, u32[]{:S(2)}, u32[]{:S(2)}) %collective-permute-start.16) | collective-permute-done | bytes 262176 | tf_op jit(solution)/shard_map/ppermute | solution.py:28
  66.5 1.9 %collective-permute-done.18 = bf16[2,1,1,64,1024]{4,3,2,1,0:T(8,128)(2,1)S(1)} collective-permute-done((bf16[2,1,1,64,1024]{4,3,2,1,0:T(8,128)(2,1)S(1)}, bf16[2,1,1,64,1024]{4,3,2,1,0:T(8,128)(2,1)S(1)}, u32[]{:S(2)}, u32[]{:S(2)}) %collective-permute-start.18) | collective-permute-done | bytes 262176 | tf_op jit(solution)/shard_map/ppermute | solution.py:17
  68.4 1.1 %add_convert_fusion = bf16[2,1,2,64,1024]{4,3,2,1,0:T(8,128)(2,1)} fusion(f32[2,1,2,64,1024]{4,3,2,1,0:T(8,128)S(1)} %get-tuple-element.20, bf16[2,1,4,64,1024]{4,3,2,1,0:T(8,128)(2,1)S(1)} %collective-permute-done.12, bf16[2,1,1,64,1024]{4,3,2,1,0:T(8,128)(2,1)S(1)} %collective-permute-done.19, bf16[2,1,1,64,1024]{4,3,2,1,0:T(8,128)(2,1)S(1)} %collective-permute-done.18, ...), kind=kLoop, calls=%fused_computation | loop fusion | flops 2883584 | bytes 3145728 | tf_op jit(solution)/shard_map/convert_element_type | solution.py:342
  (32 shorter events, 6.6 us)
Async XLA Ops:
  0.6 23.7 %collective-permute-start.1 = (bf16[2,1,2,64,1024]{4,3,2,1,0:T(8,128)(2,1)}, bf16[2,1,2,64,1024]{4,3,2,1,0:T(8,128)(2,1)S(1)}, u32[]{:S(2)}, u32[]{:S(2)}) collective-permute-start(bf16[2,1,2,64,1024]{4,3,2,1,0:T(8,128)(2,1)} %param.5), channel_id=1, source_target_pairs={{4,8},{8,4},{12,16},{16,12},{20,24},{24,20},{5,9},{9,5},{13,17},{1... | collective-permute-start | bytes 1572872 | tf_op jit(solution)/shard_map/ppermute | solution.py:28
  4.3 26.1 %collective-permute-start = (bf16[2,1,2,64,1024]{4,3,2,1,0:T(8,128)(2,1)}, bf16[2,1,2,64,1024]{4,3,2,1,0:T(8,128)(2,1)S(1)}, u32[]{:S(2)}, u32[]{:S(2)}) collective-permute-start(bf16[2,1,2,64,1024]{4,3,2,1,0:T(8,128)(2,1)} %param.5), channel_id=1, source_target_pairs={{0,4},{4,0},{8,12},{12,8},{16,20},{20,16},{24,28},{28,24},{1,5},{5... | collective-permute-start | bytes 1572872 | tf_op jit(solution)/shard_map/ppermute | solution.py:22
  5.5 18.2 %collective-permute-start.4 = (bf16[1,1,1,64,1024]{4,3,2,1,0:T(8,128)(2,1)S(1)}, bf16[1,1,1,64,1024]{4,3,2,1,0:T(8,128)(2,1)S(1)}, u32[]{:S(2)}, u32[]{:S(2)}) collective-permute-start(bf16[1,1,1,64,1024]{4,3,2,1,0:T(8,128)(2,1)S(1)} %get-tuple-element.33.lv_ref), channel_id=1, source_target_pairs={{0,1},{1,2},{2,3},{3,0},{4,5},{5,6},{6,7},{7,4},{8,9},{9,10},{10,1... | collective-permute-start | bytes 393224 | tf_op jit(solution)/shard_map/ppermute | solution.py:17
  6.9 8.0 %collective-permute-start.2 = (bf16[1,1,1,64,1024]{4,3,2,1,0:T(8,128)(2,1)S(1)}, bf16[1,1,1,64,1024]{4,3,2,1,0:T(8,128)(2,1)S(1)}, u32[]{:S(2)}, u32[]{:S(2)}) collective-permute-start(bf16[1,1,1,64,1024]{4,3,2,1,0:T(8,128)(2,1)S(1)} %get-tuple-element.35.lk_ref), channel_id=1, source_target_pairs={{0,1},{1,2},{2,3},{3,0},{4,5},{5,6},{6,7},{7,4},{8,9},{9,10},{10,1... | collective-permute-start | bytes 393224 | tf_op jit(solution)/shard_map/ppermute | solution.py:17
  8.2 10.3 %collective-permute-start.3 = (bf16[1,1,1,64,1024]{4,3,2,1,0:T(8,128)(2,1)S(1)}, bf16[1,1,1,64,1024]{4,3,2,1,0:T(8,128)(2,1)S(1)}, u32[]{:S(2)}, u32[]{:S(2)}) collective-permute-start(bf16[1,1,1,64,1024]{4,3,2,1,0:T(8,128)(2,1)S(1)} %get-tuple-element.36.fk_ref), channel_id=1, source_target_pairs={{0,3},{1,0},{2,1},{3,2},{4,7},{5,4},{6,5},{7,6},{8,11},{9,8},{10,9... | collective-permute-start | bytes 393224 | tf_op jit(solution)/shard_map/ppermute | solution.py:17
  14.9 8.9 %collective-permute-start.5 = (bf16[1,1,1,64,1024]{4,3,2,1,0:T(8,128)(2,1)S(1)}, bf16[1,1,1,64,1024]{4,3,2,1,0:T(8,128)(2,1)S(1)}, u32[]{:S(2)}, u32[]{:S(2)}) collective-permute-start(bf16[1,1,1,64,1024]{4,3,2,1,0:T(8,128)(2,1)S(1)} %get-tuple-element.34.fv_ref), channel_id=1, source_target_pairs={{0,3},{1,0},{2,1},{3,2},{4,7},{5,4},{6,5},{7,6},{8,11},{9,8},{10,9... | collective-permute-start | bytes 393224 | tf_op jit(solution)/shard_map/ppermute | solution.py:17
  18.5 11.9 %collective-permute-start.9 = (bf16[1,1,2,64,1024]{4,3,2,1,0:T(8,128)(2,1)S(1)}, bf16[1,1,2,64,1024]{4,3,2,1,0:T(8,128)(2,1)S(1)}, u32[]{:S(2)}, u32[]{:S(2)}) collective-permute-start(bf16[1,1,2,64,1024]{4,3,2,1,0:T(8,128)(2,1)S(1)} %constant_dynamic-update-slice_fusion), channel_id=1, source_target_pairs={{4,8},{8,4},{12,16},{16,12},{20,24},{24,20},{5,9},{9,5},{13,17},{1... | collective-permute-start | bytes 786440 | tf_op jit(solution)/shard_map/ppermute | solution.py:28
  23.8 6.6 %collective-permute-start.6 = (bf16[1,1,2,64,1024]{4,3,2,1,0:T(8,128)(2,1)S(1)}, bf16[1,1,2,64,1024]{4,3,2,1,0:T(8,128)(2,1)S(1)}, u32[]{:S(2)}, u32[]{:S(2)}) collective-permute-start(bf16[1,1,2,64,1024]{4,3,2,1,0:T(8,128)(2,1)S(1)} %constant_dynamic-update-slice_fusion), channel_id=1, source_target_pairs={{0,4},{4,0},{8,12},{12,8},{16,20},{20,16},{24,28},{28,24},{1,5},{5... | collective-permute-start | bytes 786440 | tf_op jit(solution)/shard_map/ppermute | solution.py:22
  23.9 1.7 %collective-permute-start.7 = (bf16[1,1,1,64,1024]{4,3,2,1,0:T(8,128)(2,1)S(1)}, bf16[1,1,1,64,1024]{4,3,2,1,0:T(8,128)(2,1)S(1)}, u32[]{:S(2)}, u32[]{:S(2)}) collective-permute-start(bf16[1,1,1,64,1024]{4,3,2,1,0:T(8,128)(2,1)S(1)} %collective-permute-done.4.wv_ref), channel_id=1, source_target_pairs={{0,4},{4,0},{8,12},{12,8},{16,20},{20,16},{24,28},{28,24},{1,5},{5... | collective-permute-start | bytes 393224 | tf_op jit(solution)/shard_map/ppermute | solution.py:22
  24.4 3.8 %collective-permute-start.8 = (bf16[1,1,1,64,1024]{4,3,2,1,0:T(8,128)(2,1)S(1)}, bf16[1,1,1,64,1024]{4,3,2,1,0:T(8,128)(2,1)S(1)}, u32[]{:S(2)}, u32[]{:S(2)}) collective-permute-start(bf16[1,1,1,64,1024]{4,3,2,1,0:T(8,128)(2,1)S(1)} %collective-permute-done.5.ev_ref), channel_id=1, source_target_pairs={{0,4},{4,0},{8,12},{12,8},{16,20},{20,16},{24,28},{28,24},{1,5},{5... | collective-permute-start | bytes 393224 | tf_op jit(solution)/shard_map/ppermute | solution.py:22
  25.6 5.2 %collective-permute-start.11 = (bf16[1,1,1,64,1024]{4,3,2,1,0:T(8,128)(2,1)S(1)}, bf16[1,1,1,64,1024]{4,3,2,1,0:T(8,128)(2,1)S(1)}, u32[]{:S(2)}, u32[]{:S(2)}) collective-permute-start(bf16[1,1,1,64,1024]{4,3,2,1,0:T(8,128)(2,1)S(1)} %get-tuple-element.31), channel_id=1, source_target_pairs={{0,3},{1,0},{2,1},{3,2},{4,7},{5,4},{6,5},{7,6},{8,11},{9,8},{10,9... | collective-permute-start | bytes 393224 | tf_op jit(solution)/shard_map/ppermute | solution.py:17
  28.2 6.2 %collective-permute-start.10 = (bf16[1,1,1,64,1024]{4,3,2,1,0:T(8,128)(2,1)S(1)}, bf16[1,1,1,64,1024]{4,3,2,1,0:T(8,128)(2,1)S(1)}, u32[]{:S(2)}, u32[]{:S(2)}) collective-permute-start(bf16[1,1,1,64,1024]{4,3,2,1,0:T(8,128)(2,1)S(1)} %get-tuple-element.32), channel_id=1, source_target_pairs={{0,1},{1,2},{2,3},{3,0},{4,5},{5,6},{6,7},{7,4},{8,9},{9,10},{10,1... | collective-permute-start | bytes 393224 | tf_op jit(solution)/shard_map/ppermute | solution.py:17
  39.8 16.2 %collective-permute-start.12 = (bf16[2,1,4,64,1024]{4,3,2,1,0:T(8,128)(2,1)S(1)}, bf16[2,1,4,64,1024]{4,3,2,1,0:T(8,128)(2,1)S(1)}, u32[]{:S(2)}, u32[]{:S(2)}) collective-permute-start(bf16[2,1,4,64,1024]{4,3,2,1,0:T(8,128)(2,1)S(1)} %get-tuple-element.21), channel_id=1, source_target_pairs={{0,4},{4,0},{8,12},{12,8},{16,20},{20,16},{24,28},{28,24},{1,5},{5... | collective-permute-start | bytes 3145736 | tf_op jit(solution)/shard_map/ppermute | solution.py:22
  41.4 9.7 %collective-permute-start.14 = (bf16[1,1,1,64,1024]{4,3,2,1,0:T(8,128)(2,1)S(1)}, bf16[1,1,1,64,1024]{4,3,2,1,0:T(8,128)(2,1)S(1)}, u32[]{:S(2)}, u32[]{:S(2)}) collective-permute-start(bf16[1,1,1,64,1024]{4,3,2,1,0:T(8,128)(2,1)S(1)} %get-tuple-element.24), channel_id=1, source_target_pairs={{0,1},{1,2},{2,3},{3,0},{4,5},{5,6},{6,7},{7,4},{8,9},{9,10},{10,1... | collective-permute-start | bytes 393224 | tf_op jit(solution)/shard_map/ppermute | solution.py:17
  42.4 8.7 %collective-permute-start.15 = (bf16[1,1,1,64,1024]{4,3,2,1,0:T(8,128)(2,1)S(1)}, bf16[1,1,1,64,1024]{4,3,2,1,0:T(8,128)(2,1)S(1)}, u32[]{:S(2)}, u32[]{:S(2)}) collective-permute-start(bf16[1,1,1,64,1024]{4,3,2,1,0:T(8,128)(2,1)S(1)} %get-tuple-element.25), channel_id=1, source_target_pairs={{0,3},{1,0},{2,1},{3,2},{4,7},{5,4},{6,5},{7,6},{8,11},{9,8},{10,9... | collective-permute-start | bytes 393224 | tf_op jit(solution)/shard_map/ppermute | solution.py:17
  44.7 11.4 %collective-permute-start.17 = (bf16[1,1,2,64,1024]{4,3,2,1,0:T(8,128)(2,1)S(1)}, bf16[1,1,2,64,1024]{4,3,2,1,0:T(8,128)(2,1)S(1)}, u32[]{:S(2)}, u32[]{:S(2)}) collective-permute-start(bf16[1,1,2,64,1024]{4,3,2,1,0:T(8,128)(2,1)S(1)} %get-tuple-element.27), channel_id=1, source_target_pairs={{4,8},{8,4},{12,16},{16,12},{20,24},{24,20},{5,9},{9,5},{13,17},{1... | collective-permute-start | bytes 786440 | tf_op jit(solution)/shard_map/ppermute | solution.py:28
  48.3 13.4 %collective-permute-start.13 = (bf16[1,1,2,64,1024]{4,3,2,1,0:T(8,128)(2,1)S(1)}, bf16[1,1,2,64,1024]{4,3,2,1,0:T(8,128)(2,1)S(1)}, u32[]{:S(2)}, u32[]{:S(2)}) collective-permute-start(bf16[1,1,2,64,1024]{4,3,2,1,0:T(8,128)(2,1)S(1)} %get-tuple-element.22), channel_id=1, source_target_pairs={{4,8},{8,4},{12,16},{16,12},{20,24},{24,20},{5,9},{9,5},{13,17},{1... | collective-permute-start | bytes 786440 | tf_op jit(solution)/shard_map/ppermute | solution.py:28
  51.2 15.3 %collective-permute-start.16 = (bf16[1,1,2,64,1024]{4,3,2,1,0:T(8,128)(2,1)S(1)}, bf16[1,1,2,64,1024]{4,3,2,1,0:T(8,128)(2,1)S(1)}, u32[]{:S(2)}, u32[]{:S(2)}) collective-permute-start(bf16[1,1,2,64,1024]{4,3,2,1,0:T(8,128)(2,1)S(1)} %add_convert_fusion.3), channel_id=1, source_target_pairs={{4,8},{8,4},{12,16},{16,12},{20,24},{24,20},{5,9},{9,5},{13,17},{1... | collective-permute-start | bytes 786440 | tf_op jit(solution)/shard_map/ppermute | solution.py:28
  56.3 10.2 %collective-permute-start.19 = (bf16[2,1,1,64,1024]{4,3,2,1,0:T(8,128)(2,1)S(1)}, bf16[2,1,1,64,1024]{4,3,2,1,0:T(8,128)(2,1)S(1)}, u32[]{:S(2)}, u32[]{:S(2)}) collective-permute-start(bf16[2,1,1,64,1024]{4,3,2,1,0:T(8,128)(2,1)S(1)} %pad_maximum_fusion.2), channel_id=1, source_target_pairs={{0,3},{1,0},{2,1},{3,2},{4,7},{5,4},{6,5},{7,6},{8,11},{9,8},{10,9... | collective-permute-start | bytes 786440 | tf_op jit(solution)/shard_map/ppermute | solution.py:17
  56.4 12.0 %collective-permute-start.18 = (bf16[2,1,1,64,1024]{4,3,2,1,0:T(8,128)(2,1)S(1)}, bf16[2,1,1,64,1024]{4,3,2,1,0:T(8,128)(2,1)S(1)}, u32[]{:S(2)}, u32[]{:S(2)}) collective-permute-start(bf16[2,1,1,64,1024]{4,3,2,1,0:T(8,128)(2,1)S(1)} %pad_maximum_fusion.1), channel_id=1, source_target_pairs={{0,1},{1,2},{2,3},{3,0},{4,5},{5,6},{6,7},{7,4},{8,9},{9,10},{10,1... | collective-permute-start | bytes 786440 | tf_op jit(solution)/shard_map/ppermute | solution.py:17
